TPU v7x, 32 devices: a whole 2x2x4 slice. The times are simulated.
32 devices in a mesh: blk: 8 (over y, x, core), sub: 4 (over z).
Axes of the slice: x: 2, y: 2, z: 4, core: 2. Of those that a mesh axis runs over, the one named last changes fastest.
Arguments:
- u_flow: float32 [16, 2048, 2048], P(None, 'blk', 'sub'), may hold values from -60 to 60
- v_flow: float32 [16, 2048, 2048], P(None, 'blk', 'sub'), may hold values from -60 to 60
- thickness: float32 [16], replicated, may hold values from 0.1 to 0.5
- depth_levels: int32 [2048, 2048], P('blk', 'sub'), may hold values from 1 to 16
- block_ocean: int32 [16, 16], replicated, may hold values from 0 to 1, as said below
- coef_x: float32 [2048, 2048], P('blk', 'sub'), may hold values from 0.2 to 1
- coef_y: float32 [2048, 2048], P('blk', 'sub'), may hold values from 0.2 to 1
- coef_xy: float32 [2048, 2048], P('blk', 'sub'), may hold values from 0.2 to 1
- coef_xm: float32 [2048, 2048], P('blk', 'sub'), may hold values from 0.2 to 1
- extra_diagonal: float32 [2048, 2048], P('blk', 'sub'), may hold values from 0.02 to 2
Outputs:
- surface_height: float32 [2048, 2048], P('blk', 'sub')
- residual: float32 [2048, 2048], P('blk', 'sub')
Inputs may be any that keep to these rules, and one draw needn't show every extreme that they name: `block_ocean`: in every band of 256 rows of cells that one index of blk holds, exactly three quarters of the blocks are ocean blocks.
All inputs are finite; a program needn't handle non-finite values.
Results may differ from a plain program's by a relative error of at most 0.0003.
Values sent between devices are 32-bit elements; how exact they have to be, the bound alone decides.
No kernel may reach another device: no remote copies, remote signals or barrier semaphores. Data moves between devices by JAX's collectives and lax.ppermute only.
A program may use at most 128 MiB of HBM per device.

v0:
```python
import jax
import jax.numpy as jnp
from jax import lax
from jax.sharding import PartitionSpec as P

BLOCK = 128
ITERS = 4


OFFSETS = ((1, 0), (-1, 0), (0, 1), (0, -1), (1, 1), (-1, -1), (1, -1), (-1, 1))


def padded_2(value, sides, width):
    for axis, dim in sides:
        peers, length = (lax.axis_size(axis), value.shape[dim])
        up = [(i, (i + 1) % peers) for i in range(peers - 1)]
        down = [(j, i) for i, j in up]
        last = lax.slice_in_dim(value, length - width, length, axis=dim)
        initial = lax.slice_in_dim(value, 0, width, axis=dim)
        before = lax.ppermute(last, axis, up)
        after = lax.ppermute(initial, axis, down)
        value = jnp.concatenate([before, value, after], axis=dim)
    return value


def column_sums(u_flow, v_flow, thickness, depth_levels, ocean_mask):

    def add_level(level_index, totals):
        active = (depth_levels > level_index).astype(jnp.float32) * thickness[level_index]
        return (totals[0] + active * u_flow[level_index], totals[1] + active * v_flow[level_index])

    empty = jnp.zeros(depth_levels.shape, jnp.float32)
    flux_u, flux_v = lax.fori_loop(0, u_flow.shape[0], add_level, (empty, empty))
    return (ocean_mask * flux_u, ocean_mask * flux_v)


def neighbour_weights(padded):
    return [
        padded[0, ..., 1:-1, 1:-1],
        padded[0, ..., :-2, 1:-1],
        padded[1, ..., 1:-1, 1:-1],
        padded[1, ..., 1:-1, :-2],
        padded[2, ..., 1:-1, 1:-1],
        padded[2, ..., :-2, :-2],
        padded[3, ..., 1:-1, 1:-1],
        padded[3, ..., :-2, 2:],
    ]


def center_of(weights, extra_diagonal):
    center = extra_diagonal
    for weight in weights:
        center = center + weight
    return center


def operate(padded_field, weights, center, ocean_mask):
    row_count, col_count = center.shape[-2:]
    beside = jnp.zeros(center.shape, jnp.float32)
    for offset, weight in zip(OFFSETS, weights):
        beside = (
            beside
            + weight
            * padded_field[
                ...,
                1 + offset[0] : 1 + offset[0] + row_count,
                1 + offset[1] : 1 + offset[1] + col_count,
            ]
        )
    return ocean_mask * (center * padded_field[..., 1:-1, 1:-1] - beside)


def chron_gear(forcing, inverse, apply_operator):
    surface_height = jnp.zeros(forcing.shape, jnp.float32)
    residual = forcing
    search = jnp.zeros(forcing.shape, jnp.float32)
    search_image = jnp.zeros(forcing.shape, jnp.float32)
    rho_old = jnp.float32(1.0)
    sigma_value = jnp.float32(0.0)
    for iteration in range(ITERS):
        scaled = residual * inverse
        applied = apply_operator(scaled)
        rho_now, curvature = lax.psum(
            (jnp.sum(residual * scaled), jnp.sum(scaled * applied)), ("blk", "sub")
        )
        beta_ratio = rho_now / rho_old
        sigma_value = curvature - beta_ratio * beta_ratio * sigma_value
        alpha_step = rho_now / sigma_value
        rho_old = rho_now
        search = scaled + beta_ratio * search
        search_image = applied + beta_ratio * search_image
        surface_height = surface_height + alpha_step * search
        residual = residual - alpha_step * search_image
    return (surface_height, residual)


def body(
    u_flow,
    v_flow,
    thickness,
    depth_levels,
    block_ocean,
    coef_x,
    coef_y,
    coef_xy,
    coef_xm,
    extra_diagonal,
):
    row_count, col_count = depth_levels.shape
    block_rows = row_count // BLOCK
    block_cols = col_count // BLOCK
    blk_index = lax.axis_index("blk")
    sub_index = lax.axis_index("sub")
    tile_blocks = lax.dynamic_slice(
        block_ocean, (blk_index * block_rows, sub_index * block_cols), (block_rows, block_cols)
    )
    ocean_mask = jnp.repeat(jnp.repeat(tile_blocks, BLOCK, axis=0), BLOCK, axis=1).astype(
        jnp.float32
    )
    flux_u, flux_v = column_sums(u_flow, v_flow, thickness, depth_levels, ocean_mask)
    padded_flux = padded_2(jnp.stack([flux_u, flux_v]), (("blk", 1), ("sub", 2)), 1)
    forcing = ocean_mask * (
        0.5
        * (
            padded_flux[0, 2:, 1:-1]
            - padded_flux[0, :-2, 1:-1]
            + (padded_flux[1, 1:-1, 2:] - padded_flux[1, 1:-1, :-2])
        )
    )
    padded_coefs = padded_2(
        jnp.stack([coef_x, coef_y, coef_xy, coef_xm]), (("blk", 1), ("sub", 2)), 1
    )
    weights = neighbour_weights(padded_coefs)
    center = center_of(weights, extra_diagonal)
    inverse = 1.0 / center

    def apply_tiles(scaled):
        widened = padded_2(scaled, (("blk", 0), ("sub", 1)), 1)
        return operate(widened, weights, center, ocean_mask)

    return chron_gear(forcing, inverse, apply_tiles)


def solution(mesh):
    placed = (
        P(None, "blk", "sub"),
        P(None, "blk", "sub"),
        P(),
        P("blk", "sub"),
        P(),
        P("blk", "sub"),
        P("blk", "sub"),
        P("blk", "sub"),
        P("blk", "sub"),
        P("blk", "sub"),
    )
    return jax.shard_map(
        body,
        mesh=mesh,
        in_specs=placed,
        out_specs=(P("blk", "sub"), P("blk", "sub")),
        check_vma=False,
    )
```

profile of v0, /device:TPU:0, one launch (start us, length us, event | category | flops | bytes accessed | tf_op | source)
XLA Modules:
  0.0 399.1 jit_solution(7396352455479402402)
XLA Ops:
  4.6 2.0 pad_maximum_fusion.1
  8.0 2.4 collective-permute-start.4
  11.7 69.3 %while.16 = (s32[]{:T(128)}, f32[256,512]{1,0:T(8,128)S(1)}, f32[256,512]{1,0:T(8,128)S(1)}, s32[256,512]{1,0:T(8,128)S(1)}, f32[16]{0:T(128)S(1)}, /*index=5*/f...) while((s32[]{:T(128)}, f32[256,512]{1,0:T(8,128)S(1)}, ...), condition=%wide.region_1.0_spmd.clone, body=%wide.region_0.0_spmd.clone.sunk | while | flops 1179651 | bytes 3933820 | solution.py:33
  12.3 1.9 fusion.67
  14.2 1.8 fusion.68
  16.6 1.9 fusion.67
  18.5 1.8 fusion.68
  20.9 1.9 fusion.67
  22.8 1.8 fusion.68
  25.2 1.9 fusion.67
  27.2 1.8 fusion.68
  29.6 1.9 fusion.67
  31.5 1.8 fusion.68
  33.9 1.9 fusion.67
  35.8 1.8 fusion.68
  38.2 1.9 fusion.67
  40.2 1.8 fusion.68
  42.6 1.9 fusion.67
  44.5 1.8 fusion.68
  46.9 1.9 fusion.67
  48.8 1.8 fusion.68
  51.2 1.9 fusion.67
  53.1 1.8 fusion.68
  55.5 1.9 fusion.67
  57.5 1.8 fusion.68
  59.9 1.9 fusion.67
  61.8 1.8 fusion.68
  64.2 1.9 fusion.67
  66.1 1.8 fusion.68
  68.5 1.9 fusion.67
  70.5 1.8 fusion.68
  72.9 1.9 fusion.67
  74.8 1.8 fusion.68
  77.2 1.9 fusion.67
  79.1 1.8 fusion.68
  84.5 5.8 %collective-permute-start.1 = (f32[2,1,512]{2,1,0:T(1,128)S(1)}, f32[2,1,512]{2,1,0:T(1,128)S(1)}, u32[]{:S(2)}, u32[]{:S(2)}) collective-permute-start(f32[2,1,512]{2,1,0:T(1,128)S(1)} %get-tuple-element.210), channel_id=1, source_target_pairs={{0,4},{4,8},{8,12},{12,16},{16,20},{20,24},{24,28},{1,5},{5,9},{9,... | collective-permute-start | bytes 12296 | tf_op jit(solution)/shard_map/ppermute | solution.py:20
  90.3 2.0 copy.48
  92.3 2.0 pad_maximum_fusion
  102.0 6.0 %collective-permute-start.3 = (f32[2,258,1]{2,1,0:T(8,128)}, f32[2,258,1]{2,1,0:T(8,128)}, u32[]{:S(2)}, u32[]{:S(2)}) collective-permute-start(f32[2,258,1]{2,1,0:T(8,128)} %get-tuple-element.209), channel_id=1, source_target_pairs={{0,1},{1,2},{2,3},{4,5},{5,6},{6,7},{8,9},{9,10},{10,11},{12,13},{... | collective-permute-start | bytes 6200 | tf_op jit(solution)/shard_map/ppermute | solution.py:20
  108.0 3.7 copy.51
  111.9 3.4 collective-permute-start.6
  116.6 11.5 %pad_maximum_fusion.14 = f32[1,256,512]{2,0,1:T(1,128)S(1)} fusion(f32[4,258,1]{2,0,1:T(4,128)} %copy.53, f32[4,1,512]{2,0,1:T(4,128)S(1)} %collective-permute-done.5, f32[4,1,512]{2,0,1:T(4,128)S(1)} %collective-permute-done.4, f32[1,256,512]{2,0,1:T(1,128)} %copy-done.37, f32[1,256,512]{2,0,1:T(1,128)} %copy-done.35, f32[1,256,512]{2,0,1:T(1,128)} %copy-done.33, ...), kind=kLoop, calls=%fused_computation.96 | loop fusion | flops 786432 | bytes 2641952 | tf_op jit(solution)/shard_map/concatenate | solution.py:22
  129.1 3.9 fusion.55
  134.5 3.2 collective-permute-start.9
  139.9 4.6 %collective-permute-start.11 = (f32[258,1]{1,0:T(8,128)S(1)}, f32[258,1]{1,0:T(8,128)S(1)}, u32[]{:S(2)}, u32[]{:S(2)}) collective-permute-start(f32[258,1]{1,0:T(8,128)S(1)} %get-tuple-element.226), channel_id=1, source_target_pairs={{0,1},{1,2},{2,3},{4,5},{5,6},{6,7},{8,9},{9,10},{10,11},{12,13},{... | collective-permute-start | bytes 3104 | tf_op jit(solution)/shard_map/ppermute | solution.py:20
  144.4 1.8 collective-permute-done.10
  148.3 2.5 multiply_reduce_fusion.6
  150.8 44.2 %all-reduce.3 = (f32[]{:T(128)}, f32[]{:T(128)}) all-reduce(f32[]{:T(128)} %get-tuple-element.162, f32[]{:T(128)} %get-tuple-element.161), channel_id=1, replica_groups=mesh['blk'=8,'sub'=4] {'blk','sub'}, use_global_device_ids=true, to_apply=%region_3.0 | all-reduce | flops 2 | bytes 16 | tf_op jit(solution)/shard_map/psum | solution.py:83
  201.4 3.0 collective-permute-start.13
  206.7 4.6 %collective-permute-start.15 = (f32[258,1]{1,0:T(8,128)S(1)}, f32[258,1]{1,0:T(8,128)S(1)}, u32[]{:S(2)}, u32[]{:S(2)}) collective-permute-start(f32[258,1]{1,0:T(8,128)S(1)} %get-tuple-element.222), channel_id=1, source_target_pairs={{0,1},{1,2},{2,3},{4,5},{5,6},{6,7},{8,9},{9,10},{10,11},{12,13},{... | collective-permute-start | bytes 3104 | tf_op jit(solution)/shard_map/ppermute | solution.py:20
  215.0 2.4 multiply_reduce_fusion.4
  217.4 43.6 %all-reduce.2 = (f32[]{:T(128)}, f32[]{:T(128)}) all-reduce(f32[]{:T(128)} %get-tuple-element.160, f32[]{:T(128)} %get-tuple-element.159), channel_id=1, replica_groups=mesh['blk'=8,'sub'=4] {'blk','sub'}, use_global_device_ids=true, to_apply=%region_7.0 | all-reduce | flops 2 | bytes 16 | tf_op jit(solution)/shard_map/psum | solution.py:83
  263.8 2.5 fusion.53
  267.9 3.0 collective-permute-start.17
  273.2 4.8 %collective-permute-start.19 = (f32[258,1]{1,0:T(8,128)S(1)}, f32[258,1]{1,0:T(8,128)S(1)}, u32[]{:S(2)}, u32[]{:S(2)}) collective-permute-start(f32[258,1]{1,0:T(8,128)S(1)} %get-tuple-element.218), channel_id=1, source_target_pairs={{0,1},{1,2},{2,3},{4,5},{5,6},{6,7},{8,9},{9,10},{10,11},{12,13},{... | collective-permute-start | bytes 3104 | tf_op jit(solution)/shard_map/ppermute | solution.py:20
  279.4 2.0 collective-permute-done.19
  281.7 2.4 multiply_reduce_fusion.2
  284.1 43.2 %all-reduce.1 = (f32[]{:T(128)}, f32[]{:T(128)}) all-reduce(f32[]{:T(128)} %get-tuple-element.158, f32[]{:T(128)} %get-tuple-element.157), channel_id=1, replica_groups=mesh['blk'=8,'sub'=4] {'blk','sub'}, use_global_device_ids=true, to_apply=%region_11.0 | all-reduce | flops 2 | bytes 16 | tf_op jit(solution)/shard_map/psum | solution.py:83
  330.1 1.7 fusion.52
  333.5 3.0 collective-permute-start.21
  338.7 4.6 %collective-permute-start.23 = (f32[258,1]{1,0:T(8,128)S(1)}, f32[258,1]{1,0:T(8,128)S(1)}, u32[]{:S(2)}, u32[]{:S(2)}) collective-permute-start(f32[258,1]{1,0:T(8,128)S(1)} %get-tuple-element.214), channel_id=1, source_target_pairs={{0,1},{1,2},{2,3},{4,5},{5,6},{6,7},{8,9},{9,10},{10,11},{12,13},{... | collective-permute-start | bytes 3104 | tf_op jit(solution)/shard_map/ppermute | solution.py:20
  347.0 2.4 multiply_reduce_fusion
  349.4 43.2 %all-reduce = (f32[]{:T(128)}, f32[]{:T(128)}) all-reduce(f32[]{:T(128)} %get-tuple-element.156, f32[]{:T(128)} %get-tuple-element.155), channel_id=1, replica_groups=mesh['blk'=8,'sub'=4] {'blk','sub'}, use_global_device_ids=true, to_apply=%region_15.0 | all-reduce | flops 2 | bytes 16 | tf_op jit(solution)/shard_map/psum | solution.py:83
  395.5 3.6 multiply_subtract_fusion
  (172 shorter events, 56.6 us)
Async XLA Ops:
  0.6 3.1 copy-start.1
  0.6 3.5 copy-start
  2.1 4.4 %copy-start.31 = (f32[1,256,512]{2,0,1:T(1,128)}, f32[1,256,512]{2,0,1:T(1,128)S(1)}, u32[]{:S(2)}) copy-start(f32[1,256,512]{2,0,1:T(1,128)S(1)} %stack.27) | copy-start | bytes 1572868
  4.5 3.4 copy-start.37
  4.5 7.1 %copy-start.9 = (s32[256,512]{1,0:T(8,128)S(1)}, s32[256,512]{1,0:T(8,128)}, u32[]{:S(2)}) copy-start(s32[256,512]{1,0:T(8,128)} %param.15) | copy-start | bytes 1572868
  4.6 7.1 %copy-start.44 = (f32[16]{0:T(128)S(1)}, f32[16]{0:T(128)}, u32[]{:S(2)}) copy-start(f32[16]{0:T(128)} %param.14) | copy-start | bytes 196
  8.0 84.3 %collective-permute-start.4 = (f32[4,1,512]{2,0,1:T(4,128)S(1)}, f32[4,1,512]{2,0,1:T(4,128)S(1)}, u32[]{:S(2)}, u32[]{:S(2)}) collective-permute-start(f32[4,1,512]{2,0,1:T(4,128)S(1)} %get-tuple-element.206), channel_id=1, source_target_pairs={{0,4},{4,8},{8,12},{12,16},{16,20},{20,24},{24,28},{1,5},{5,9},{9,... | collective-permute-start | bytes 24584 | tf_op jit(solution)/shard_map/ppermute | solution.py:20
  10.3 82.0 %collective-permute-start.5 = (f32[4,1,512]{2,0,1:T(4,128)S(1)}, f32[4,1,512]{2,0,1:T(4,128)S(1)}, u32[]{:S(2)}, u32[]{:S(2)}) collective-permute-start(f32[4,1,512]{2,0,1:T(4,128)S(1)} %get-tuple-element.207), channel_id=1, source_target_pairs={{4,0},{8,4},{12,8},{16,12},{20,16},{24,20},{28,24},{5,1},{9,5},{13... | collective-permute-start | bytes 24584 | tf_op jit(solution)/shard_map/ppermute | solution.py:21
  81.7 8.5 %copy-start.27 = (f32[4,256,512]{2,0,1:T(4,128)S(1)}, f32[4,256,512]{2,0,1:T(4,128)}, u32[]{:S(2)}) copy-start(f32[4,256,512]{2,0,1:T(4,128)} %copy-done.26) | copy-start | bytes 6291460
  82.3 17.5 %copy-start.28 = (f32[1,256,512]{2,1,0:T(8,128)}, f32[1,256,512]{2,1,0:T(8,128)S(1)}, u32[]{:S(2)}) copy-start(f32[1,256,512]{2,1,0:T(8,128)S(1)} %get-tuple-element.236) | copy-start | bytes 1572868
  83.0 9.3 %copy-start.32 = (f32[1,256,512]{2,0,1:T(1,128)S(1)}, f32[1,256,512]{2,0,1:T(1,128)}, u32[]{:S(2)}) copy-start(f32[1,256,512]{2,0,1:T(1,128)} %copy-done.31) | copy-start | bytes 1572868
  83.0 9.3 %copy-start.34 = (f32[1,256,512]{2,0,1:T(1,128)S(1)}, f32[1,256,512]{2,0,1:T(1,128)}, u32[]{:S(2)}) copy-start(f32[1,256,512]{2,0,1:T(1,128)} %copy-done.33) | copy-start | bytes 1572868
  83.1 9.3 %copy-start.36 = (f32[1,256,512]{2,0,1:T(1,128)S(1)}, f32[1,256,512]{2,0,1:T(1,128)}, u32[]{:S(2)}) copy-start(f32[1,256,512]{2,0,1:T(1,128)} %copy-done.35) | copy-start | bytes 1572868
  83.1 9.3 %copy-start.38 = (f32[1,256,512]{2,0,1:T(1,128)S(1)}, f32[1,256,512]{2,0,1:T(1,128)}, u32[]{:S(2)}) copy-start(f32[1,256,512]{2,0,1:T(1,128)} %copy-done.37) | copy-start | bytes 1572868
  83.1 16.7 %collective-permute-start = (f32[2,1,512]{2,1,0:T(1,128)S(1)}, f32[2,1,512]{2,1,0:T(1,128)S(1)}, u32[]{:S(2)}, u32[]{:S(2)}) collective-permute-start(f32[2,1,512]{2,1,0:T(1,128)S(1)} %get-tuple-element.211), channel_id=1, source_target_pairs={{4,0},{8,4},{12,8},{16,12},{20,16},{24,20},{28,24},{5,1},{9,5},{13... | collective-permute-start | bytes 12296 | tf_op jit(solution)/shard_map/ppermute | solution.py:21
  84.5 15.3 %collective-permute-start.1 = (f32[2,1,512]{2,1,0:T(1,128)S(1)}, f32[2,1,512]{2,1,0:T(1,128)S(1)}, u32[]{:S(2)}, u32[]{:S(2)}) collective-permute-start(f32[2,1,512]{2,1,0:T(1,128)S(1)} %get-tuple-element.210), channel_id=1, source_target_pairs={{0,4},{4,8},{8,12},{12,16},{16,20},{20,24},{24,28},{1,5},{5,9},{9,... | collective-permute-start | bytes 12296 | tf_op jit(solution)/shard_map/ppermute | solution.py:20
  95.8 4.0 %copy-start.30 = (f32[1,256,512]{2,1,0:T(8,128)S(1)}, f32[1,256,512]{2,1,0:T(8,128)}, u32[]{:S(2)}) copy-start(f32[1,256,512]{2,1,0:T(8,128)} %copy-done.29) | copy-start | bytes 1572868
  98.5 16.9 %collective-permute-start.7 = (f32[4,258,1]{1,0,2:T(4,128)S(1)}, f32[4,258,1]{1,0,2:T(4,128)S(1)}, u32[]{:S(2)}, u32[]{:S(2)}) collective-permute-start(f32[4,258,1]{1,0,2:T(4,128)S(1)} %copy.52), channel_id=1, source_target_pairs={{1,0},{2,1},{3,2},{5,4},{6,5},{7,6},{9,8},{10,9},{11,10},{13,12},{... | collective-permute-start | bytes 12392 | tf_op jit(solution)/shard_map/ppermute | solution.py:21
  100.7 28.4 %collective-permute-start.2 = (f32[2,258,1]{2,1,0:T(8,128)}, f32[2,258,1]{2,1,0:T(8,128)S(1)}, u32[]{:S(2)}, u32[]{:S(2)}) collective-permute-start(f32[2,258,1]{2,1,0:T(8,128)} %get-tuple-element.208), channel_id=1, source_target_pairs={{1,0},{2,1},{3,2},{5,4},{6,5},{7,6},{9,8},{10,9},{11,10},{13,12},{... | collective-permute-start | bytes 6200 | tf_op jit(solution)/shard_map/ppermute | solution.py:21
  102.0 9.7 %copy-start.43 = (f32[4,258,1]{2,0,1:T(4,128)S(1)}, f32[4,258,1]{2,0,1:T(4,128)}, u32[]{:S(2)}) copy-start(f32[4,258,1]{2,0,1:T(4,128)} %get-tuple-element.204) | copy-start | bytes 12388
  102.0 27.1 %collective-permute-start.3 = (f32[2,258,1]{2,1,0:T(8,128)}, f32[2,258,1]{2,1,0:T(8,128)}, u32[]{:S(2)}, u32[]{:S(2)}) collective-permute-start(f32[2,258,1]{2,1,0:T(8,128)} %get-tuple-element.209), channel_id=1, source_target_pairs={{0,1},{1,2},{2,3},{4,5},{5,6},{6,7},{8,9},{9,10},{10,11},{12,13},{... | collective-permute-start | bytes 6200 | tf_op jit(solution)/shard_map/ppermute | solution.py:20
  111.9 16.1 %collective-permute-start.6 = (f32[4,258,1]{1,0,2:T(4,128)S(1)}, f32[4,258,1]{1,0,2:T(4,128)S(1)}, u32[]{:S(2)}, u32[]{:S(2)}) collective-permute-start(f32[4,258,1]{1,0,2:T(4,128)S(1)} %copy.49), channel_id=1, source_target_pairs={{0,1},{1,2},{2,3},{4,5},{5,6},{6,7},{8,9},{9,10},{10,11},{12,13},{... | collective-permute-start | bytes 12392 | tf_op jit(solution)/shard_map/ppermute | solution.py:20
  115.4 13.7 %copy-start.2 = (f32[256,512]{1,0:T(8,128)S(1)}, f32[256,512]{1,0:T(8,128)}, u32[]{:S(2)}) copy-start(f32[256,512]{1,0:T(8,128)} %param.18) | copy-start | bytes 1572868
  115.4 13.7 %copy-start.3 = (f32[256,512]{1,0:T(8,128)S(1)}, f32[256,512]{1,0:T(8,128)}, u32[]{:S(2)}) copy-start(f32[256,512]{1,0:T(8,128)} %param.17) | copy-start | bytes 1572868
  133.0 17.8 %copy-start.5 = (f32[256,512]{1,0:T(8,128)}, f32[256,512]{1,0:T(8,128)S(1)}, u32[]{:S(2)}) copy-start(f32[256,512]{1,0:T(8,128)S(1)} %get-tuple-element.198) | copy-start | bytes 1572868
  133.0 17.8 %copy-start.14 = (f32[256,512]{1,0:T(8,128)}, f32[256,512]{1,0:T(8,128)S(1)}, u32[]{:S(2)}) copy-start(f32[256,512]{1,0:T(8,128)S(1)} %get-tuple-element.200) | copy-start | bytes 1572868
  133.0 17.8 %copy-start.18 = (f32[256,512]{1,0:T(8,128)}, f32[256,512]{1,0:T(8,128)S(1)}, u32[]{:S(2)}) copy-start(f32[256,512]{1,0:T(8,128)S(1)} %get-tuple-element.201) | copy-start | bytes 1572868
  133.0 17.7 %copy-start.22 = (f32[256,512]{1,0:T(8,128)}, f32[256,512]{1,0:T(8,128)S(1)}, u32[]{:S(2)}) copy-start(f32[256,512]{1,0:T(8,128)S(1)} %get-tuple-element.202) | copy-start | bytes 1572868
  133.0 17.7 %copy-start.39 = (f32[256,512]{1,0:T(8,128)}, f32[256,512]{1,0:T(8,128)S(1)}, u32[]{:S(2)}) copy-start(f32[256,512]{1,0:T(8,128)S(1)} %get-tuple-element.203) | copy-start | bytes 1572868
  133.0 15.2 %copy-start.10 = (f32[256,512]{1,0:T(8,128)S(1)}, f32[256,512]{1,0:T(8,128)}, u32[]{:S(2)}) copy-start(f32[256,512]{1,0:T(8,128)} %param.21) | copy-start | bytes 1572868
  133.1 4.6 %collective-permute-start.8 = (f32[1,512]{1,0:T(1,128)S(1)}, f32[1,512]{1,0:T(1,128)S(1)}, u32[]{:S(2)}, u32[]{:S(2)}) collective-permute-start(f32[1,512]{1,0:T(1,128)S(1)} %get-tuple-element.235), channel_id=1, source_target_pairs={{4,0},{8,4},{12,8},{16,12},{20,16},{24,20},{28,24},{5,1},{9,5},{13... | collective-permute-start | bytes 6152 | tf_op jit(solution)/shard_map/ppermute | solution.py:21
  134.5 4.0 collective-permute-start.9
  138.6 7.7 %collective-permute-start.10 = (f32[258,1]{1,0:T(8,128)S(1)}, f32[258,1]{1,0:T(8,128)S(1)}, u32[]{:S(2)}, u32[]{:S(2)}) collective-permute-start(f32[258,1]{1,0:T(8,128)S(1)} %get-tuple-element.227), channel_id=1, source_target_pairs={{1,0},{2,1},{3,2},{5,4},{6,5},{7,6},{9,8},{10,9},{11,10},{13,12},{... | collective-permute-start | bytes 3104 | tf_op jit(solution)/shard_map/ppermute | solution.py:21
  139.9 8.1 %collective-permute-start.11 = (f32[258,1]{1,0:T(8,128)S(1)}, f32[258,1]{1,0:T(8,128)S(1)}, u32[]{:S(2)}, u32[]{:S(2)}) collective-permute-start(f32[258,1]{1,0:T(8,128)S(1)} %get-tuple-element.226), channel_id=1, source_target_pairs={{0,1},{1,2},{2,3},{4,5},{5,6},{6,7},{8,9},{9,10},{10,11},{12,13},{... | collective-permute-start | bytes 3104 | tf_op jit(solution)/shard_map/ppermute | solution.py:20
  199.8 17.6 %copy-start.6 = (f32[256,512]{1,0:T(8,128)}, f32[256,512]{1,0:T(8,128)S(1)}, u32[]{:S(2)}) copy-start(f32[256,512]{1,0:T(8,128)S(1)} %get-tuple-element.195) | copy-start | bytes 1572868
  199.8 17.6 %copy-start.41 = (f32[256,512]{1,0:T(8,128)}, f32[256,512]{1,0:T(8,128)S(1)}, u32[]{:S(2)}) copy-start(f32[256,512]{1,0:T(8,128)S(1)} %get-tuple-element.196) | copy-start | bytes 1572868
  199.8 15.1 %copy-start.11 = (f32[256,512]{1,0:T(8,128)S(1)}, f32[256,512]{1,0:T(8,128)}, u32[]{:S(2)}) copy-start(f32[256,512]{1,0:T(8,128)} %param.21) | copy-start | bytes 1572868
  199.8 15.1 %copy-start.15 = (f32[256,512]{1,0:T(8,128)S(1)}, f32[256,512]{1,0:T(8,128)}, u32[]{:S(2)}) copy-start(f32[256,512]{1,0:T(8,128)} %copy-done.14) | copy-start | bytes 1572868
  199.8 15.1 %copy-start.19 = (f32[256,512]{1,0:T(8,128)S(1)}, f32[256,512]{1,0:T(8,128)}, u32[]{:S(2)}) copy-start(f32[256,512]{1,0:T(8,128)} %copy-done.18) | copy-start | bytes 1572868
  199.9 15.1 %copy-start.23 = (f32[256,512]{1,0:T(8,128)S(1)}, f32[256,512]{1,0:T(8,128)}, u32[]{:S(2)}) copy-start(f32[256,512]{1,0:T(8,128)} %copy-done.22) | copy-start | bytes 1572868
  199.9 4.6 %collective-permute-start.12 = (f32[1,512]{1,0:T(1,128)S(1)}, f32[1,512]{1,0:T(1,128)S(1)}, u32[]{:S(2)}, u32[]{:S(2)}) collective-permute-start(f32[1,512]{1,0:T(1,128)S(1)} %get-tuple-element.233), channel_id=1, source_target_pairs={{4,0},{8,4},{12,8},{16,12},{20,16},{24,20},{28,24},{5,1},{9,5},{13... | collective-permute-start | bytes 6152 | tf_op jit(solution)/shard_map/ppermute | solution.py:21
  201.4 3.8 collective-permute-start.13
  205.4 7.5 %collective-permute-start.14 = (f32[258,1]{1,0:T(8,128)S(1)}, f32[258,1]{1,0:T(8,128)S(1)}, u32[]{:S(2)}, u32[]{:S(2)}) collective-permute-start(f32[258,1]{1,0:T(8,128)S(1)} %get-tuple-element.223), channel_id=1, source_target_pairs={{1,0},{2,1},{3,2},{5,4},{6,5},{7,6},{9,8},{10,9},{11,10},{13,12},{... | collective-permute-start | bytes 3104 | tf_op jit(solution)/shard_map/ppermute | solution.py:21
  206.7 8.0 %collective-permute-start.15 = (f32[258,1]{1,0:T(8,128)S(1)}, f32[258,1]{1,0:T(8,128)S(1)}, u32[]{:S(2)}, u32[]{:S(2)}) collective-permute-start(f32[258,1]{1,0:T(8,128)S(1)} %get-tuple-element.222), channel_id=1, source_target_pairs={{0,1},{1,2},{2,3},{4,5},{5,6},{6,7},{8,9},{9,10},{10,11},{12,13},{... | collective-permute-start | bytes 3104 | tf_op jit(solution)/shard_map/ppermute | solution.py:20
  266.3 17.8 %copy-start.7 = (f32[256,512]{1,0:T(8,128)}, f32[256,512]{1,0:T(8,128)S(1)}, u32[]{:S(2)}) copy-start(f32[256,512]{1,0:T(8,128)S(1)} %get-tuple-element.191) | copy-start | bytes 1572868
  266.3 17.8 %copy-start.42 = (f32[256,512]{1,0:T(8,128)}, f32[256,512]{1,0:T(8,128)S(1)}, u32[]{:S(2)}) copy-start(f32[256,512]{1,0:T(8,128)S(1)} %get-tuple-element.192) | copy-start | bytes 1572868
  266.3 15.3 %copy-start.12 = (f32[256,512]{1,0:T(8,128)S(1)}, f32[256,512]{1,0:T(8,128)}, u32[]{:S(2)}) copy-start(f32[256,512]{1,0:T(8,128)} %param.21) | copy-start | bytes 1572868
  266.3 15.3 %copy-start.16 = (f32[256,512]{1,0:T(8,128)S(1)}, f32[256,512]{1,0:T(8,128)}, u32[]{:S(2)}) copy-start(f32[256,512]{1,0:T(8,128)} %copy-done.14) | copy-start | bytes 1572868
  266.3 15.3 %copy-start.20 = (f32[256,512]{1,0:T(8,128)S(1)}, f32[256,512]{1,0:T(8,128)}, u32[]{:S(2)}) copy-start(f32[256,512]{1,0:T(8,128)} %copy-done.18) | copy-start | bytes 1572868
  266.3 15.3 %copy-start.24 = (f32[256,512]{1,0:T(8,128)S(1)}, f32[256,512]{1,0:T(8,128)}, u32[]{:S(2)}) copy-start(f32[256,512]{1,0:T(8,128)} %copy-done.22) | copy-start | bytes 1572868
  266.3 4.6 %collective-permute-start.16 = (f32[1,512]{1,0:T(1,128)S(1)}, f32[1,512]{1,0:T(1,128)S(1)}, u32[]{:S(2)}, u32[]{:S(2)}) collective-permute-start(f32[1,512]{1,0:T(1,128)S(1)} %get-tuple-element.231), channel_id=1, source_target_pairs={{4,0},{8,4},{12,8},{16,12},{20,16},{24,20},{28,24},{5,1},{9,5},{13... | collective-permute-start | bytes 6152 | tf_op jit(solution)/shard_map/ppermute | solution.py:21
  267.9 3.8 collective-permute-start.17
  271.9 7.5 %collective-permute-start.18 = (f32[258,1]{1,0:T(8,128)S(1)}, f32[258,1]{1,0:T(8,128)S(1)}, u32[]{:S(2)}, u32[]{:S(2)}) collective-permute-start(f32[258,1]{1,0:T(8,128)S(1)} %get-tuple-element.219), channel_id=1, source_target_pairs={{1,0},{2,1},{3,2},{5,4},{6,5},{7,6},{9,8},{10,9},{11,10},{13,12},{... | collective-permute-start | bytes 3104 | tf_op jit(solution)/shard_map/ppermute | solution.py:21
  273.2 8.2 %collective-permute-start.19 = (f32[258,1]{1,0:T(8,128)S(1)}, f32[258,1]{1,0:T(8,128)S(1)}, u32[]{:S(2)}, u32[]{:S(2)}) collective-permute-start(f32[258,1]{1,0:T(8,128)S(1)} %get-tuple-element.218), channel_id=1, source_target_pairs={{0,1},{1,2},{2,3},{4,5},{5,6},{6,7},{8,9},{9,10},{10,11},{12,13},{... | collective-permute-start | bytes 3104 | tf_op jit(solution)/shard_map/ppermute | solution.py:20
  331.8 17.6 %copy-start.8 = (f32[256,512]{1,0:T(8,128)}, f32[256,512]{1,0:T(8,128)S(1)}, u32[]{:S(2)}) copy-start(f32[256,512]{1,0:T(8,128)S(1)} %get-tuple-element.188) | copy-start | bytes 1572868
  331.8 17.6 %copy-start.40 = (f32[256,512]{1,0:T(8,128)}, f32[256,512]{1,0:T(8,128)S(1)}, u32[]{:S(2)}) copy-start(f32[256,512]{1,0:T(8,128)S(1)} %get-tuple-element.189) | copy-start | bytes 1572868
  331.8 15.1 %copy-start.13 = (f32[256,512]{1,0:T(8,128)S(1)}, f32[256,512]{1,0:T(8,128)}, u32[]{:S(2)}) copy-start(f32[256,512]{1,0:T(8,128)} %param.21) | copy-start | bytes 1572868
  331.8 15.1 %copy-start.17 = (f32[256,512]{1,0:T(8,128)S(1)}, f32[256,512]{1,0:T(8,128)}, u32[]{:S(2)}) copy-start(f32[256,512]{1,0:T(8,128)} %copy-done.14) | copy-start | bytes 1572868
  331.9 15.1 %copy-start.21 = (f32[256,512]{1,0:T(8,128)S(1)}, f32[256,512]{1,0:T(8,128)}, u32[]{:S(2)}) copy-start(f32[256,512]{1,0:T(8,128)} %copy-done.18) | copy-start | bytes 1572868
  331.9 15.1 %copy-start.25 = (f32[256,512]{1,0:T(8,128)S(1)}, f32[256,512]{1,0:T(8,128)}, u32[]{:S(2)}) copy-start(f32[256,512]{1,0:T(8,128)} %copy-done.22) | copy-start | bytes 1572868
  331.9 4.6 %collective-permute-start.20 = (f32[1,512]{1,0:T(1,128)S(1)}, f32[1,512]{1,0:T(1,128)S(1)}, u32[]{:S(2)}, u32[]{:S(2)}) collective-permute-start(f32[1,512]{1,0:T(1,128)S(1)} %get-tuple-element.229), channel_id=1, source_target_pairs={{4,0},{8,4},{12,8},{16,12},{20,16},{24,20},{28,24},{5,1},{9,5},{13... | collective-permute-start | bytes 6152 | tf_op jit(solution)/shard_map/ppermute | solution.py:21
  333.5 3.8 collective-permute-start.21
  337.4 7.5 %collective-permute-start.22 = (f32[258,1]{1,0:T(8,128)S(1)}, f32[258,1]{1,0:T(8,128)S(1)}, u32[]{:S(2)}, u32[]{:S(2)}) collective-permute-start(f32[258,1]{1,0:T(8,128)S(1)} %get-tuple-element.215), channel_id=1, source_target_pairs={{1,0},{2,1},{3,2},{5,4},{6,5},{7,6},{9,8},{10,9},{11,10},{13,12},{... | collective-permute-start | bytes 3104 | tf_op jit(solution)/shard_map/ppermute | solution.py:21
  338.7 8.0 %collective-permute-start.23 = (f32[258,1]{1,0:T(8,128)S(1)}, f32[258,1]{1,0:T(8,128)S(1)}, u32[]{:S(2)}, u32[]{:S(2)}) collective-permute-start(f32[258,1]{1,0:T(8,128)S(1)} %get-tuple-element.214), channel_id=1, source_target_pairs={{0,1},{1,2},{2,3},{4,5},{5,6},{6,7},{8,9},{9,10},{10,11},{12,13},{... | collective-permute-start | bytes 3104 | tf_op jit(solution)/shard_map/ppermute | solution.py:20
  (5 other events, 8.8 us)
where the time goes:
time: 402 us; the launch traced here: 399 us
  blocking collectives  174 us (43%)
  other arithmetic  102 us (25%)
  starting transfers between devices  64.8 us (16%)
  local copies, waits for them, and re-layouts  27.6 us (7%)
  waiting for transfers between devices  16.9 us (4%)
  between operations  13.2 us (3%)
    psum x4, blocking collectives, chron_gear(): lax.psum((jnp.sum(residual * scaled), jnp.sum(scaled * applied)), ('blk',...  174 us
    ppermute x12, starting transfers between devices, padded_2(): before = lax.ppermute(last, axis, up)  48.2 us
    add x16, other arithmetic, add_level(): totals[1] + active * v_flow[level_index]  30.7 us
    add x16, other arithmetic, add_level(): totals[0] + active * u_flow[level_index]  29.4 us
    ppermute x12, starting transfers between devices, padded_2(): after = lax.ppermute(initial, axis, down)  16.5 us
    concatenate x10, other arithmetic, padded_2(): value = jnp.concatenate([before, value, after], axis=dim)  15.1 us
    ppermute x12, waiting for transfers between devices, padded_2(): before = lax.ppermute(last, axis, up)  10.4 us
    reduce_sum x4, other arithmetic, chron_gear(): jnp.sum(scaled * applied)  9.76 us
  transfers between devices with their start and end apart: 24, of which 12 were waited for; matrix products, arithmetic and copies ran while one was open for 24% of the time, Pallas kernels for 0%

commit v1 on v0

v1 whole, which is shorter than its diff:
```python
import functools

import jax
import jax.numpy as jnp
from jax import lax
from jax.experimental import pallas as pl
from jax.experimental.pallas import tpu as pltpu
from jax.sharding import PartitionSpec as P

BLOCK = 128
ITERS = 4
HALO = ITERS
LANES = 128
ROWS = 8
FIELDS = 8
CHUNK = 32
F32 = jnp.float32
VMEM = pl.BlockSpec(memory_space=pltpu.VMEM)
SMEM = pl.BlockSpec(memory_space=pltpu.SMEM)
HBM = pl.BlockSpec(memory_space=pltpu.HBM)
PAIRS = [(i, j) for i in range(ITERS) for j in range(i, ITERS + 1)]


def lane_of(shape):
    return lax.broadcasted_iota(jnp.int32, shape, len(shape) - 1)


def row_of(shape):
    return lax.broadcasted_iota(jnp.int32, shape, len(shape) - 2)


def left(value):
    return pltpu.roll(value, 1, 1)


def right(value):
    return pltpu.roll(value, value.shape[1] - 1, 1)


def ocean_at(ocean_ref, row, col):
    block_rows, block_cols = ocean_ref.shape
    inside = (row >= 0) & (row < block_rows) & (col >= 0) & (col < block_cols)
    entry = ocean_ref[jnp.clip(row, 0, block_rows - 1), jnp.clip(col, 0, block_cols - 1)]
    return jnp.where(inside & (entry == 1), 1.0, 0.0).astype(F32)


def flux_kernel(
    ids, thick, ocean, u_hbm, v_hbm, depth_hbm, cx_hbm, cy_hbm, cxy_hbm, cxm_hbm, ex_hbm,
    fp_ref, cp_ref, fue_ref, pack_a, pack_b,
    u_buf, v_buf, depth, cx, cy, cxy, cxm, ex, fu, fv, sems, coef_sem,
):
    levels, row_count, col_count = u_buf.shape
    tiles = col_count // LANES
    chunks = row_count // CHUNK
    quarter = row_count // 4
    blk, sub = ids[0], ids[1]
    coef_copies = [
        pltpu.make_async_copy(src, dst, coef_sem.at[i])
        for i, (src, dst) in enumerate(
            [(depth_hbm, depth), (cx_hbm, cx), (cy_hbm, cy), (cxy_hbm, cxy), (cxm_hbm, cxm), (ex_hbm, ex)]
        )
    ]

    def flow_copies(c):
        rows = pl.ds(c * CHUNK, CHUNK)
        return (
            pltpu.make_async_copy(u_hbm.at[:, rows, :], u_buf.at[:, rows, :], sems.at[0, c]),
            pltpu.make_async_copy(v_hbm.at[:, rows, :], v_buf.at[:, rows, :], sems.at[1, c]),
        )

    for copy in coef_copies:
        copy.start()
    for c in range(chunks):
        for copy in flow_copies(c):
            copy.start()
    for copy in coef_copies:
        copy.wait()

    row8 = row_of((ROWS, col_count))
    lane8 = lane_of((ROWS, col_count))

    def center_group(g, carry):
        above_x, above_xy, above_xm = carry
        rows = pl.ds(pl.multiple_of(g * ROWS, ROWS), ROWS)
        here_x, here_y, here_xy, here_xm = cx[rows], cy[rows], cxy[rows], cxm[rows]
        shift = lambda a, b: jnp.where(row8 == 0, pltpu.roll(a, 1, 0), pltpu.roll(b, 1, 0))
        total = ex[rows] + here_x
        total = total + shift(above_x, here_x)
        total = total + here_y
        total = total + jnp.where(lane8 == 0, 0.0, left(here_y))
        total = total + here_xy
        total = total + jnp.where(lane8 == 0, 0.0, left(shift(above_xy, here_xy)))
        total = total + here_xm
        total = total + jnp.where(lane8 == col_count - 1, 0.0, right(shift(above_xm, here_xm)))
        cp_ref[rows] = total
        return here_x, here_xy, here_xm

    zero = jnp.zeros((ROWS, col_count), F32)
    lax.fori_loop(0, row_count // ROWS, center_group, (zero, zero, zero))

    block_rows = row_count // BLOCK
    for c in range(chunks):
        for copy in flow_copies(c):
            copy.wait()
        block_row = blk * block_rows + c * CHUNK // BLOCK

        def sum_group(g, _, c=c, block_row=block_row):
            rows = pl.ds(pl.multiple_of(c * CHUNK + g * ROWS, ROWS), ROWS)
            for t in range(tiles):
                lanes = pl.ds(t * LANES, LANES)
                mask = ocean_at(ocean, block_row, sub * tiles + t)
                deep = depth[rows, lanes]
                total_u = jnp.zeros((ROWS, LANES), F32)
                total_v = total_u
                for k in range(levels):
                    active = jnp.where(deep > k, thick[k], 0.0)
                    total_u = total_u + active * u_buf[k, rows, lanes]
                    total_v = total_v + active * v_buf[k, rows, lanes]
                fu[rows, lanes] = mask * total_u
                fv[rows, lanes] = mask * total_v
            return 0

        lax.fori_loop(0, CHUNK // ROWS, sum_group, 0)

    even = (sub % 2) == 0
    lane1 = lane_of((ROWS, LANES))

    def force_group(k, g, _):
        base = k * quarter + g * ROWS
        rows = pl.ds(pl.multiple_of(base, ROWS), ROWS)
        here_u, here_v = fu[rows], fv[rows]
        before = fu[pl.ds(pl.multiple_of(jnp.maximum(base - ROWS, 0), ROWS), ROWS)]
        after = fu[pl.ds(pl.multiple_of(jnp.minimum(base + ROWS, row_count - ROWS), ROWS), ROWS)]
        first, final = base == 0, base == row_count - ROWS
        up = jnp.where(row8 == 0, jnp.where(first, 0.0, pltpu.roll(before, 1, 0)), pltpu.roll(here_u, 1, 0))
        down = jnp.where(
            row8 == ROWS - 1,
            jnp.where(final, 0.0, pltpu.roll(after, ROWS - 1, 0)),
            pltpu.roll(here_u, ROWS - 1, 0),
        )
        west = jnp.where(lane8 == 0, 0.0, left(here_v))
        east = jnp.where(lane8 == col_count - 1, 0.0, right(here_v))
        change = 0.5 * ((down - up) + (east - west))
        block_row = blk * block_rows + base // BLOCK
        mask = jnp.concatenate(
            [jnp.full((ROWS, LANES), ocean_at(ocean, block_row, sub * tiles + t), F32) for t in range(tiles)], axis=1
        )
        partial = mask * change
        fp_ref[rows] = partial
        fields = [partial, cx[rows], cy[rows], cxy[rows], cxm[rows], cp_ref[rows], here_v, here_u]
        to_west = jnp.zeros((ROWS, LANES), F32)
        to_east = to_west
        for f, field in enumerate(fields):
            at = 4 * f + 32 * k
            chosen = (lane1 >= at) & (lane1 < at + HALO)
            to_west = jnp.where(chosen, pltpu.roll(field[:, :LANES], at, 1), to_west)
            to_east = jnp.where(chosen, pltpu.roll(field[:, -LANES:], (at + HALO) % LANES, 1), to_east)
        at = 4 * 6 + 32 * k
        extra = pltpu.roll(fields[4][:, :LANES], (at + 1 - HALO) % LANES, 1)
        to_west = jnp.where(lane1 == at + 1, extra, to_west)
        extra = pltpu.roll(fields[3][:, -LANES:], (at + HALO + 1) % LANES, 1)
        to_east = jnp.where(lane1 == at, extra, to_east)
        packed = pl.ds(pl.multiple_of(g * ROWS, ROWS), ROWS)
        old_a = jnp.where(even, to_east, to_west)
        old_b = jnp.where(even, to_west, to_east)
        if k == 0:
            pack_a[packed] = old_a
            pack_b[packed] = old_b
        else:
            pack_a[packed] = pack_a[packed] + old_a
            pack_b[packed] = pack_b[packed] + old_b
        return 0

    for k in range(4):
        lax.fori_loop(0, quarter // ROWS, functools.partial(force_group, k), 0)
    fue_ref[0:ROWS] = fu[0:ROWS]
    fue_ref[ROWS : 2 * ROWS] = fu[row_count - ROWS : row_count]


def side_tiles(send_a, send_b, recv_a, recv_b, even, packed):
    own_a, own_b, got_a, got_b = send_a[packed], send_b[packed], recv_a[packed], recv_b[packed]
    pick = lambda a, b: jnp.where(even, a, b)
    return pick(own_b, own_a), pick(own_a, own_b), pick(got_b, got_a), pick(got_a, got_b)


def outer_tile(from_west, from_east, f, k):
    lane1 = lane_of(from_west.shape)
    at = 4 * f + 32 * k
    east = pltpu.roll(from_east, (-at) % LANES, 1)
    west = pltpu.roll(from_west, (LANES - HALO - at) % LANES, 1)
    tile = jnp.where(lane1 < HALO, east, jnp.where(lane1 >= LANES - HALO, west, 0.0))
    if f == 3:
        extra = pltpu.roll(from_west, (LANES - HALO - 1 - 4 * 6 - 32 * k) % LANES, 1)
        tile = jnp.where(lane1 == LANES - HALO - 1, extra, tile)
    if f == 4:
        extra = pltpu.roll(from_east, (HALO - 4 * 6 - 1 - 32 * k) % LANES, 1)
        tile = jnp.where(lane1 == HALO, extra, tile)
    return tile


def force_with_sides(partial, mask, sides, k):
    own_west, own_east, from_west, from_east = sides
    lane1 = lane_of(own_west.shape)
    first, last = 4 * 6 + 32 * k, 4 * 6 + 3 + 32 * k
    outer = outer_tile(from_west, from_east, 0, k)
    tail = pltpu.roll(own_east, (-last) % LANES, 1)
    head = pltpu.roll(own_west, (LANES - 1 - first) % LANES, 1)
    change = jnp.where(lane1 == 0, -tail, jnp.where(lane1 == LANES - 1, head, 0.0))
    outer = outer + 0.5 * mask[:, -LANES:] * change
    begin = partial[:, :LANES] - jnp.where(
        lane1 == 0, 0.5 * mask[:, :LANES] * pltpu.roll(from_west, (-last) % LANES, 1), 0.0
    )
    middle = partial[:, LANES:-LANES]
    end = partial[:, -LANES:] + jnp.where(
        lane1 == LANES - 1,
        0.5 * mask[:, -2 * LANES : -LANES] * pltpu.roll(from_east, (LANES - 1 - first) % LANES, 1),
        0.0,
    )
    return jnp.concatenate([begin, middle, end, outer], axis=1)


def mask_row(ocean, block_row, sub, tiles):
    lane1 = lane_of((1, LANES))
    parts = [jnp.full((1, LANES), ocean_at(ocean, block_row, sub * tiles + t), F32) for t in range(tiles)]
    east = ocean_at(ocean, block_row, (sub + 1) * tiles)
    west = ocean_at(ocean, block_row, sub * tiles - 1)
    parts.append(jnp.where(lane1 < LANES // 2, east, west))
    return jnp.concatenate(parts, axis=1)


def edge_kernel(ids, ocean, fp, cx, cy, cxy, cxm, cp, fue, send_a, send_b, recv_a, recv_b, rows_a, rows_b):
    row_count, col_count = fp.shape
    tiles = col_count // LANES
    block_rows = row_count // BLOCK
    blk, sub = ids[0], ids[1]
    even_sub, even_blk = (sub % 2) == 0, (blk % 2) == 0
    quarter = row_count // 4
    row8 = row_of((ROWS, col_count + LANES))
    lane8 = lane_of((ROWS, col_count + LANES))
    crosses_west = (lane8 == 0) | (lane8 == col_count)
    crosses_east = (lane8 == col_count - 1) | (lane8 == col_count + LANES - 1)
    results = []
    for top in (True, False):
        base = 0 if top else row_count - ROWS
        k = base // quarter
        rows = slice(base, base + ROWS)
        packed = slice(base % quarter, base % quarter + ROWS)
        sides = side_tiles(send_a, send_b, recv_a, recv_b, even_sub, packed)
        block_row = blk * block_rows + base // BLOCK
        mask = jnp.broadcast_to(mask_row(ocean, block_row, sub, tiles), (ROWS, col_count + LANES))
        fields = [force_with_sides(fp[rows], mask, sides, k)]
        for f, field in enumerate([cx, cy, cxy, cxm, cp]):
            fields.append(jnp.concatenate([field[rows], outer_tile(sides[2], sides[3], f + 1, k)], axis=1))
        flux = jnp.concatenate(
            [fue[0:ROWS] if top else fue[ROWS : 2 * ROWS], outer_tile(sides[2], sides[3], 7, k)], axis=1
        )
        if top:
            fields[1] = jnp.where(row8 == 3, pltpu.roll(flux, 3, 0), fields[1])
            half = lambda v: v
        else:
            side = jnp.where(crosses_west, left(fields[2]) + left(pltpu.roll(fields[3], 1, 0)), 0.0)
            side = side + jnp.where(crosses_east, right(pltpu.roll(fields[4], 1, 0)), 0.0)
            fields[5] = fields[5] + jnp.where(row8 == 4, side, 0.0)
            fields[2] = jnp.where(row8 == 4, pltpu.roll(flux, 5, 0), fields[2])
            half = lambda v: pltpu.roll(v, 4, 0)
        pieces = []
        for pair in range(3):
            one, two = half(fields[2 * pair]), half(fields[2 * pair + 1])
            pieces.append(jnp.where(row8 < 4, one, pltpu.roll(two, 4, 0)))
        results.append(pieces)
    for pair in range(3):
        rows = slice(pair * ROWS, (pair + 1) * ROWS)
        rows_a[rows] = jnp.where(even_blk, results[1][pair], results[0][pair])
        rows_b[rows] = jnp.where(even_blk, results[0][pair], results[1][pair])


def basis_kernel(
    ids, ocean, fp, cx, cy, cxy, cxm, cp, fue, send_a, send_b, recv_a, recv_b, rows_a, rows_b,
    c0, c1, c2, c3, c4, center_ref, gram_ref,
    wx, wy, wxy, wxm, nx, nxy, nxm, inv, v0, v1, v2, v3,
):
    row_count, col_count = fp.shape
    tiles = col_count // LANES
    wide = col_count + LANES
    block_rows = row_count // BLOCK
    quarter = row_count // 4
    groups = row_count // ROWS
    blk, sub = ids[0], ids[1]
    even_sub, even_blk = (sub % 2) == 0, (blk % 2) == 0
    row8 = row_of((ROWS, wide))
    lane8 = lane_of((ROWS, wide))

    def at(g):
        return pl.ds(pl.multiple_of(g * ROWS, ROWS), ROWS)

    pick = lambda flag, a, b: jnp.where(flag, a, b)
    pieces = []
    for pair in range(3):
        rows = slice(pair * ROWS, (pair + 1) * ROWS)
        below = pick(even_blk, rows_a[rows], rows_b[rows])
        above = pick(even_blk, rows_b[rows], rows_a[rows])
        pieces.append(jnp.where(row8 < 4, below, pltpu.roll(above, 4, 0)))
        pieces.append(jnp.where(row8 < 4, pltpu.roll(below, 4, 0), above))
    force_out, x_out, y_out, xy_out, xm_out, center_out = pieces
    flux_below = x_out[3:4]
    flux_above = y_out[4:5]
    for k in range(4):

        def widen(g, _, k=k):
            group = k * (quarter // ROWS) + g
            rows = at(group)
            sides = side_tiles(send_a, send_b, recv_a, recv_b, even_sub, at(g))
            for f, (own, ring) in enumerate([(cx, wx), (cy, wy), (cxy, wxy), (cxm, wxm), (cp, inv)]):
                ring[at(group + 1)] = jnp.concatenate(
                    [own[rows], outer_tile(sides[2], sides[3], f + 1, k)], axis=1
                )
            mask = jnp.broadcast_to(
                mask_row(ocean, blk * block_rows + group * ROWS // BLOCK, sub, tiles), (ROWS, wide)
            )
            v0[at(group + 1)] = force_with_sides(fp[rows], mask, sides, k)
            return 0

        lax.fori_loop(0, quarter // ROWS, widen, 0)

    for ring, out in [(wx, x_out), (wy, y_out), (wxy, xy_out), (wxm, xm_out)]:
        ring[at(groups + 1)] = out
        ring[at(0)] = out

    packed_first = slice(0, ROWS)
    packed_last = slice(quarter - ROWS, quarter)
    sides_first = side_tiles(send_a, send_b, recv_a, recv_b, even_sub, packed_first)
    sides_last = side_tiles(send_a, send_b, recv_a, recv_b, even_sub, packed_last)
    flux_first = jnp.concatenate([fue[0:1], outer_tile(sides_first[2], sides_first[3], 7, 0)[0:1]], axis=1)
    flux_last = jnp.concatenate(
        [fue[2 * ROWS - 1 : 2 * ROWS], outer_tile(sides_last[2], sides_last[3], 7, 3)[ROWS - 1 : ROWS]], axis=1
    )
    mask_first = mask_row(ocean, blk * block_rows, sub, tiles)
    mask_last = mask_row(ocean, (blk + 1) * block_rows - 1, sub, tiles)
    mask_below = mask_row(ocean, (blk + 1) * block_rows, sub, tiles)
    mask_above = mask_row(ocean, blk * block_rows - 1, sub, tiles)
    v0[at(1)] = v0[at(1)] - jnp.where(row8 == 0, 0.5 * mask_first * flux_above, 0.0)
    v0[at(groups)] = v0[at(groups)] + jnp.where(row8 == ROWS - 1, 0.5 * mask_last * flux_below, 0.0)
    force_out = force_out - jnp.where(row8 == 0, 0.5 * mask_below * flux_last, 0.0)
    force_out = force_out + jnp.where(row8 == ROWS - 1, 0.5 * mask_above * flux_first, 0.0)
    v0[at(groups + 1)] = force_out
    inv[at(groups + 1)] = center_out

    crosses_west = (lane8 == 0) | (lane8 == col_count)
    crosses_east = (lane8 == col_count - 1) | (lane8 == wide - 1)

    def scale(g, _):
        ring = at(g + 1)
        before = at(g)
        shift = lambda ref: jnp.where(row8 == 0, pltpu.roll(ref[before], 1, 0), pltpu.roll(ref[ring], 1, 0))
        up_x, up_xy, up_xm = shift(wx), shift(wxy), shift(wxm)
        nx[ring] = up_x
        nxy[ring] = up_xy
        nxm[ring] = up_xm
        crosses_row = (row8 == 0) & ((g == 0) | (g == groups))
        total = inv[ring]
        total = total + jnp.where(crosses_row, up_x, 0.0)
        open_row = (row8 != 4) | (g < groups)
        total = total + jnp.where(open_row & crosses_west, left(wy[ring]), 0.0)
        total = total + jnp.where(crosses_row | (open_row & crosses_west), left(up_xy), 0.0)
        total = total + jnp.where(crosses_row | (open_row & crosses_east), right(up_xm), 0.0)
        own_row = blk * block_rows + g * ROWS // BLOCK
        own = mask_row(ocean, own_row, sub, tiles)
        mask = jnp.where(g == groups, jnp.where(row8 < 4, mask_below, mask_above), own)
        inverse = jnp.where(mask > 0.0, 1.0 / jnp.where(mask > 0.0, total, 1.0), 0.0)
        inv[ring] = inverse
        scaled = v0[ring] * inverse
        v0[ring] = scaled

        @pl.when(g < groups)
        def _():
            center_ref[at(g)] = total[:, :col_count]
            c0[at(g)] = scaled[:, :col_count]

        return 0

    lax.fori_loop(0, groups + 1, scale, 0)

    def wrap(ref):
        ref[at(0)] = ref[at(groups + 1)]
        ref[at(groups + 2)] = ref[at(1)]

    def spread(source, g):
        ring = at(g + 1)
        here, before, after = source[ring], source[at(g)], source[at(g + 2)]
        up = jnp.where(row8 == 0, pltpu.roll(before, 1, 0), pltpu.roll(here, 1, 0))
        down = jnp.where(row8 == ROWS - 1, pltpu.roll(after, ROWS - 1, 0), pltpu.roll(here, ROWS - 1, 0))
        side = wy[ring]
        total = wx[ring] * down + nx[ring] * up
        total = total + side * right(here)
        total = total + wxy[ring] * right(down) + wxm[ring] * left(down)
        total = total + left(side * here + nxy[ring] * up)
        total = total + right(nxm[ring] * up)
        return inv[ring] * total, here

    def step(source, target, out, subtract):
        def body(g, _):
            moved, here = spread(source, g)
            result = here - moved if subtract else moved
            target[at(g + 1)] = result

            @pl.when(g < groups)
            def _():
                out[at(g)] = result[:, :col_count]

            return 0

        lax.fori_loop(0, groups + 1, body, 0)
        wrap(target)

    wrap(v0)
    step(v0, v1, c1, True)
    step(v1, v2, c2, False)
    step(v2, v3, c3, False)

    def last(g, sums):
        moved, here = spread(v3, g)
        rows = at(g)
        final = moved[:, :col_count]
        c4[rows] = final
        basis = [c0[rows], c1[rows], c2[rows], here[:, :col_count], final]
        center = center_ref[rows]
        weighted = [center * b for b in basis]
        new = []
        for (i, j), total in zip(PAIRS, sums):
            product = basis[i] * weighted[j]
            part = product[:, :LANES]
            for t in range(1, tiles):
                part = part + product[:, t * LANES : (t + 1) * LANES]
            new.append(total + part)
        return tuple(new)

    empty = tuple(jnp.zeros((ROWS, LANES), F32) for _ in PAIRS)
    sums = lax.fori_loop(0, groups, last, empty)
    lane1 = lane_of((1, LANES))
    packed = jnp.zeros((1, LANES), F32)
    for index, total in enumerate(sums):
        packed = jnp.where(lane1 == index, jnp.sum(jnp.sum(total, axis=0, keepdims=True), axis=1, keepdims=True), packed)
    gram_ref[...] = jnp.broadcast_to(packed, gram_ref.shape)


def finish_kernel(gram_ref, c0, c1, c2, c3, c4, center_ref, height_ref, residual_ref):
    lane1 = lane_of((1, LANES))
    entries = jnp.sum(gram_ref[...], axis=0, keepdims=True)
    size = ITERS + 1
    gram = {}
    for index, (i, j) in enumerate(PAIRS):
        entry = jnp.sum(jnp.where(lane1 == index, entries, 0.0), axis=1, keepdims=True)
        gram[i, j] = entry
        gram[j, i] = entry
    zero = jnp.zeros((1, 1), F32)
    one = jnp.ones((1, 1), F32)

    def image(coefs):
        result = [zero, coefs[0] + coefs[1]]
        for j in range(2, size):
            own = coefs[j] if j < size - 1 else zero
            result.append(own - coefs[j - 1])
        return result

    def form(one_side, products):
        total = zero
        for a, b in zip(one_side, products):
            total = total + a * b
        return total

    scaled = [one] + [zero] * (size - 1)
    search = [zero] * size
    height = [zero] * size
    rho_old, sigma = one, zero
    for iteration in range(ITERS):
        limit = iteration + 1
        products = []
        for j in range(size):
            total = zero
            for i in range(limit):
                total = total + scaled[i] * gram[i, j]
            products.append(total)
        rho = form(scaled[:limit], products)
        curvature = form(image(scaled)[: limit + 1], products)
        beta = rho / rho_old
        sigma = curvature - beta * beta * sigma
        alpha = rho / sigma
        rho_old = rho
        search = [s + beta * q for s, q in zip(scaled, search)]
        height = [h + alpha * q for h, q in zip(height, search)]
        scaled = [s - alpha * q for s, q in zip(scaled, image(search))]

    def combine(g, _):
        rows = pl.ds(pl.multiple_of(g * ROWS, ROWS), ROWS)
        basis = [ref[rows] for ref in (c0, c1, c2, c3, c4)]
        total = height[0] * basis[0]
        for j in range(1, size - 1):
            total = total + height[j] * basis[j]
        height_ref[rows] = total
        total = scaled[0] * basis[0]
        for j in range(1, size):
            total = total + scaled[j] * basis[j]
        residual_ref[rows] = center_ref[rows] * total
        return 0

    lax.fori_loop(0, c0.shape[0] // ROWS, combine, 0)


def swap(value, axis, parity):
    peers = lax.axis_size(axis)
    pairs = []
    for i in range(parity, peers - 1, 2):
        pairs += [(i, i + 1), (i + 1, i)]
    return lax.ppermute(value, axis, pairs)


def body(u_flow, v_flow, thickness, depth_levels, block_ocean, coef_x, coef_y, coef_xy, coef_xm, extra_diagonal):
    levels, row_count, col_count = u_flow.shape
    wide = col_count + LANES
    plane = jax.ShapeDtypeStruct((row_count, col_count), F32)
    strip = jax.ShapeDtypeStruct((row_count // 4, LANES), F32)
    ids = jnp.stack([lax.axis_index("blk"), lax.axis_index("sub")]).astype(jnp.int32)
    flow = pltpu.VMEM((levels, row_count, col_count), F32)
    field = pltpu.VMEM((row_count, col_count), F32)
    fp, cp, fue, send_a, send_b = pl.pallas_call(
        flux_kernel,
        out_shape=(plane, plane, jax.ShapeDtypeStruct((2 * ROWS, col_count), F32), strip, strip),
        in_specs=[SMEM, SMEM, SMEM] + [HBM] * 8,
        out_specs=(VMEM,) * 5,
        scratch_shapes=[flow, flow, pltpu.VMEM((row_count, col_count), jnp.int32)]
        + [field] * 7
        + [pltpu.SemaphoreType.DMA((2, row_count // CHUNK)), pltpu.SemaphoreType.DMA((6,))],
        compiler_params=pltpu.CompilerParams(vmem_limit_bytes=40 << 20),
        name="flux",
    )(ids, thickness, block_ocean, u_flow, v_flow, depth_levels, coef_x, coef_y, coef_xy, coef_xm, extra_diagonal)
    recv_a, recv_b = swap(send_a, "sub", 0), swap(send_b, "sub", 1)
    edge = jax.ShapeDtypeStruct((3 * ROWS, wide), F32)
    edge_a, edge_b = pl.pallas_call(
        edge_kernel,
        out_shape=(edge, edge),
        in_specs=[SMEM, SMEM] + [VMEM] * 11,
        out_specs=(VMEM,) * 2,
        compiler_params=pltpu.CompilerParams(vmem_limit_bytes=16 << 20),
        name="edge",
    )(ids, block_ocean, fp, coef_x, coef_y, coef_xy, coef_xm, cp, fue, send_a, send_b, recv_a, recv_b)
    rows_a, rows_b = swap(edge_a, "blk", 0), swap(edge_b, "blk", 1)
    devices = lax.axis_size("blk") * lax.axis_size("sub")
    ring = pltpu.VMEM((row_count + 3 * ROWS, wide), F32)
    *basis, center, gram = pl.pallas_call(
        basis_kernel,
        out_shape=(plane,) * 6 + (jax.ShapeDtypeStruct((devices, LANES), F32),),
        in_specs=[SMEM, SMEM] + [VMEM] * 13,
        out_specs=(VMEM,) * 7,
        scratch_shapes=[ring] * 12,
        compiler_params=pltpu.CompilerParams(vmem_limit_bytes=32 << 20),
        name="basis",
    )(
        ids, block_ocean, fp, coef_x, coef_y, coef_xy, coef_xm, cp, fue,
        send_a, send_b, recv_a, recv_b, rows_a, rows_b,
    )
    gram = lax.all_to_all(gram, ("blk", "sub"), 0, 0, tiled=True)
    return pl.pallas_call(
        finish_kernel,
        out_shape=(plane, plane),
        in_specs=[VMEM] * 7,
        out_specs=(VMEM,) * 2,
        compiler_params=pltpu.CompilerParams(vmem_limit_bytes=16 << 20),
        name="finish",
    )(gram, *basis, center)


def solution(mesh):
    placed = (
        P(None, "blk", "sub"),
        P(None, "blk", "sub"),
        P(),
        P("blk", "sub"),
        P(),
        P("blk", "sub"),
        P("blk", "sub"),
        P("blk", "sub"),
        P("blk", "sub"),
        P("blk", "sub"),
    )
    return jax.shard_map(
        body,
        mesh=mesh,
        in_specs=placed,
        out_specs=(P("blk", "sub"), P("blk", "sub")),
        check_vma=False,
    )
```

time: 402 us -> 73.5 us (0.18)
  blocking collectives: 174 us -> 20.4 us
  other arithmetic: 102 us -> 0.08 us
  starting transfers between devices: 64.8 us -> 4.5 us
  Pallas kernels: 0 us -> 34.5 us
  local copies, waits for them, and re-layouts: 27.6 us -> 11 us
  waiting for transfers between devices: 16.9 us -> 1.8 us
  between operations: 13.2 us -> 0.69 us
    psum x4 -> x0, blocking collectives: 174 us -> none  [chron_gear(): lax.psum((jnp.sum(residual * scaled), jnp.sum(scaled * applied)), ('blk',...]
    ppermute x24 -> x4, starting transfers between devices: 64.8 us -> 4.5 us  [swap(): return lax.ppermute(value, axis, pairs)]
    add x32 -> x0, other arithmetic: 60.1 us -> none  [the longest x16 30.7 us: add_level(): totals[1] + active * v_flow[level_index]]
    pallas_call x0 -> x4, Pallas kernels: none -> 34.5 us  [the longest x1 20.6 us: body(): pl.pallas_call(basis_kernel, out_shape=(plane,) * 6 + (jax.ShapeDtypeStru...]
    all_to_all x0 -> x1, blocking collectives: none -> 20.4 us  [body(): gram = lax.all_to_all(gram, ('blk', 'sub'), 0, 0, tiled=True)]
    ppermute x24 -> x4, waiting for transfers between devices: 16.9 us -> 1.8 us  [swap(): return lax.ppermute(value, axis, pairs)]
    concatenate x10 -> x0, other arithmetic: 15.1 us -> none  [padded_2(): value = jnp.concatenate([before, value, after], axis=dim)]
    reduce_sum x4 -> x0, other arithmetic: 9.76 us -> none  [chron_gear(): jnp.sum(scaled * applied)]
  transfers between devices with their start and end apart: 24 -> 4, of which waited for: 12 -> 2; matrix products, arithmetic and copies ran while one was open for 24% -> 0% of each run, Pallas kernels for 0% -> 0%
where the time goes in v1:
time: 73.5 us; the launch traced here: 73 us
  Pallas kernels  34.5 us (47%)
  blocking collectives  20.4 us (28%)
  local copies, waits for them, and re-layouts  11 us (15%)
  starting transfers between devices  4.5 us (6%)
  waiting for transfers between devices  1.8 us (2%)
    pallas_call x1, Pallas kernels, body(): pl.pallas_call(basis_kernel, out_shape=(plane,) * 6 + (jax.ShapeDtypeStru...  20.6 us
    all_to_all x1, blocking collectives, body(): gram = lax.all_to_all(gram, ('blk', 'sub'), 0, 0, tiled=True)  20.4 us
    pallas_call x1, Pallas kernels, body(): pl.pallas_call(flux_kernel, out_shape=(plane, plane, jax.ShapeDtypeStruct...  11.5 us
    unnamed x18, local copies, waits for them, and re-layouts  11 us
    ppermute x4, starting transfers between devices, swap(): return lax.ppermute(value, axis, pairs)  4.5 us
    ppermute x4, waiting for transfers between devices, swap(): return lax.ppermute(value, axis, pairs)  1.8 us
    pallas_call x1, Pallas kernels, body(): pl.pallas_call(finish_kernel, out_shape=(plane, plane), in_specs=[VMEM] *...  1.6 us
  transfers between devices with their start and end apart: 4, of which 2 were waited for; matrix products, arithmetic and copies ran while one was open for 0% of the time, Pallas kernels for 0%

profile of v1, /device:TPU:0, one launch (start us, length us, event | category | flops | bytes accessed | tf_op | source)
XLA Modules:
  0.0 73.0 jit_solution(70195097311596218)
XLA Ops:
  0.6 0.1 pad_add_fusion.ids
  0.7 0.0 copy-start
  0.7 3.4 %copy-done = f32[16,256,512]{2,1,0:T(8,128)S(1)} copy-done((f32[16,256,512]{2,1,0:T(8,128)S(1)}, f32[16,256,512]{2,1,0:T(8,128)}, u32[]{:S(2)}) %copy-start) | copy-done | bytes 8388632
  4.1 0.0 copy-start.1
  4.1 1.0 %copy-done.1 = f32[256,512]{1,0:T(8,128)S(1)} copy-done((f32[256,512]{1,0:T(8,128)S(1)}, f32[256,512]{1,0:T(8,128)}, u32[]{:S(2)}) %copy-start.1) | copy-done | bytes 524312
  5.1 0.0 copy-start.2
  5.1 1.0 %copy-done.2 = f32[256,512]{1,0:T(8,128)S(1)} copy-done((f32[256,512]{1,0:T(8,128)S(1)}, f32[256,512]{1,0:T(8,128)}, u32[]{:S(2)}) %copy-start.2) | copy-done | bytes 524312
  6.2 0.0 copy-start.3
  6.2 1.0 %copy-done.3 = f32[256,512]{1,0:T(8,128)S(1)} copy-done((f32[256,512]{1,0:T(8,128)S(1)}, f32[256,512]{1,0:T(8,128)}, u32[]{:S(2)}) %copy-start.3) | copy-done | bytes 524312
  7.2 0.0 copy-start.4
  7.2 1.0 %copy-done.4 = f32[256,512]{1,0:T(8,128)S(1)} copy-done((f32[256,512]{1,0:T(8,128)S(1)}, f32[256,512]{1,0:T(8,128)}, u32[]{:S(2)}) %copy-start.4) | copy-done | bytes 524312
  8.3 0.0 copy-start.5
  8.3 1.0 %copy-done.5 = s32[256,512]{1,0:T(8,128)S(1)} copy-done((s32[256,512]{1,0:T(8,128)S(1)}, s32[256,512]{1,0:T(8,128)}, u32[]{:S(2)}) %copy-start.5) | copy-done | bytes 524312
  9.3 0.0 copy-start.6
  9.3 1.0 %copy-done.6 = f32[256,512]{1,0:T(8,128)S(1)} copy-done((f32[256,512]{1,0:T(8,128)S(1)}, f32[256,512]{1,0:T(8,128)}, u32[]{:S(2)}) %copy-start.6) | copy-done | bytes 524312
  10.3 0.0 copy-start.7
  10.3 0.7 copy-done.7
  11.0 0.0 copy-start.8
  11.0 0.7 copy-done.8
  11.7 11.5 %flux.1 = (f32[256,512]{1,0:T(8,128)S(1)}, f32[256,512]{1,0:T(8,128)S(1)}, f32[16,512]{1,0:T(8,128)S(1)}, f32[64,128]{1,0:T(8,128)S(1)}, f32[64,128]{1,0:T(8,128)S(1)}) custom-call(s32[2]{0:T(128)S(1)} %pad_add_fusion.ids, f32[16]{0:T(128)S(1)} %copy-done.8, s32[16,16]{1,0:T(8,128)S(1)} %copy-done.7, f32[16,256,512]{2,1,0:T(8,128)S(1)} %copy-done, ...), custom_call_target="tpu_custom_call" | custom-call | tf_op jit(solution)/shard_map/flux/pallas_call | solution.py:525
  23.2 3.1 %collective-permute-start = (f32[64,128]{1,0:T(8,128)S(1)}, f32[64,128]{1,0:T(8,128)S(1)}, u32[]{:S(2)}, u32[]{:S(2)}) collective-permute-start(f32[64,128]{1,0:T(8,128)S(1)} %get-tuple-element.19.send_a), channel_id=1, source_target_pairs={{0,1},{1,0},{2,3},{3,2},{4,5},{5,4},{6,7},{7,6},{8,9},{9,8},{10,11... | collective-permute-start | bytes 98312 | tf_op jit(solution)/shard_map/ppermute | solution.py:514
  26.3 0.7 collective-permute-start.1
  27.0 1.2 %collective-permute-done.recv_a = f32[64,128]{1,0:T(8,128)S(1)} collective-permute-done((f32[64,128]{1,0:T(8,128)S(1)}, f32[64,128]{1,0:T(8,128)S(1)}, u32[]{:S(2)}, u32[]{:S(2)}) %collective-permute-start) | collective-permute-done | bytes 32800 | tf_op jit(solution)/shard_map/ppermute | solution.py:514
  28.2 0.0 collective-permute-done.1.recv_b
  28.2 0.8 %edge.1 = (f32[24,640]{1,0:T(8,128)S(1)}, f32[24,640]{1,0:T(8,128)S(1)}) custom-call(s32[2]{0:T(128)S(1)} %pad_add_fusion.ids, s32[16,16]{1,0:T(8,128)S(1)} %copy-done.7, f32[256,512]{1,0:T(8,128)S(1)} %get-tuple-element.16.fp, f32[256,512]{1,0:T(8,128)S(1)} %copy-done.1, f32[256,512]{1,0:T(8,128)S(1)} %copy-done.2, f32[256,512]{1,0:T(8,128)S(1)} %copy-done.3, ...), custom_call_target="tpu_custom_call" | custom-call | tf_op jit(solution)/shard_map/edge/pallas_call | solution.py:538
  29.1 0.1 collective-permute-start.2
  29.1 0.7 collective-permute-start.3
  29.8 0.6 collective-permute-done.2.rows_a
  30.4 0.0 collective-permute-done.3.rows_b
  30.4 20.6 %basis.1 = (f32[256,512]{1,0:T(8,128)S(1)}, f32[256,512]{1,0:T(8,128)S(1)}, f32[256,512]{1,0:T(8,128)S(1)}, f32[256,512]{1,0:T(8,128)S(1)}, f32[256,512]{1,0:T(8...) custom-call(s32[2]{0:T(128)S(1)} %pad_add_fusion.ids, s32[16,16]{1,0:T(8,128)S(1)} %copy-done.7, ...), custom_call_target="tpu_custom_call" | custom-call | tf_op jit(solution)/shard_map/basis/pallas_call | solution.py:549
  51.0 20.4 %all_to_all.11 = f32[32,1,128]{2,1,0:T(1,128)S(1)} all-to-all(f32[32,1,128]{2,1,0:T(1,128)S(1)} %bitcast.7), channel_id=1, replica_groups=mesh['blk'=8,'sub'=4] {'blk','sub'}, dimensions={0} | all-to-all | bytes 32768 | tf_op jit(solution)/shard_map/all_to_all | solution.py:561
  71.4 1.6 %finish.1 = (f32[256,512]{1,0:T(8,128)}, f32[256,512]{1,0:T(8,128)}) custom-call(f32[32,128]{1,0:T(8,128)S(1)} %bitcast.6, f32[256,512]{1,0:T(8,128)S(1)} %get-tuple-element.24.c0, f32[256,512]{1,0:T(8,128)S(1)} %get-tuple-element.25.c1, f32[256,512]{1,0:T(8,128)S(1)} %get-tuple-element.26.c2, f32[256,512]{1,0:T(8,128)S(1)} %get-tuple-element.27.c3, ...), custom_call_target="tpu_custom_call" | custom-call | tf_op jit(solution)/shard_map/finish/pallas_call | solution.py:562
Async XLA Ops:
  0.7 3.4 %copy-start = (f32[16,256,512]{2,1,0:T(8,128)S(1)}, f32[16,256,512]{2,1,0:T(8,128)}, u32[]{:S(2)}) copy-start(f32[16,256,512]{2,1,0:T(8,128)} %u_hbm.1) | copy-start | bytes 25165828
  4.1 1.0 %copy-start.1 = (f32[256,512]{1,0:T(8,128)S(1)}, f32[256,512]{1,0:T(8,128)}, u32[]{:S(2)}) copy-start(f32[256,512]{1,0:T(8,128)} %cx.3) | copy-start | bytes 1572868
  5.1 1.0 %copy-start.2 = (f32[256,512]{1,0:T(8,128)S(1)}, f32[256,512]{1,0:T(8,128)}, u32[]{:S(2)}) copy-start(f32[256,512]{1,0:T(8,128)} %cy.3) | copy-start | bytes 1572868
  6.2 1.0 %copy-start.3 = (f32[256,512]{1,0:T(8,128)S(1)}, f32[256,512]{1,0:T(8,128)}, u32[]{:S(2)}) copy-start(f32[256,512]{1,0:T(8,128)} %cxy.3) | copy-start | bytes 1572868
  7.2 1.0 %copy-start.4 = (f32[256,512]{1,0:T(8,128)S(1)}, f32[256,512]{1,0:T(8,128)}, u32[]{:S(2)}) copy-start(f32[256,512]{1,0:T(8,128)} %cxm.3) | copy-start | bytes 1572868
  8.3 1.0 %copy-start.5 = (s32[256,512]{1,0:T(8,128)S(1)}, s32[256,512]{1,0:T(8,128)}, u32[]{:S(2)}) copy-start(s32[256,512]{1,0:T(8,128)} %depth_hbm.1) | copy-start | bytes 1572868
  9.3 1.0 %copy-start.6 = (f32[256,512]{1,0:T(8,128)S(1)}, f32[256,512]{1,0:T(8,128)}, u32[]{:S(2)}) copy-start(f32[256,512]{1,0:T(8,128)} %ex_hbm.1) | copy-start | bytes 1572868
  10.3 0.7 copy-start.7
  11.0 0.7 copy-start.8
  23.2 5.0 %collective-permute-start = (f32[64,128]{1,0:T(8,128)S(1)}, f32[64,128]{1,0:T(8,128)S(1)}, u32[]{:S(2)}, u32[]{:S(2)}) collective-permute-start(f32[64,128]{1,0:T(8,128)S(1)} %get-tuple-element.19.send_a), channel_id=1, source_target_pairs={{0,1},{1,0},{2,3},{3,2},{4,5},{5,4},{6,7},{7,6},{8,9},{9,8},{10,11... | collective-permute-start | bytes 98312 | tf_op jit(solution)/shard_map/ppermute | solution.py:514
  26.3 1.9 %collective-permute-start.1 = (f32[64,128]{1,0:T(8,128)S(1)}, f32[64,128]{1,0:T(8,128)S(1)}, u32[]{:S(2)}, u32[]{:S(2)}) collective-permute-start(f32[64,128]{1,0:T(8,128)S(1)} %get-tuple-element.20.send_b), channel_id=1, source_target_pairs={{1,2},{2,1},{5,6},{6,5},{9,10},{10,9},{13,14},{14,13},{17,18},{18,... | collective-permute-start | bytes 98312 | tf_op jit(solution)/shard_map/ppermute | solution.py:514
  29.1 1.3 %collective-permute-start.2 = (f32[24,640]{1,0:T(8,128)S(1)}, f32[24,640]{1,0:T(8,128)S(1)}, u32[]{:S(2)}, u32[]{:S(2)}) collective-permute-start(f32[24,640]{1,0:T(8,128)S(1)} %get-tuple-element.21), channel_id=1, source_target_pairs={{0,4},{4,0},{8,12},{12,8},{16,20},{20,16},{24,28},{28,24},{1,5},{5... | collective-permute-start | bytes 184328 | tf_op jit(solution)/shard_map/ppermute | solution.py:514
  29.1 1.2 %collective-permute-start.3 = (f32[24,640]{1,0:T(8,128)S(1)}, f32[24,640]{1,0:T(8,128)S(1)}, u32[]{:S(2)}, u32[]{:S(2)}) collective-permute-start(f32[24,640]{1,0:T(8,128)S(1)} %get-tuple-element.22), channel_id=1, source_target_pairs={{4,8},{8,4},{12,16},{16,12},{20,24},{24,20},{5,9},{9,5},{13,17},{1... | collective-permute-start | bytes 184328 | tf_op jit(solution)/shard_map/ppermute | solution.py:514

commit v2 on v1

v2 whole, which is shorter than its diff:
```python
import functools

import jax
import jax.numpy as jnp
from jax import lax
from jax.experimental import pallas as pl
from jax.experimental.pallas import tpu as pltpu
from jax.sharding import PartitionSpec as P

BLOCK = 128
ITERS = 4
HALO = ITERS
LANES = 128
ROWS = 8
CHUNK = 32
AHEAD = 3
UNROLL = 4
F32 = jnp.float32
FLUX_LIMIT = 40 << 20
VMEM = pl.BlockSpec(memory_space=pltpu.VMEM)
SMEM = pl.BlockSpec(memory_space=pltpu.SMEM)
HBM = pl.BlockSpec(memory_space=pltpu.HBM)
PAIRS = [(i, j) for i in range(ITERS) for j in range(i, ITERS + 1)]


def lane_of(shape):
    return lax.broadcasted_iota(jnp.int32, shape, len(shape) - 1)


def row_of(shape):
    return lax.broadcasted_iota(jnp.int32, shape, len(shape) - 2)


def shifted_rows(before, here):
    return jnp.where(row_of(here.shape) == 0, before, here)


def left(value):
    return pltpu.roll(value, 1, 1)


def right(value):
    return pltpu.roll(value, value.shape[1] - 1, 1)


def down(value):
    return pltpu.roll(value, 1, 0)


def two_sum(a, b):
    total = a + b
    other = total - a
    return total, (a - (total - other)) + (b - other)


def ocean_at(ocean_ref, row, col):
    block_rows, block_cols = ocean_ref.shape
    inside = (row >= 0) & (row < block_rows) & (col >= 0) & (col < block_cols)
    entry = ocean_ref[jnp.clip(row, 0, block_rows - 1), jnp.clip(col, 0, block_cols - 1)]
    return jnp.where(inside & (entry == 1), 1.0, 0.0).astype(F32)


def flux_kernel(
    ids, thick, ocean, u_hbm, v_hbm, depth_hbm, cx_hbm, cy_hbm, cxy_hbm, cxm_hbm, ex_hbm,
    fp_ref, cp_ref, edge_ref, pack_a, pack_b, ax, ay, axy, axm, inv, c0,
    u_buf, v_buf, depth, ex, fu, fv, masks, sems, coef_sem,
):
    levels, row_count, col_count = u_buf.shape
    tiles = col_count // LANES
    chunks = row_count // CHUNK
    groups = row_count // ROWS
    steps = CHUNK // ROWS
    blk, sub = ids[0], ids[1]
    block_rows = row_count // BLOCK
    own = (pl.ds(0, row_count), pl.ds(0, col_count))
    coef_copies = [
        pltpu.make_async_copy(src, dst, coef_sem.at[i])
        for i, (src, dst) in enumerate(
            [
                (depth_hbm, depth), (ex_hbm, ex), (cx_hbm, ax.at[own]), (cy_hbm, ay.at[own]),
                (cxy_hbm, axy.at[own]), (cxm_hbm, axm.at[own]),
            ]
        )
    ]

    def flow_copies(c):
        rows = pl.ds(pl.multiple_of(c * CHUNK, CHUNK), CHUNK)
        return (
            pltpu.make_async_copy(u_hbm.at[:, rows, :], u_buf.at[:, rows, :], sems.at[0, c]),
            pltpu.make_async_copy(v_hbm.at[:, rows, :], v_buf.at[:, rows, :], sems.at[1, c]),
        )

    coef_copies[0].start()
    for copy in flow_copies(0):
        copy.start()
    for copy in coef_copies[1:]:
        copy.start()
    for c in range(1, AHEAD):
        for copy in flow_copies(c):
            copy.start()
    for b in range(block_rows):
        for t in range(tiles):
            masks[pl.ds(b * ROWS, ROWS), pl.ds(t * LANES, LANES)] = jnp.full(
                (ROWS, LANES), ocean_at(ocean, blk * block_rows + b, sub * tiles + t), F32
            )
    coef_copies[0].wait()

    row8 = row_of((ROWS, col_count))
    lane8 = lane_of((ROWS, col_count))
    lane1 = lane_of((ROWS, LANES))
    cols = pl.ds(0, col_count)
    even = (sub % 2) == 0

    def at(g):
        return pl.ds(pl.multiple_of(g * ROWS, ROWS), ROWS)

    def west_of(value):
        return jnp.where(lane8 == 0, 0.0, left(value))

    def east_of(value):
        return jnp.where(lane8 == col_count - 1, 0.0, right(value))

    def rolled_fields(rows):
        return [
            down(v) for v in (ax[rows, cols], west_of(axy[rows, cols]), east_of(axm[rows, cols]), fu[rows])
        ]

    def mask_at(g):
        return pl.ds(pl.multiple_of(g * ROWS // BLOCK * ROWS, ROWS), ROWS)

    def sum_group(g):
        rows = at(g)
        for t in range(tiles):
            lanes = pl.ds(t * LANES, LANES)
            mask = masks[mask_at(g), lanes]
            deep = depth[rows, lanes]
            total_u = jnp.zeros((ROWS, LANES), F32)
            total_v = total_u
            for k in range(levels):
                active = jnp.where(deep > k, thick[k], 0.0)
                total_u = total_u + active * u_buf[k, rows, lanes]
                total_v = total_v + active * v_buf[k, rows, lanes]
            fu[rows, lanes] = mask * total_u
            fv[rows, lanes] = mask * total_v

    def group_work(g, k, before):
        rows = at(g)
        here_x, here_y, here_xy, here_xm = ax[rows, cols], ay[rows, cols], axy[rows, cols], axm[rows, cols]
        here_u, here_v = fu[rows], fv[rows]
        west_xy, east_xm, west_y = west_of(here_xy), east_of(here_xm), west_of(here_y)
        rolled = [down(v) for v in (here_x, west_xy, east_xm, here_u)]
        up_x, up_west, up_east, up_u = [shifted_rows(a, b) for a, b in zip(before, rolled)]
        total = ex[rows] + here_x
        total = total + up_x
        total = total + here_y
        total = total + west_y
        total = total + here_xy
        total = total + up_west
        total = total + here_xm
        total = total + up_east
        cp_ref[rows] = total
        after = fu[at(jnp.minimum(g + 1, groups - 1))]
        after = jnp.where(g + 1 < groups, pltpu.roll(after, ROWS - 1, 0), 0.0)
        below = jnp.where(row8 == ROWS - 1, after, pltpu.roll(here_u, ROWS - 1, 0))
        change = 0.5 * ((below - up_u) + (east_of(here_v) - west_of(here_v)))
        mask = masks[mask_at(g)]
        partial = mask * change
        inverse = mask * (1.0 / total)
        fp_ref[rows] = partial
        inv[rows, cols] = inverse
        c0[rows, cols] = partial * inverse
        fields = [partial, here_x, here_y, here_xy, here_xm, total, here_v, here_u]
        to_west = jnp.zeros((ROWS, LANES), F32)
        to_east = to_west
        for f, field in enumerate(fields):
            lane = 4 * f + 32 * k
            chosen = (lane1 >= lane) & (lane1 < lane + HALO)
            to_west = jnp.where(chosen, pltpu.roll(field[:, :LANES], lane, 1), to_west)
            to_east = jnp.where(chosen, pltpu.roll(field[:, -LANES:], (lane + HALO) % LANES, 1), to_east)
        lane = 4 * 6 + 32 * k
        extra = pltpu.roll(here_xm[:, :LANES], (lane + 1 - HALO) % LANES, 1)
        to_west = jnp.where(lane1 == lane + 1, extra, to_west)
        extra = pltpu.roll(here_xy[:, -LANES:], (lane + HALO + 1) % LANES, 1)
        to_east = jnp.where(lane1 == lane, extra, to_east)
        packed = at(g // 4)
        for_a = jnp.where(even, to_east, to_west)
        for_b = jnp.where(even, to_west, to_east)
        if k == 0:
            pack_a[packed] = for_a
            pack_b[packed] = for_b
        else:
            pack_a[packed] = pack_a[packed] + for_a
            pack_b[packed] = pack_b[packed] + for_b
        return rolled

    def work_from(g, k):
        before = rolled_fields(at(jnp.maximum(g - 1, 0)))
        return group_work(g, k, [jnp.where(g > 0, b, 0.0) for b in before])

    def chunk(c, _):
        for copy in flow_copies(c):
            copy.wait()

        @pl.when(c + AHEAD < chunks)
        def _():
            for copy in flow_copies(c + AHEAD):
                copy.start()

        lax.fori_loop(0, steps, lambda i, _: (sum_group(c * steps + i), 0)[1], 0)

        @pl.when(c == 0)
        def _():
            for copy in coef_copies[1:]:
                copy.wait()

        @pl.when(c > 0)
        def _():
            work_from(c * steps - 1, 3)

        carry = work_from(c * steps, 0)
        for k in range(1, steps - 1):
            carry = group_work(c * steps + k, k, carry)
        return 0

    lax.fori_loop(0, chunks, chunk, 0)
    work_from(groups - 1, 3)
    for side, base in enumerate((0, row_count - ROWS)):
        rows = pl.ds(base, ROWS)
        for f, field in enumerate(
            [fp_ref[rows], ax[rows, cols], ay[rows, cols], axy[rows, cols], axm[rows, cols], cp_ref[rows], fu[rows]]
        ):
            edge_ref[pl.ds((side * 7 + f) * ROWS, ROWS)] = field


def side_tiles(send_a, send_b, recv_a, recv_b, even, packed):
    own_a, own_b, got_a, got_b = send_a[packed], send_b[packed], recv_a[packed], recv_b[packed]
    pick = lambda a, b: jnp.where(even, a, b)
    return pick(own_b, own_a), pick(own_a, own_b), pick(got_b, got_a), pick(got_a, got_b)


def outer_tile(from_west, from_east, f, k):
    lane1 = lane_of(from_west.shape)
    at = 4 * f + 32 * k
    east = pltpu.roll(from_east, (-at) % LANES, 1)
    west = pltpu.roll(from_west, (LANES - HALO - at) % LANES, 1)
    tile = jnp.where(lane1 < HALO, east, jnp.where(lane1 >= LANES - HALO, west, 0.0))
    if f == 3:
        extra = pltpu.roll(from_west, (LANES - HALO - 1 - 4 * 6 - 32 * k) % LANES, 1)
        tile = jnp.where(lane1 == LANES - HALO - 1, extra, tile)
    if f == 4:
        extra = pltpu.roll(from_east, (HALO - 4 * 6 - 1 - 32 * k) % LANES, 1)
        tile = jnp.where(lane1 == HALO, extra, tile)
    return tile


def force_with_sides(partial, mask, sides, k):
    own_west, own_east, from_west, from_east = sides
    lane1 = lane_of(own_west.shape)
    first, last = 4 * 6 + 32 * k, 4 * 6 + 3 + 32 * k
    outer = outer_tile(from_west, from_east, 0, k)
    tail = pltpu.roll(own_east, (-last) % LANES, 1)
    head = pltpu.roll(own_west, (LANES - 1 - first) % LANES, 1)
    change = jnp.where(lane1 == 0, -tail, jnp.where(lane1 == LANES - 1, head, 0.0))
    outer = outer + 0.5 * mask[:, -LANES:] * change
    begin = partial[:, :LANES] - jnp.where(
        lane1 == 0, 0.5 * mask[:, :LANES] * pltpu.roll(from_west, (-last) % LANES, 1), 0.0
    )
    middle = partial[:, LANES:-LANES]
    end = partial[:, -LANES:] + jnp.where(
        lane1 == LANES - 1,
        0.5 * mask[:, -2 * LANES : -LANES] * pltpu.roll(from_east, (LANES - 1 - first) % LANES, 1),
        0.0,
    )
    return jnp.concatenate([begin, middle, end, outer], axis=1)


def mask_row(ocean, block_row, sub, tiles):
    lane1 = lane_of((1, LANES))
    parts = [jnp.full((1, LANES), ocean_at(ocean, block_row, sub * tiles + t), F32) for t in range(tiles)]
    east = ocean_at(ocean, block_row, (sub + 1) * tiles)
    west = ocean_at(ocean, block_row, sub * tiles - 1)
    parts.append(jnp.where(lane1 < LANES // 2, east, west))
    return jnp.concatenate(parts, axis=1)


def edge_kernel(ids, ocean, edges, send_a, send_b, recv_a, recv_b, rows_a, rows_b, *, row_count):
    col_count = edges.shape[1]
    tiles = col_count // LANES
    block_rows = row_count // BLOCK
    blk, sub = ids[0], ids[1]
    even_sub, even_blk = (sub % 2) == 0, (blk % 2) == 0
    shape = (ROWS, col_count + LANES)
    row8, lane8 = row_of(shape), lane_of(shape)
    crosses_west = (lane8 == 0) | (lane8 == col_count)
    crosses_east = (lane8 == col_count - 1) | (lane8 == col_count + LANES - 1)
    strips = row_count // (4 * ROWS)
    results = []
    for side, top in enumerate((True, False)):
        k = 0 if top else 3
        packed = pl.ds(0 if top else (strips - 1) * ROWS, ROWS)
        rows = [edges[pl.ds((side * 7 + f) * ROWS, ROWS)] for f in range(7)]
        sides = side_tiles(send_a, send_b, recv_a, recv_b, even_sub, packed)
        block_row = blk * block_rows + (0 if top else block_rows - 1)
        mask = jnp.broadcast_to(mask_row(ocean, block_row, sub, tiles), shape)
        fields = [force_with_sides(rows[0], mask, sides, k)]
        for f in range(1, 6):
            fields.append(jnp.concatenate([rows[f], outer_tile(sides[2], sides[3], f, k)], axis=1))
        flux = jnp.concatenate([rows[6], outer_tile(sides[2], sides[3], 7, k)], axis=1)
        if top:
            fields[1] = jnp.where(row8 == 3, pltpu.roll(flux, 3, 0), fields[1])
            half = lambda v: v
        else:
            extra = jnp.where(crosses_west, left(fields[2]) + left(down(fields[3])), 0.0)
            extra = extra + jnp.where(crosses_east, right(down(fields[4])), 0.0)
            fields[5] = fields[5] + jnp.where(row8 == 4, extra, 0.0)
            fields[2] = jnp.where(row8 == 4, pltpu.roll(flux, 5, 0), fields[2])
            half = lambda v: pltpu.roll(v, 4, 0)
        pieces = []
        for pair in range(3):
            one, two = half(fields[2 * pair]), half(fields[2 * pair + 1])
            pieces.append(jnp.where(row8 < 4, one, pltpu.roll(two, 4, 0)))
        results.append(pieces)
    for pair in range(3):
        rows = slice(pair * ROWS, (pair + 1) * ROWS)
        rows_a[rows] = jnp.where(even_blk, results[1][pair], results[0][pair])
        rows_b[rows] = jnp.where(even_blk, results[0][pair], results[1][pair])


def prepare_kernel(ax, ay, axy, axm, bly, nx, nxy, nxm, lxy, rxm):
    row_count, wide = ax.shape[0] - ROWS, ax.shape[1]
    cols = pl.ds(0, wide - LANES)
    lane8 = lane_of((ROWS, wide - LANES))
    end = lane8 == wide - LANES - 1

    def body(g, before):
        rows = pl.ds(pl.multiple_of(g * ROWS, ROWS), ROWS)
        here_xy, here_xm = axy[rows, cols], axm[rows, cols]
        bly[rows, cols] = jnp.where(lane8 == 0, 0.0, left(ay[rows, cols]))
        lxy[rows, cols] = jnp.where(lane8 == 0, 0.0, left(here_xy))
        rxm[rows, cols] = jnp.where(end, 0.0, right(here_xm))
        rolled = tuple(down(v) for v in (ax[rows, cols], here_xy, here_xm))
        for ring, a, b in zip((nx, nxy, nxm), before, rolled):
            ring[rows, cols] = shifted_rows(a, b)
        return rolled

    zero = jnp.zeros(lane8.shape, F32)
    lax.fori_loop(0, row_count // ROWS, body, (zero, zero, zero), unroll=4)


def widen_kernel(
    ids, ocean, fp, send_a, send_b, recv_a, recv_b,
    ax_in, ay_in, bly_in, nx_in, nxy_in, nxm_in, lxy_in, rxm_in, inv_in, c0_in, center_in,
    outer_center, ax, ay, bly, nx, nxy, nxm, lxy, rxm, inv, c0, center,
):
    row_count, col_count = fp.shape
    tiles = col_count // LANES
    block_rows = row_count // BLOCK
    groups = row_count // ROWS
    blk, sub = ids[0], ids[1]
    even_sub = (sub % 2) == 0
    lane1 = lane_of((ROWS, LANES))
    first, last, outer = pl.ds(0, LANES), pl.ds(col_count - LANES, LANES), pl.ds(col_count, LANES)
    west_edge, east_edge = lane1 == 0, lane1 == LANES - 1

    def at(g):
        return pl.ds(pl.multiple_of(g * ROWS, ROWS), ROWS)

    def widen(p, before):
        sides = side_tiles(send_a, send_b, recv_a, recv_b, even_sub, at(p))
        own_west, own_east, from_west, from_east = sides
        for k in range(4):
            g = 4 * p + k
            rows = at(g)
            new_f, new_x, new_y, new_xy, new_xm, new_c = [outer_tile(from_west, from_east, f, k) for f in range(6)]
            end_y = pltpu.roll(own_east, (-(4 * 2 + 3 + 32 * k)) % LANES, 1)
            end_xy = pltpu.roll(own_east, (-(4 * 3 + 3 + 32 * k)) % LANES, 1)
            begin_xm = pltpu.roll(own_west, (LANES - 1 - 4 * 4 - 32 * k) % LANES, 1)
            left_y, left_xy, right_xm = left(new_y), left(new_xy), right(new_xm)
            outer_y = jnp.where(west_edge, end_y, left_y)
            outer_xy = jnp.where(west_edge, end_xy, left_xy)
            outer_xm = jnp.where(east_edge, begin_xm, right_xm)
            rolled = [down(v) for v in (new_x, new_xy, new_xm, outer_xy, outer_xm, left_xy, right_xm)]
            up_x, up_xy, up_xm, up_outer_xy, up_outer_xm, up_left, up_right = [
                shifted_rows(a, b) for a, b in zip(before, rolled)
            ]
            before = rolled
            ax[rows, outer] = new_x
            ay[rows, outer] = new_y
            bly[rows, outer] = outer_y
            lxy[rows, outer] = outer_xy
            rxm[rows, outer] = outer_xm
            nx[rows, outer] = up_x
            nxy[rows, outer] = up_xy
            nxm[rows, outer] = up_xm
            bly[rows, first] = jnp.where(west_edge, left_y, bly[rows, first])
            lxy[rows, first] = jnp.where(west_edge, left_xy, lxy[rows, first])
            rxm[rows, last] = jnp.where(east_edge, right_xm, rxm[rows, last])
            center_first = center[rows, first] + jnp.where(west_edge, left_y + up_left, 0.0)
            center_last = center[rows, last] + jnp.where(east_edge, up_right, 0.0)
            center_outer = new_c + jnp.where(west_edge, outer_y + up_outer_xy, 0.0)
            center_outer = center_outer + jnp.where(east_edge, up_outer_xm, 0.0)
            center[rows, first] = center_first
            center[rows, last] = center_last
            outer_center[rows] = center_outer
            block_row = blk * block_rows + g * ROWS // BLOCK
            mask_first = ocean_at(ocean, block_row, sub * tiles)
            mask_last = ocean_at(ocean, block_row, (sub + 1) * tiles - 1)
            mask_outer = jnp.where(
                lane1 < LANES // 2,
                ocean_at(ocean, block_row, (sub + 1) * tiles),
                ocean_at(ocean, block_row, sub * tiles - 1),
            )
            near, far = 4 * 6 + 32 * k, 4 * 6 + 3 + 32 * k
            tail = pltpu.roll(own_east, (-far) % LANES, 1)
            begin = pltpu.roll(own_west, (LANES - 1 - near) % LANES, 1)
            from_w = pltpu.roll(from_west, (-far) % LANES, 1)
            from_e = pltpu.roll(from_east, (LANES - 1 - near) % LANES, 1)
            force_first = fp[rows, first] - jnp.where(west_edge, (0.5 * mask_first) * from_w, 0.0)
            force_last = fp[rows, last] + jnp.where(east_edge, (0.5 * mask_last) * from_e, 0.0)
            change = jnp.where(west_edge, -tail, jnp.where(east_edge, begin, 0.0))
            force_outer = new_f + 0.5 * mask_outer * change
            inverse_first = mask_first * (1.0 / center_first)
            inverse_last = mask_last * (1.0 / center_last)
            inverse_outer = jnp.where(mask_outer > 0.0, 1.0 / jnp.where(center_outer > 0.0, center_outer, 1.0), 0.0)
            inv[rows, first] = inverse_first
            inv[rows, last] = inverse_last
            inv[rows, outer] = inverse_outer
            c0[rows, first] = force_first * inverse_first
            c0[rows, last] = force_last * inverse_last
            c0[rows, outer] = force_outer * inverse_outer
        return tuple(before)

    zero = jnp.zeros((ROWS, LANES), F32)
    lax.fori_loop(0, groups // 4, widen, (zero,) * 7)


def basis_kernel(
    ids, ocean, outer_center, edges, send_a, send_b, recv_a, recv_b, rows_a, rows_b,
    ax_in, ay_in, bly_in, nx_in, nxy_in, nxm_in, lxy_in, rxm_in, inv_in, c0_in, center_in,
    c1, c2, c3, c4, gram_ref, ax, ay, bly, nx, nxy, nxm, lxy, rxm, inv, c0, center,
):
    row_count, col_count = center.shape
    tiles = col_count // LANES
    wide = col_count + LANES
    block_rows = row_count // BLOCK
    groups = row_count // ROWS
    blk, sub = ids[0], ids[1]
    even_sub, even_blk = (sub % 2) == 0, (blk % 2) == 0
    row8, lane8 = row_of((ROWS, wide)), lane_of((ROWS, wide))
    row1, lane1 = row_of((ROWS, LANES)), lane_of((ROWS, LANES))
    first, last, outer = pl.ds(0, LANES), pl.ds(col_count - LANES, LANES), pl.ds(col_count, LANES)
    west_edge, east_edge = lane1 == 0, lane1 == LANES - 1

    def at(g):
        return pl.ds(pl.multiple_of(g * ROWS, ROWS), ROWS)

    pieces = []
    for pair in range(3):
        rows = slice(pair * ROWS, (pair + 1) * ROWS)
        below = jnp.where(even_blk, rows_a[rows], rows_b[rows])
        above = jnp.where(even_blk, rows_b[rows], rows_a[rows])
        pieces.append(jnp.where(row8 < 4, below, pltpu.roll(above, 4, 0)))
        pieces.append(jnp.where(row8 < 4, pltpu.roll(below, 4, 0), above))
    out_f, out_x, out_y, out_xy, out_xm, out_c = pieces
    flux_below, flux_above = out_x[3:4], out_y[4:5]

    def mask_of(block_row):
        return jnp.broadcast_to(mask_row(ocean, block_row, sub, tiles), (ROWS, wide))

    def edge_group(side, k):
        strip = 0 if side == 0 else groups // 4 - 1
        sides = side_tiles(send_a, send_b, recv_a, recv_b, even_sub, at(strip))
        get = lambda f: edges[pl.ds((side * 7 + f) * ROWS, ROWS)]
        full = [
            jnp.concatenate([get(e), outer_tile(sides[2], sides[3], f, k)], axis=1)
            for e, f in ((1, 1), (3, 3), (4, 4), (6, 7))
        ]
        mask = mask_of(blk * block_rows + (0 if side == 0 else block_rows - 1))
        return full, mask, force_with_sides(get(0), mask, sides, k)

    (_, _, _, flux_first), mask_first, force_first = edge_group(0, 0)
    (x_last, xy_last, xm_last, flux_last), mask_last, force_last = edge_group(1, 3)
    mask_below, mask_above = mask_of((blk + 1) * block_rows), mask_of(blk * block_rows - 1)

    def inverse_of(mask, total):
        return jnp.where(mask > 0.0, 1.0 / jnp.where(total > 0.0, total, 1.0), 0.0)

    head = row8 == 0
    own_first = pl.ds(0, ROWS)
    up = []
    for ring, out in ((nx, out_x), (nxy, out_xy), (nxm, out_xm)):
        moved = jnp.where(head, down(out), ring[own_first])
        ring[own_first] = moved
        up.append(moved)
    total = jnp.concatenate([center[own_first], outer_center[own_first]], axis=1)
    total = total + jnp.where(head, up[0] + left(up[1]) + right(up[2]), 0.0)
    center[own_first] = total[:, :col_count]
    inverse = inverse_of(mask_first, total)
    inv[own_first] = inverse
    c0[own_first] = inverse * (force_first - jnp.where(head, 0.5 * mask_first * flux_above, 0.0))
    own_last = pl.ds(row_count - ROWS, ROWS)
    c0[own_last] = inv[own_last] * (
        force_last + jnp.where(row8 == ROWS - 1, 0.5 * mask_last * flux_below, 0.0)
    )
    ring_rows = pl.ds(row_count, ROWS)
    up = [
        jnp.where(head, down(before), down(out))
        for before, out in ((x_last, out_x), (xy_last, out_xy), (xm_last, out_xm))
    ]
    left_y = left(out_y)
    for ring, value in (
        (ax, out_x), (ay, out_y), (bly, left_y), (nx, up[0]), (nxy, up[1]), (nxm, up[2]),
        (lxy, left(out_xy)), (rxm, right(out_xm)),
    ):
        ring[ring_rows] = value
    crosses_west = (row8 != 4) & ((lane8 == 0) | (lane8 == col_count))
    crosses_east = (row8 != 4) & ((lane8 == col_count - 1) | (lane8 == wide - 1))
    total = out_c + jnp.where(head, up[0], 0.0)
    total = total + jnp.where(crosses_west, left_y, 0.0)
    total = total + jnp.where(head | crosses_west, left(up[1]), 0.0)
    total = total + jnp.where(head | crosses_east, right(up[2]), 0.0)
    inverse = inverse_of(jnp.where(row8 < 4, mask_below, mask_above), total)
    out_f = out_f - jnp.where(head, 0.5 * mask_below * flux_last[ROWS - 1 : ROWS], 0.0)
    out_f = out_f + jnp.where(row8 == ROWS - 1, 0.5 * mask_above * flux_first[0:1], 0.0)
    inv[ring_rows] = inverse
    c0[ring_rows] = inverse * out_f

    def sides_of(source, g, width):
        value = source[at(g)]
        return left(value)[:, :width], right(value)[:, :width]

    def terms(source, g, width, turned):
        rows, cols = at(g), pl.ds(0, width)
        west, east = turned
        here = source[rows, cols]
        same = ay[rows, cols] * east + bly[rows, cols] * west
        after = ax[rows, cols] * here + lxy[rows, cols] * west + rxm[rows, cols] * east
        before = nx[rows, cols] * here + nxy[rows, cols] * east + nxm[rows, cols] * west
        return same, down(after), pltpu.roll(before, ROWS - 1, 0)

    def sweep(source, count, width, finish):
        ring_turned, turned, following = [sides_of(source, g, width) for g in (groups, 0, 1)]
        _, ring_after, _ = terms(source, groups, width, ring_turned)
        same, after, own_first = terms(source, 0, width, turned)
        tail = row_of((ROWS, width)) == ROWS - 1

        def body(g, carry):
            partial, own, previous, turned = carry
            following = sides_of(source, jnp.minimum(g + 1, groups), width)
            same, after, later = terms(source, g, width, turned)
            finish(g - 1, partial + jnp.where(tail, later, own))
            return same + shifted_rows(previous, after), later, after, following

        carry = (same + shifted_rows(ring_after, after), own_first, after, following)
        partial, own, _, turned = lax.fori_loop(1, count, body, carry, unroll=UNROLL)
        if count > groups:
            later = own_first
        else:
            later = terms(source, groups, width, turned)[2]
        finish(count - 1, partial + jnp.where(tail, later, own))

    def step(source, target, subtract):
        def finish(g, total):
            rows = at(g)
            moved = inv[rows] * total
            target[rows] = source[rows] - moved if subtract else moved

        sweep(source, groups + 1, wide, finish)

    step(c0, c1, True)
    step(c1, c2, False)
    step(c2, c3, False)

    cols = pl.ds(0, col_count)

    def last_finish(g, total):
        c4[at(g)] = inv[at(g), cols] * total

    sweep(c3, groups, col_count, last_finish)

    def add_products(g, sums):
        rows = at(g)
        basis = [ref[rows, cols] for ref in (c0, c1, c2, c3)] + [c4[rows]]
        weight = center[rows]
        weighted = [weight * b for b in basis]
        new = []
        for (i, j), total in zip(PAIRS, sums):
            product = basis[i] * weighted[j]
            part = product[:, :LANES]
            for t in range(1, tiles):
                part = part + product[:, t * LANES : (t + 1) * LANES]
            new.append(total + part)
        return tuple(new)

    zero = jnp.zeros((ROWS, LANES), F32)
    sums = lax.fori_loop(0, groups, add_products, tuple(zero for _ in PAIRS), unroll=2)

    count = len(PAIRS)
    high = jnp.zeros((2 * ROWS, LANES), F32)
    low = high
    place = row_of((2 * ROWS, LANES))
    for index, total in enumerate(sums):
        error = jnp.zeros_like(total)
        for shift in (4, 2, 1):
            total, rounding = two_sum(total, pltpu.roll(total, shift, 0))
            error = error + pltpu.roll(error, shift, 0) + rounding
        high = jnp.where(place == index, total[0:1], high)
        low = jnp.where(place == index, error[0:1], low)
    for shift in (64, 32, 16, 8, 4, 2, 1):
        high, rounding = two_sum(high, pltpu.roll(high, shift, 1))
        low = low + pltpu.roll(low, shift, 1) + rounding
    lane2 = lane_of((2 * ROWS, LANES))
    packed = jnp.where(lane2 == place, high, jnp.where(lane2 == place + LANES // 2, low, 0.0))
    gram_ref[...] = jnp.broadcast_to(jnp.sum(packed, axis=0, keepdims=True), gram_ref.shape)


def finish_kernel(gram_ref, c0, c1, c2, c3, c4, center_ref, height_ref, residual_ref):
    lane1 = lane_of((1, LANES))
    high = gram_ref[...]
    low = jnp.zeros_like(high)
    while high.shape[0] > 1:
        half = high.shape[0] // 2
        high, rounding = two_sum(high[:half], high[half:])
        low = low[:half] + low[half:] + rounding
    entries = high + (low + pltpu.roll(high, LANES // 2, 1))
    size = ITERS + 1
    gram = {}
    for index, (i, j) in enumerate(PAIRS):
        entry = jnp.sum(jnp.where(lane1 == index, entries, 0.0), axis=1, keepdims=True)
        gram[i, j] = entry
        gram[j, i] = entry
    zero = jnp.zeros((1, 1), F32)
    one = jnp.ones((1, 1), F32)

    def image(coefs):
        result = [zero, coefs[0] + coefs[1]]
        for j in range(2, size):
            own = coefs[j] if j < size - 1 else zero
            result.append(own - coefs[j - 1])
        return result

    def form(one_side, products):
        total = zero
        for a, b in zip(one_side, products):
            total = total + a * b
        return total

    scaled = [one] + [zero] * (size - 1)
    search = [zero] * size
    height = [zero] * size
    rho_old, sigma = one, zero
    for iteration in range(ITERS):
        limit = iteration + 1
        products = []
        for j in range(size):
            total = zero
            for i in range(limit):
                total = total + scaled[i] * gram[i, j]
            products.append(total)
        rho = form(scaled[:limit], products)
        curvature = form(image(scaled)[: limit + 1], products)
        beta = rho / rho_old
        sigma = curvature - beta * beta * sigma
        alpha = rho / sigma
        rho_old = rho
        search = [s + beta * q for s, q in zip(scaled, search)]
        height = [h + alpha * q for h, q in zip(height, search)]
        scaled = [s - alpha * q for s, q in zip(scaled, image(search))]

    def combine(g, _):
        rows = pl.ds(pl.multiple_of(g * ROWS, ROWS), ROWS)
        cols = pl.ds(0, center_ref.shape[1])
        basis = [ref[rows, cols] for ref in (c0, c1, c2, c3, c4)]
        total = height[0] * basis[0]
        for j in range(1, size - 1):
            total = total + height[j] * basis[j]
        height_ref[rows] = total
        total = scaled[0] * basis[0]
        for j in range(1, size):
            total = total + scaled[j] * basis[j]
        residual_ref[rows] = center_ref[rows] * total
        return 0

    lax.fori_loop(0, center_ref.shape[0] // ROWS, combine, 0, unroll=2)


def swap(value, axis, parity):
    peers = lax.axis_size(axis)
    pairs = []
    for i in range(parity, peers - 1, 2):
        pairs += [(i, i + 1), (i + 1, i)]
    return lax.ppermute(value, axis, pairs)


def body(u_flow, v_flow, thickness, depth_levels, block_ocean, coef_x, coef_y, coef_xy, coef_xm, extra_diagonal):
    levels, row_count, col_count = u_flow.shape
    wide = col_count + LANES
    shape = lambda *dims: pltpu.VMEM(dims, F32)
    final = jax.ShapeDtypeStruct((row_count, col_count), F32)
    far = lambda array: pltpu.with_memory_space_constraint(array, pltpu.HBM)
    plane = shape(row_count, col_count)
    ring = shape(row_count + ROWS, wide)
    strip = shape(row_count // 4, LANES)
    ids = jnp.stack([lax.axis_index("blk"), lax.axis_index("sub")]).astype(jnp.int32)
    flow = pltpu.VMEM((levels, row_count, col_count), F32)
    field = pltpu.VMEM((row_count, col_count), F32)
    fp, cp, edges, send_a, send_b, *rings = pl.pallas_call(
        flux_kernel,
        out_shape=(plane, plane, shape(14 * ROWS, col_count), strip, strip) + (ring,) * 6,
        in_specs=[SMEM, SMEM, SMEM] + [HBM] * 8,
        out_specs=(VMEM,) * 11,
        scratch_shapes=[flow, flow, pltpu.VMEM((row_count, col_count), jnp.int32)]
        + [field] * 3
        + [pltpu.VMEM((row_count // BLOCK * ROWS, col_count), F32)]
        + [pltpu.SemaphoreType.DMA((2, row_count // CHUNK)), pltpu.SemaphoreType.DMA((6,))],
        compiler_params=pltpu.CompilerParams(vmem_limit_bytes=FLUX_LIMIT),
        name="flux",
    )(
        ids, thickness, block_ocean,
        *[far(a) for a in (u_flow, v_flow, depth_levels, coef_x, coef_y, coef_xy, coef_xm, extra_diagonal)],
    )
    recv_a, recv_b = swap(send_a, "sub", 0), swap(send_b, "sub", 1)
    ax, ay, axy, axm, inv, c0 = rings
    moved = pl.pallas_call(
        prepare_kernel,
        out_shape=(ring,) * 6,
        in_specs=[VMEM] * 4,
        out_specs=(VMEM,) * 6,
        compiler_params=pltpu.CompilerParams(vmem_limit_bytes=8 << 20),
        cost_estimate=pl.CostEstimate(flops=10 << 20, bytes_accessed=4 << 20, transcendentals=0),
        name="prepare",
    )(ax, ay, axy, axm)
    edge = shape(3 * ROWS, wide)
    edge_a, edge_b = pl.pallas_call(
        functools.partial(edge_kernel, row_count=row_count),
        out_shape=(edge, edge),
        in_specs=[SMEM, SMEM] + [VMEM] * 5,
        out_specs=(VMEM,) * 2,
        compiler_params=pltpu.CompilerParams(vmem_limit_bytes=8 << 20),
        name="edge",
    )(ids, block_ocean, edges, send_a, send_b, recv_a, recv_b)
    rows_a, rows_b = swap(edge_a, "blk", 0), swap(edge_b, "blk", 1)
    outer_center, *rings = pl.pallas_call(
        widen_kernel,
        out_shape=(shape(row_count, LANES),) + (ring,) * 10 + (plane,),
        in_specs=[SMEM, SMEM] + [VMEM] * 16,
        out_specs=(VMEM,) * 12,
        input_output_aliases={7 + i: 1 + i for i in range(11)},
        compiler_params=pltpu.CompilerParams(vmem_limit_bytes=8 << 20),
        cost_estimate=pl.CostEstimate(flops=10 << 20, bytes_accessed=4 << 20, transcendentals=0),
        name="widen",
    )(ids, block_ocean, fp, send_a, send_b, recv_a, recv_b, ax, ay, *moved, inv, c0, cp)
    devices = lax.axis_size("blk") * lax.axis_size("sub")
    c1, c2, c3, c4, gram, *rest = pl.pallas_call(
        basis_kernel,
        out_shape=(ring, ring, ring, plane, shape(devices, LANES)) + (ring,) * 10 + (plane,),
        in_specs=[SMEM, SMEM] + [VMEM] * 19,
        out_specs=(VMEM,) * 16,
        input_output_aliases={10 + i: 5 + i for i in range(11)},
        compiler_params=pltpu.CompilerParams(vmem_limit_bytes=8 << 20),
        name="basis",
    )(ids, block_ocean, outer_center, edges, send_a, send_b, recv_a, recv_b, rows_a, rows_b, *rings)
    c0, center = rest[-2], rest[-1]
    gram = lax.all_to_all(gram, ("blk", "sub"), 0, 0, tiled=True)
    return pl.pallas_call(
        finish_kernel,
        out_shape=(final, final),
        in_specs=[VMEM] * 7,
        out_specs=(VMEM,) * 2,
        compiler_params=pltpu.CompilerParams(vmem_limit_bytes=8 << 20),
        name="finish",
    )(gram, c0, c1, c2, c3, c4, center)


def solution(mesh):
    placed = (
        P(None, "blk", "sub"),
        P(None, "blk", "sub"),
        P(),
        P("blk", "sub"),
        P(),
        P("blk", "sub"),
        P("blk", "sub"),
        P("blk", "sub"),
        P("blk", "sub"),
        P("blk", "sub"),
    )
    return jax.shard_map(
        body,
        mesh=mesh,
        in_specs=placed,
        out_specs=(P("blk", "sub"), P("blk", "sub")),
        check_vma=False,
    )
```

time: 73.5 us -> 47.9 us (0.65)
  Pallas kernels: 34.5 us -> 22.2 us
  local copies, waits for them, and re-layouts: 11 us -> 1.35 us
  blocking collectives: 20.4 us -> 17.6 us
    pallas_call x4 -> x6, Pallas kernels: 34.5 us -> 22.2 us  [the longest x1 9.42 us: body(): pl.pallas_call(flux_kernel, out_shape=(plane, plane, shape(14 * ROWS, col...]
    unnamed x18 -> x4, local copies, waits for them, and re-layouts: 11 us -> 1.35 us
    all_to_all x1, blocking collectives: 20.4 us -> 17.6 us  [body(): gram = lax.all_to_all(gram, ('blk', 'sub'), 0, 0, tiled=True)]
  transfers between devices with their start and end apart: 4 -> 4, of which waited for: 2 -> 1; matrix products, arithmetic and copies ran while one was open for 0% -> 0% of each run, Pallas kernels for 0% -> 7%
where the time goes in v2:
time: 47.9 us; the launch traced here: 47.6 us
  Pallas kernels  22.2 us (46%)
  blocking collectives  17.6 us (37%)
  starting transfers between devices  4.5 us (9%)
  local copies, waits for them, and re-layouts  1.35 us (3%)
  waiting for transfers between devices  1.24 us (3%)
  between operations  0.71 us (1%)
    all_to_all x1, blocking collectives, body(): gram = lax.all_to_all(gram, ('blk', 'sub'), 0, 0, tiled=True)  17.6 us
    pallas_call x1, Pallas kernels, body(): pl.pallas_call(flux_kernel, out_shape=(plane, plane, shape(14 * ROWS, col...  9.42 us
    pallas_call x1, Pallas kernels, body(): pl.pallas_call(basis_kernel, out_shape=(ring, ring, ring, plane, shape(de...  6.72 us
    ppermute x4, starting transfers between devices, swap(): return lax.ppermute(value, axis, pairs)  4.5 us
    pallas_call x1, Pallas kernels, body(): pl.pallas_call(widen_kernel, out_shape=(shape(row_count, LANES),) + (ring...  2.54 us
    pallas_call x1, Pallas kernels, body(): pl.pallas_call(finish_kernel, out_shape=(final, final), in_specs=[VMEM] *...  1.66 us
    unnamed x4, local copies, waits for them, and re-layouts  1.35 us
    ppermute x4, waiting for transfers between devices, swap(): return lax.ppermute(value, axis, pairs)  1.24 us
  transfers between devices with their start and end apart: 4, of which 1 were waited for; matrix products, arithmetic and copies ran while one was open for 0% of the time, Pallas kernels for 7%

profile of v2, /device:TPU:0, one launch (start us, length us, event | category | flops | bytes accessed | tf_op | source)
XLA Modules:
  0.0 47.6 jit_solution(14022040479600411946)
XLA Ops:
  0.6 0.1 pad_add_fusion.ids
  0.7 0.0 copy-start
  0.7 0.7 %copy-done = s32[16,16]{1,0:T(8,128)S(1)} copy-done((s32[16,16]{1,0:T(8,128)S(1)}, s32[16,16]{1,0:T(8,128)}, u32[]{:S(2)}) %copy-start) | copy-done | bytes 1048
  1.4 0.0 copy-start.1
  1.4 0.7 %copy-done.1 = f32[16]{0:T(128)S(1)} copy-done((f32[16]{0:T(128)S(1)}, f32[16]{0:T(128)}, u32[]{:S(2)}) %copy-start.1) | copy-done | bytes 88
  2.1 9.4 %flux.1 = (f32[256,512]{1,0:T(8,128)S(1)}, f32[256,512]{1,0:T(8,128)S(1)}, f32[112,512]{1,0:T(8,128)S(1)}, f32[64,128]{1,0:T(8,128)S(1)}, f32[64,128]{1,0:T(8,12...) custom-call(s32[2]{0:T(128)S(1)} %pad_add_fusion.ids, ...), custom_call_target="tpu_custom_call" | custom-call | tf_op jit(solution)/shard_map/flux/pallas_call | solution.py:707
  11.5 3.1 %collective-permute-start = (f32[64,128]{1,0:T(8,128)S(1)}, f32[64,128]{1,0:T(8,128)S(1)}, u32[]{:S(2)}, u32[]{:S(2)}) collective-permute-start(f32[64,128]{1,0:T(8,128)S(1)} %get-tuple-element.41.send_a), channel_id=1, source_target_pairs={{0,1},{1,0},{2,3},{3,2},{4,5},{5,4},{6,7},{7,6},{8,9},{9,8},{10,11... | collective-permute-start | bytes 98312 | tf_op jit(solution)/shard_map/ppermute | solution.py:692
  14.6 0.7 %collective-permute-start.1 = (f32[64,128]{1,0:T(8,128)S(1)}, f32[64,128]{1,0:T(8,128)S(1)}, u32[]{:S(2)}, u32[]{:S(2)}) collective-permute-start(f32[64,128]{1,0:T(8,128)S(1)} %get-tuple-element.42.send_b), channel_id=1, source_target_pairs={{1,2},{2,1},{5,6},{6,5},{9,10},{10,9},{13,14},{14,13},{17,18},{18,... | collective-permute-start | bytes 98312 | tf_op jit(solution)/shard_map/ppermute | solution.py:692
  15.3 1.2 %collective-permute-done.recv_a = f32[64,128]{1,0:T(8,128)S(1)} collective-permute-done((f32[64,128]{1,0:T(8,128)S(1)}, f32[64,128]{1,0:T(8,128)S(1)}, u32[]{:S(2)}, u32[]{:S(2)}) %collective-permute-start) | collective-permute-done | bytes 32800 | tf_op jit(solution)/shard_map/ppermute | solution.py:692
  16.5 0.0 collective-permute-done.1.recv_b
  16.5 0.8 %edge.1 = (f32[24,640]{1,0:T(8,128)S(1)}, f32[24,640]{1,0:T(8,128)S(1)}) custom-call(s32[2]{0:T(128)S(1)} %pad_add_fusion.ids, s32[16,16]{1,0:T(8,128)S(1)} %copy-done, f32[112,512]{1,0:T(8,128)S(1)} %get-tuple-element.57.edges, f32[64,128]{1,0:T(8,128)S(1)} %get-tuple-element.41.send_a, f32[64,128]{1,0:T(8,128)S(1)} %get-tuple-element.42.send_b, ...), custom_call_target="tpu_custom_call" | custom-call | tf_op jit(solution)/shard_map/edge/pallas_call | solution.py:734
  17.3 0.1 collective-permute-start.2
  17.4 0.7 %collective-permute-start.3 = (f32[24,640]{1,0:T(8,128)S(1)}, f32[24,640]{1,0:T(8,128)S(1)}, u32[]{:S(2)}, u32[]{:S(2)}) collective-permute-start(f32[24,640]{1,0:T(8,128)S(1)} %get-tuple-element.59), channel_id=1, source_target_pairs={{4,8},{8,4},{12,16},{16,12},{20,24},{24,20},{5,9},{9,5},{13,17},{1... | collective-permute-start | bytes 184328 | tf_op jit(solution)/shard_map/ppermute | solution.py:692
  18.1 1.0 %prepare.1 = (f32[264,640]{1,0:T(8,128)S(1)}, f32[264,640]{1,0:T(8,128)S(1)}, f32[264,640]{1,0:T(8,128)S(1)}, f32[264,640]{1,0:T(8,128)S(1)}, f32[264,640]{1,0:T(8,128)S(1)}, /*index=5*/f32[264,640]{1,0:T(8,128)S(1)}) custom-call(f32[264,640]{1,0:T(8,128)S(1)} %get-tuple-element.43.ax.ax_in, f32[264,640]{1,0:T(8,128)S(1)} %get-tuple-element.44.ay.ay_in, ...), custom_call_target="tpu_custom_call" | custom-call | flops 10485760 | bytes 4194304 | tf_op jit(solution)/shard_map/prepare/pallas_call | solution.py:724
  19.1 2.5 %widen.1 = (f32[256,128]{1,0:T(8,128)S(1)}, f32[264,640]{1,0:T(8,128)S(1)}, f32[264,640]{1,0:T(8,128)S(1)}, f32[264,640]{1,0:T(8,128)S(1)}, f32[264,640]{1,0:T(8...) custom-call(s32[2]{0:T(128)S(1)} %pad_add_fusion.ids, ...), custom_call_target="tpu_custom_call", output_to_operand_aliasing={{1}: (7, {}), {2}: (8, {}), {3}: (9, {}), {4}: (10, {}), {5... | custom-call | flops 10485760 | bytes 4194304 | tf_op jit(solution)/shard_map/widen/pallas_call | solution.py:743
  21.6 0.0 collective-permute-done.2.rows_a
  21.6 0.0 collective-permute-done.3.rows_b
  21.7 6.7 %basis.1 = (f32[264,640]{1,0:T(8,128)S(1)}, f32[264,640]{1,0:T(8,128)S(1)}, f32[264,640]{1,0:T(8,128)S(1)}, f32[256,512]{1,0:T(8,128)S(1)}, f32[32,128]{1,0:T(8,...) custom-call(s32[2]{0:T(128)S(1)} %pad_add_fusion.ids, ...), custom_call_target="tpu_custom_call", output_to_operand_aliasing={{5}: (10, {}), {6}: (11, {}), {7}: (12, {}), {8}: (13, {}),... | custom-call | tf_op jit(solution)/shard_map/basis/pallas_call | solution.py:754
  28.4 17.6 %all_to_all.11 = f32[32,1,128]{2,1,0:T(1,128)S(1)} all-to-all(f32[32,1,128]{2,1,0:T(1,128)S(1)} %bitcast.7), channel_id=1, replica_groups=mesh['blk'=8,'sub'=4] {'blk','sub'}, dimensions={0} | all-to-all | bytes 32768 | tf_op jit(solution)/shard_map/all_to_all | solution.py:764
  46.0 1.7 %finish.1 = (f32[256,512]{1,0:T(8,128)}, f32[256,512]{1,0:T(8,128)}) custom-call(f32[32,128]{1,0:T(8,128)S(1)} %bitcast.6, f32[264,640]{1,0:T(8,128)S(1)} %get-tuple-element.72.c0, f32[264,640]{1,0:T(8,128)S(1)} %get-tuple-element.73.c1, f32[264,640]{1,0:T(8,128)S(1)} %get-tuple-element.74.c2, f32[264,640]{1,0:T(8,128)S(1)} %get-tuple-element.75.c3, ...), custom_call_target="tpu_custom_call" | custom-call | tf_op jit(solution)/shard_map/finish/pallas_call | solution.py:765
Async XLA Ops:
  0.7 0.7 %copy-start = (s32[16,16]{1,0:T(8,128)S(1)}, s32[16,16]{1,0:T(8,128)}, u32[]{:S(2)}) copy-start(s32[16,16]{1,0:T(8,128)} %ocean.7) | copy-start | bytes 3076
  1.4 0.7 %copy-start.1 = (f32[16]{0:T(128)S(1)}, f32[16]{0:T(128)}, u32[]{:S(2)}) copy-start(f32[16]{0:T(128)} %thick.1) | copy-start | bytes 196
  11.5 5.0 %collective-permute-start = (f32[64,128]{1,0:T(8,128)S(1)}, f32[64,128]{1,0:T(8,128)S(1)}, u32[]{:S(2)}, u32[]{:S(2)}) collective-permute-start(f32[64,128]{1,0:T(8,128)S(1)} %get-tuple-element.41.send_a), channel_id=1, source_target_pairs={{0,1},{1,0},{2,3},{3,2},{4,5},{5,4},{6,7},{7,6},{8,9},{9,8},{10,11... | collective-permute-start | bytes 98312 | tf_op jit(solution)/shard_map/ppermute | solution.py:692
  14.6 1.9 %collective-permute-start.1 = (f32[64,128]{1,0:T(8,128)S(1)}, f32[64,128]{1,0:T(8,128)S(1)}, u32[]{:S(2)}, u32[]{:S(2)}) collective-permute-start(f32[64,128]{1,0:T(8,128)S(1)} %get-tuple-element.42.send_b), channel_id=1, source_target_pairs={{1,2},{2,1},{5,6},{6,5},{9,10},{10,9},{13,14},{14,13},{17,18},{18,... | collective-permute-start | bytes 98312 | tf_op jit(solution)/shard_map/ppermute | solution.py:692
  17.3 4.3 %collective-permute-start.2 = (f32[24,640]{1,0:T(8,128)S(1)}, f32[24,640]{1,0:T(8,128)S(1)}, u32[]{:S(2)}, u32[]{:S(2)}) collective-permute-start(f32[24,640]{1,0:T(8,128)S(1)} %get-tuple-element.58), channel_id=1, source_target_pairs={{0,4},{4,0},{8,12},{12,8},{16,20},{20,16},{24,28},{28,24},{1,5},{5... | collective-permute-start | bytes 184328 | tf_op jit(solution)/shard_map/ppermute | solution.py:692
  17.4 4.2 %collective-permute-start.3 = (f32[24,640]{1,0:T(8,128)S(1)}, f32[24,640]{1,0:T(8,128)S(1)}, u32[]{:S(2)}, u32[]{:S(2)}) collective-permute-start(f32[24,640]{1,0:T(8,128)S(1)} %get-tuple-element.59), channel_id=1, source_target_pairs={{4,8},{8,4},{12,16},{16,12},{20,24},{24,20},{5,9},{9,5},{13,17},{1... | collective-permute-start | bytes 184328 | tf_op jit(solution)/shard_map/ppermute | solution.py:692

commit v3 on v2

--- a/solution.py
+++ b/solution.py
@@ -14,11 +14,10 @@
 ROWS = 8
 CHUNK = 32
 AHEAD = 3
-UNROLL = 4
+UNROLL = 8
 F32 = jnp.float32
 FLUX_LIMIT = 40 << 20
 VMEM = pl.BlockSpec(memory_space=pltpu.VMEM)
-SMEM = pl.BlockSpec(memory_space=pltpu.SMEM)
 HBM = pl.BlockSpec(memory_space=pltpu.HBM)
 PAIRS = [(i, j) for i in range(ITERS) for j in range(i, ITERS + 1)]
 
@@ -61,16 +60,16 @@
 
 
 def flux_kernel(
-    ids, thick, ocean, u_hbm, v_hbm, depth_hbm, cx_hbm, cy_hbm, cxy_hbm, cxm_hbm, ex_hbm,
-    fp_ref, cp_ref, edge_ref, pack_a, pack_b, ax, ay, axy, axm, inv, c0,
-    u_buf, v_buf, depth, ex, fu, fv, masks, sems, coef_sem,
+    thick_hbm, ocean_hbm, u_hbm, v_hbm, depth_hbm, cx_hbm, cy_hbm, cxy_hbm, cxm_hbm, ex_hbm,
+    fp_ref, cp_ref, edge_ref, pack_a, pack_b, ax, ay, axy, axm, inv, c0, masks,
+    u_buf, v_buf, depth, ex, fu, fv, thick, ocean, sems, coef_sem, small_sem,
 ):
     levels, row_count, col_count = u_buf.shape
     tiles = col_count // LANES
     chunks = row_count // CHUNK
     groups = row_count // ROWS
     steps = CHUNK // ROWS
-    blk, sub = ids[0], ids[1]
+    blk, sub = own_place()
     block_rows = row_count // BLOCK
     own = (pl.ds(0, row_count), pl.ds(0, col_count))
     coef_copies = [
@@ -90,6 +89,12 @@
             pltpu.make_async_copy(v_hbm.at[:, rows, :], v_buf.at[:, rows, :], sems.at[1, c]),
         )
 
+    small_copies = [
+        pltpu.make_async_copy(src, dst, small_sem.at[i])
+        for i, (src, dst) in enumerate([(thick_hbm, thick), (ocean_hbm, ocean)])
+    ]
+    for copy in small_copies:
+        copy.start()
     coef_copies[0].start()
     for copy in flow_copies(0):
         copy.start()
@@ -98,11 +103,13 @@
     for c in range(1, AHEAD):
         for copy in flow_copies(c):
             copy.start()
-    for b in range(block_rows):
-        for t in range(tiles):
-            masks[pl.ds(b * ROWS, ROWS), pl.ds(t * LANES, LANES)] = jnp.full(
-                (ROWS, LANES), ocean_at(ocean, blk * block_rows + b, sub * tiles + t), F32
-            )
+    for copy in small_copies:
+        copy.wait()
+    for place in range(block_rows + 2):
+        block_row = blk * block_rows + (place if place <= block_rows else -1)
+        masks[mask_group(place)] = jnp.broadcast_to(
+            mask_row(ocean, block_row, sub, tiles), (ROWS, col_count + LANES)
+        )
     coef_copies[0].wait()
 
     row8 = row_of((ROWS, col_count))
@@ -125,14 +132,11 @@
             down(v) for v in (ax[rows, cols], west_of(axy[rows, cols]), east_of(axm[rows, cols]), fu[rows])
         ]
 
-    def mask_at(g):
-        return pl.ds(pl.multiple_of(g * ROWS // BLOCK * ROWS, ROWS), ROWS)
-
     def sum_group(g):
         rows = at(g)
         for t in range(tiles):
             lanes = pl.ds(t * LANES, LANES)
-            mask = masks[mask_at(g), lanes]
+            mask = masks[mask_group(g * ROWS // BLOCK), lanes]
             deep = depth[rows, lanes]
             total_u = jnp.zeros((ROWS, LANES), F32)
             total_v = total_u
@@ -163,7 +167,7 @@
         after = jnp.where(g + 1 < groups, pltpu.roll(after, ROWS - 1, 0), 0.0)
         below = jnp.where(row8 == ROWS - 1, after, pltpu.roll(here_u, ROWS - 1, 0))
         change = 0.5 * ((below - up_u) + (east_of(here_v) - west_of(here_v)))
-        mask = masks[mask_at(g)]
+        mask = masks[mask_group(g * ROWS // BLOCK), cols]
         partial = mask * change
         inverse = mask * (1.0 / total)
         fp_ref[rows] = partial
@@ -274,6 +278,16 @@
     return jnp.concatenate([begin, middle, end, outer], axis=1)
 
 
+def own_place():
+    return lax.axis_index("blk"), lax.axis_index("sub")
+
+
+def mask_group(block):
+    if isinstance(block, int):
+        return pl.ds(block * ROWS, ROWS)
+    return pl.ds(pl.multiple_of(block * ROWS, ROWS), ROWS)
+
+
 def mask_row(ocean, block_row, sub, tiles):
     lane1 = lane_of((1, LANES))
     parts = [jnp.full((1, LANES), ocean_at(ocean, block_row, sub * tiles + t), F32) for t in range(tiles)]
@@ -283,11 +297,11 @@
     return jnp.concatenate(parts, axis=1)
 
 
-def edge_kernel(ids, ocean, edges, send_a, send_b, recv_a, recv_b, rows_a, rows_b, *, row_count):
+def edge_kernel(masks, edges, send_a, send_b, recv_a, recv_b, _, rows_a, rows_b, *, row_count):
     col_count = edges.shape[1]
     tiles = col_count // LANES
     block_rows = row_count // BLOCK
-    blk, sub = ids[0], ids[1]
+    blk, sub = own_place()
     even_sub, even_blk = (sub % 2) == 0, (blk % 2) == 0
     shape = (ROWS, col_count + LANES)
     row8, lane8 = row_of(shape), lane_of(shape)
@@ -300,8 +314,7 @@
         packed = pl.ds(0 if top else (strips - 1) * ROWS, ROWS)
         rows = [edges[pl.ds((side * 7 + f) * ROWS, ROWS)] for f in range(7)]
         sides = side_tiles(send_a, send_b, recv_a, recv_b, even_sub, packed)
-        block_row = blk * block_rows + (0 if top else block_rows - 1)
-        mask = jnp.broadcast_to(mask_row(ocean, block_row, sub, tiles), shape)
+        mask = masks[mask_group(0 if top else block_rows - 1)]
         fields = [force_with_sides(rows[0], mask, sides, k)]
         for f in range(1, 6):
             fields.append(jnp.concatenate([rows[f], outer_tile(sides[2], sides[3], f, k)], axis=1))
@@ -348,7 +361,7 @@
 
 
 def widen_kernel(
-    ids, ocean, fp, send_a, send_b, recv_a, recv_b,
+    masks, fp, send_a, send_b, recv_a, recv_b,
     ax_in, ay_in, bly_in, nx_in, nxy_in, nxm_in, lxy_in, rxm_in, inv_in, c0_in, center_in,
     outer_center, ax, ay, bly, nx, nxy, nxm, lxy, rxm, inv, c0, center,
 ):
@@ -356,7 +369,7 @@
     tiles = col_count // LANES
     block_rows = row_count // BLOCK
     groups = row_count // ROWS
-    blk, sub = ids[0], ids[1]
+    blk, sub = own_place()
     even_sub = (sub % 2) == 0
     lane1 = lane_of((ROWS, LANES))
     first, last, outer = pl.ds(0, LANES), pl.ds(col_count - LANES, LANES), pl.ds(col_count, LANES)
@@ -402,14 +415,8 @@
             center[rows, first] = center_first
             center[rows, last] = center_last
             outer_center[rows] = center_outer
-            block_row = blk * block_rows + g * ROWS // BLOCK
-            mask_first = ocean_at(ocean, block_row, sub * tiles)
-            mask_last = ocean_at(ocean, block_row, (sub + 1) * tiles - 1)
-            mask_outer = jnp.where(
-                lane1 < LANES // 2,
-                ocean_at(ocean, block_row, (sub + 1) * tiles),
-                ocean_at(ocean, block_row, sub * tiles - 1),
-            )
+            block = mask_group(g * ROWS // BLOCK)
+            mask_first, mask_last, mask_outer = masks[block, first], masks[block, last], masks[block, outer]
             near, far = 4 * 6 + 32 * k, 4 * 6 + 3 + 32 * k
             tail = pltpu.roll(own_east, (-far) % LANES, 1)
             begin = pltpu.roll(own_west, (LANES - 1 - near) % LANES, 1)
@@ -435,7 +442,7 @@
 
 
 def basis_kernel(
-    ids, ocean, outer_center, edges, send_a, send_b, recv_a, recv_b, rows_a, rows_b,
+    masks, outer_center, edges, send_a, send_b, recv_a, recv_b, rows_a, rows_b,
     ax_in, ay_in, bly_in, nx_in, nxy_in, nxm_in, lxy_in, rxm_in, inv_in, c0_in, center_in,
     c1, c2, c3, c4, gram_ref, ax, ay, bly, nx, nxy, nxm, lxy, rxm, inv, c0, center,
 ):
@@ -444,7 +451,7 @@
     wide = col_count + LANES
     block_rows = row_count // BLOCK
     groups = row_count // ROWS
-    blk, sub = ids[0], ids[1]
+    blk, sub = own_place()
     even_sub, even_blk = (sub % 2) == 0, (blk % 2) == 0
     row8, lane8 = row_of((ROWS, wide)), lane_of((ROWS, wide))
     row1, lane1 = row_of((ROWS, LANES)), lane_of((ROWS, LANES))
@@ -464,9 +471,6 @@
     out_f, out_x, out_y, out_xy, out_xm, out_c = pieces
     flux_below, flux_above = out_x[3:4], out_y[4:5]
 
-    def mask_of(block_row):
-        return jnp.broadcast_to(mask_row(ocean, block_row, sub, tiles), (ROWS, wide))
-
     def edge_group(side, k):
         strip = 0 if side == 0 else groups // 4 - 1
         sides = side_tiles(send_a, send_b, recv_a, recv_b, even_sub, at(strip))
@@ -475,12 +479,12 @@
             jnp.concatenate([get(e), outer_tile(sides[2], sides[3], f, k)], axis=1)
             for e, f in ((1, 1), (3, 3), (4, 4), (6, 7))
         ]
-        mask = mask_of(blk * block_rows + (0 if side == 0 else block_rows - 1))
+        mask = masks[mask_group(0 if side == 0 else block_rows - 1)]
         return full, mask, force_with_sides(get(0), mask, sides, k)
 
     (_, _, _, flux_first), mask_first, force_first = edge_group(0, 0)
     (x_last, xy_last, xm_last, flux_last), mask_last, force_last = edge_group(1, 3)
-    mask_below, mask_above = mask_of((blk + 1) * block_rows), mask_of(blk * block_rows - 1)
+    mask_below, mask_above = masks[mask_group(block_rows)], masks[mask_group(block_rows + 1)]
 
     def inverse_of(mask, total):
         return jnp.where(mask > 0.0, 1.0 / jnp.where(total > 0.0, total, 1.0), 0.0)
@@ -701,23 +705,23 @@
     plane = shape(row_count, col_count)
     ring = shape(row_count + ROWS, wide)
     strip = shape(row_count // 4, LANES)
-    ids = jnp.stack([lax.axis_index("blk"), lax.axis_index("sub")]).astype(jnp.int32)
     flow = pltpu.VMEM((levels, row_count, col_count), F32)
     field = pltpu.VMEM((row_count, col_count), F32)
-    fp, cp, edges, send_a, send_b, *rings = pl.pallas_call(
+    fp, cp, edges, send_a, send_b, *rings, masks = pl.pallas_call(
         flux_kernel,
-        out_shape=(plane, plane, shape(14 * ROWS, col_count), strip, strip) + (ring,) * 6,
-        in_specs=[SMEM, SMEM, SMEM] + [HBM] * 8,
-        out_specs=(VMEM,) * 11,
+        out_shape=(plane, plane, shape(14 * ROWS, col_count), strip, strip)
+        + (ring,) * 6
+        + (shape((row_count // BLOCK + 2) * ROWS, wide),),
+        in_specs=[HBM] * 10,
+        out_specs=(VMEM,) * 12,
         scratch_shapes=[flow, flow, pltpu.VMEM((row_count, col_count), jnp.int32)]
         + [field] * 3
-        + [pltpu.VMEM((row_count // BLOCK * ROWS, col_count), F32)]
-        + [pltpu.SemaphoreType.DMA((2, row_count // CHUNK)), pltpu.SemaphoreType.DMA((6,))],
+        + [pltpu.SMEM(thickness.shape, F32), pltpu.SMEM(block_ocean.shape, jnp.int32)]
+        + [pltpu.SemaphoreType.DMA((2, row_count // CHUNK)), pltpu.SemaphoreType.DMA((6,)), pltpu.SemaphoreType.DMA((2,))],
         compiler_params=pltpu.CompilerParams(vmem_limit_bytes=FLUX_LIMIT),
         name="flux",
     )(
-        ids, thickness, block_ocean,
-        *[far(a) for a in (u_flow, v_flow, depth_levels, coef_x, coef_y, coef_xy, coef_xm, extra_diagonal)],
+        *[far(a) for a in (thickness, block_ocean, u_flow, v_flow, depth_levels, coef_x, coef_y, coef_xy, coef_xm, extra_diagonal)],
     )
     recv_a, recv_b = swap(send_a, "sub", 0), swap(send_b, "sub", 1)
     ax, ay, axy, axm, inv, c0 = rings
@@ -734,32 +738,32 @@
     edge_a, edge_b = pl.pallas_call(
         functools.partial(edge_kernel, row_count=row_count),
         out_shape=(edge, edge),
-        in_specs=[SMEM, SMEM] + [VMEM] * 5,
+        in_specs=[VMEM] * 7,
         out_specs=(VMEM,) * 2,
         compiler_params=pltpu.CompilerParams(vmem_limit_bytes=8 << 20),
         name="edge",
-    )(ids, block_ocean, edges, send_a, send_b, recv_a, recv_b)
+    )(masks, edges, send_a, send_b, recv_a, recv_b, moved[0])
     rows_a, rows_b = swap(edge_a, "blk", 0), swap(edge_b, "blk", 1)
     outer_center, *rings = pl.pallas_call(
         widen_kernel,
         out_shape=(shape(row_count, LANES),) + (ring,) * 10 + (plane,),
-        in_specs=[SMEM, SMEM] + [VMEM] * 16,
+        in_specs=[VMEM] * 17,
         out_specs=(VMEM,) * 12,
-        input_output_aliases={7 + i: 1 + i for i in range(11)},
+        input_output_aliases={6 + i: 1 + i for i in range(11)},
         compiler_params=pltpu.CompilerParams(vmem_limit_bytes=8 << 20),
         cost_estimate=pl.CostEstimate(flops=10 << 20, bytes_accessed=4 << 20, transcendentals=0),
         name="widen",
-    )(ids, block_ocean, fp, send_a, send_b, recv_a, recv_b, ax, ay, *moved, inv, c0, cp)
+    )(masks, fp, send_a, send_b, recv_a, recv_b, ax, ay, *moved, inv, c0, cp)
     devices = lax.axis_size("blk") * lax.axis_size("sub")
     c1, c2, c3, c4, gram, *rest = pl.pallas_call(
         basis_kernel,
         out_shape=(ring, ring, ring, plane, shape(devices, LANES)) + (ring,) * 10 + (plane,),
-        in_specs=[SMEM, SMEM] + [VMEM] * 19,
+        in_specs=[VMEM] * 20,
         out_specs=(VMEM,) * 16,
-        input_output_aliases={10 + i: 5 + i for i in range(11)},
+        input_output_aliases={9 + i: 5 + i for i in range(11)},
         compiler_params=pltpu.CompilerParams(vmem_limit_bytes=8 << 20),
         name="basis",
-    )(ids, block_ocean, outer_center, edges, send_a, send_b, recv_a, recv_b, rows_a, rows_b, *rings)
+    )(masks, outer_center, edges, send_a, send_b, recv_a, recv_b, rows_a, rows_b, *rings)
     c0, center = rest[-2], rest[-1]
     gram = lax.all_to_all(gram, ("blk", "sub"), 0, 0, tiled=True)
     return pl.pallas_call(

time: 47.9 us -> 44.1 us (0.921)
  Pallas kernels: 22.2 us -> 19.3 us
  blocking collectives: 17.6 us -> 19.2 us
  local copies, waits for them, and re-layouts: 1.35 us -> 0 us
  waiting for transfers between devices: 1.24 us -> 0.25 us
    all_to_all x1, blocking collectives: 17.6 us -> 19.2 us  [body(): gram = lax.all_to_all(gram, ('blk', 'sub'), 0, 0, tiled=True)]
    unnamed x4 -> x0, local copies, waits for them, and re-layouts: 1.35 us -> none
    pallas_call x1, Pallas kernels: 6.72 us -> 5.7 us  [body(): pl.pallas_call(basis_kernel, out_shape=(ring, ring, ring, plane, shape(de...]
    ppermute x4, waiting for transfers between devices: 1.24 us -> 0.25 us  [swap(): return lax.ppermute(value, axis, pairs)]
    pallas_call x1, Pallas kernels: 2.54 us -> 1.69 us  [body(): pl.pallas_call(widen_kernel, out_shape=(shape(row_count, LANES),) + (ring...]
    pallas_call x1, Pallas kernels: 0.83 us -> 0.16 us  [body(): pl.pallas_call(functools.partial(edge_kernel, row_count=row_count), out_s...]
  transfers between devices with their start and end apart: 4 -> 4, of which waited for: 1 -> 1; matrix products, arithmetic and copies ran while one was open for 0% -> 0% of each run, Pallas kernels for 7% -> 6%
where the time goes in v3:
time: 44.1 us; the launch traced here: 44 us
  Pallas kernels  19.3 us (44%)
  blocking collectives  19.2 us (44%)
  starting transfers between devices  4.5 us (10%)
  between operations  0.7 us (2%)
    all_to_all x1, blocking collectives, body(): gram = lax.all_to_all(gram, ('blk', 'sub'), 0, 0, tiled=True)  19.2 us
    pallas_call x1, Pallas kernels, body(): pl.pallas_call(flux_kernel, out_shape=(plane, plane, shape(14 * ROWS, col...  9.12 us
    pallas_call x1, Pallas kernels, body(): pl.pallas_call(basis_kernel, out_shape=(ring, ring, ring, plane, shape(de...  5.7 us
    ppermute x4, starting transfers between devices, swap(): return lax.ppermute(value, axis, pairs)  4.5 us
    pallas_call x1, Pallas kernels, body(): pl.pallas_call(widen_kernel, out_shape=(shape(row_count, LANES),) + (ring...  1.69 us
    pallas_call x1, Pallas kernels, body(): pl.pallas_call(finish_kernel, out_shape=(final, final), in_specs=[VMEM] *...  1.65 us
    pallas_call x1, Pallas kernels, body(): pl.pallas_call(prepare_kernel, out_shape=(ring,) * 6, in_specs=[VMEM] * 4...  0.98 us
  transfers between devices with their start and end apart: 4, of which 1 were waited for; matrix products, arithmetic and copies ran while one was open for 0% of the time, Pallas kernels for 6%

profile of v3, /device:TPU:0, one launch (start us, length us, event | category | flops | bytes accessed | tf_op | source)
XLA Modules:
  0.0 44.0 jit_solution(17069022989366583585)
XLA Ops:
  0.6 9.1 %flux.1 = (f32[256,512]{1,0:T(8,128)S(1)}, f32[256,512]{1,0:T(8,128)S(1)}, f32[112,512]{1,0:T(8,128)S(1)}, f32[64,128]{1,0:T(8,128)S(1)}, f32[64,128]{1,0:T(8,12...) custom-call(f32[16]{0:T(128)} %thick_hbm.1, ...), custom_call_target="tpu_custom_call" | custom-call | tf_op jit(solution)/shard_map/flux/pallas_call | solution.py:710
  9.8 3.1 %collective-permute-start = (f32[64,128]{1,0:T(8,128)S(1)}, f32[64,128]{1,0:T(8,128)S(1)}, u32[]{:S(2)}, u32[]{:S(2)}) collective-permute-start(f32[64,128]{1,0:T(8,128)S(1)} %get-tuple-element.43.send_a), channel_id=1, source_target_pairs={{0,1},{1,0},{2,3},{3,2},{4,5},{5,4},{6,7},{7,6},{8,9},{9,8},{10,11... | collective-permute-start | bytes 98312 | tf_op jit(solution)/shard_map/ppermute | solution.py:696
  12.9 0.7 %collective-permute-start.1 = (f32[64,128]{1,0:T(8,128)S(1)}, f32[64,128]{1,0:T(8,128)S(1)}, u32[]{:S(2)}, u32[]{:S(2)}) collective-permute-start(f32[64,128]{1,0:T(8,128)S(1)} %get-tuple-element.44.send_b), channel_id=1, source_target_pairs={{1,2},{2,1},{5,6},{6,5},{9,10},{10,9},{13,14},{14,13},{17,18},{18,... | collective-permute-start | bytes 98312 | tf_op jit(solution)/shard_map/ppermute | solution.py:696
  13.5 1.0 %prepare.1 = (f32[264,640]{1,0:T(8,128)S(1)}, f32[264,640]{1,0:T(8,128)S(1)}, f32[264,640]{1,0:T(8,128)S(1)}, f32[264,640]{1,0:T(8,128)S(1)}, f32[264,640]{1,0:T(8,128)S(1)}, /*index=5*/f32[264,640]{1,0:T(8,128)S(1)}) custom-call(f32[264,640]{1,0:T(8,128)S(1)} %get-tuple-element.45.ax.ax_in, f32[264,640]{1,0:T(8,128)S(1)} %get-tuple-element.46.ay.ay_in, ...), custom_call_target="tpu_custom_call" | custom-call | flops 10485760 | bytes 4194304 | tf_op jit(solution)/shard_map/prepare/pallas_call | solution.py:728
  14.5 0.2 collective-permute-done.recv_a
  14.8 0.0 collective-permute-done.1.recv_b
  14.8 0.2 edge.1
  14.9 0.1 collective-permute-start.2
  15.0 0.7 %collective-permute-start.3 = (f32[24,640]{1,0:T(8,128)S(1)}, f32[24,640]{1,0:T(8,128)S(1)}, u32[]{:S(2)}, u32[]{:S(2)}) collective-permute-start(f32[24,640]{1,0:T(8,128)S(1)} %get-tuple-element.61), channel_id=1, source_target_pairs={{4,8},{8,4},{12,16},{16,12},{20,24},{24,20},{5,9},{9,5},{13,17},{1... | collective-permute-start | bytes 184328 | tf_op jit(solution)/shard_map/ppermute | solution.py:696
  15.7 1.7 %widen.1 = (f32[256,128]{1,0:T(8,128)S(1)}, f32[264,640]{1,0:T(8,128)S(1)}, f32[264,640]{1,0:T(8,128)S(1)}, f32[264,640]{1,0:T(8,128)S(1)}, f32[264,640]{1,0:T(8...) custom-call(f32[32,640]{1,0:T(8,128)S(1)} %get-tuple-element.41.mask, ...), custom_call_target="tpu_custom_call", output_to_operand_aliasing={{1}: (6, {}), {2}: (7, {}), {3}: (8, {}), {4}: (9, {}), {5}... | custom-call | flops 10485760 | bytes 4194304 | tf_op jit(solution)/shard_map/widen/pallas_call | solution.py:747
  17.4 0.0 collective-permute-done.2.rows_a
  17.4 0.0 collective-permute-done.3.rows_b
  17.4 5.7 %basis.1 = (f32[264,640]{1,0:T(8,128)S(1)}, f32[264,640]{1,0:T(8,128)S(1)}, f32[264,640]{1,0:T(8,128)S(1)}, f32[256,512]{1,0:T(8,128)S(1)}, f32[32,128]{1,0:T(8,...) custom-call(f32[32,640]{1,0:T(8,128)S(1)} %get-tuple-element.41.mask, ...), custom_call_target="tpu_custom_call", output_to_operand_aliasing={{5}: (9, {}), {6}: (10, {}), {7}: (11, {}), {8}: (12, {}), ... | custom-call | tf_op jit(solution)/shard_map/basis/pallas_call | solution.py:758
  23.1 19.2 %all_to_all.11 = f32[32,1,128]{2,1,0:T(1,128)S(1)} all-to-all(f32[32,1,128]{2,1,0:T(1,128)S(1)} %bitcast.5), channel_id=1, replica_groups=mesh['blk'=8,'sub'=4] {'blk','sub'}, dimensions={0} | all-to-all | bytes 32768 | tf_op jit(solution)/shard_map/all_to_all | solution.py:768
  42.3 1.7 %finish.1 = (f32[256,512]{1,0:T(8,128)}, f32[256,512]{1,0:T(8,128)}) custom-call(f32[32,128]{1,0:T(8,128)S(1)} %bitcast.4, f32[264,640]{1,0:T(8,128)S(1)} %get-tuple-element.74.c0, f32[264,640]{1,0:T(8,128)S(1)} %get-tuple-element.75.c1, f32[264,640]{1,0:T(8,128)S(1)} %get-tuple-element.76.c2, f32[264,640]{1,0:T(8,128)S(1)} %get-tuple-element.77.c3, ...), custom_call_target="tpu_custom_call" | custom-call | tf_op jit(solution)/shard_map/finish/pallas_call | solution.py:769
Async XLA Ops:
  9.8 5.0 %collective-permute-start = (f32[64,128]{1,0:T(8,128)S(1)}, f32[64,128]{1,0:T(8,128)S(1)}, u32[]{:S(2)}, u32[]{:S(2)}) collective-permute-start(f32[64,128]{1,0:T(8,128)S(1)} %get-tuple-element.43.send_a), channel_id=1, source_target_pairs={{0,1},{1,0},{2,3},{3,2},{4,5},{5,4},{6,7},{7,6},{8,9},{9,8},{10,11... | collective-permute-start | bytes 98312 | tf_op jit(solution)/shard_map/ppermute | solution.py:696
  12.9 1.9 %collective-permute-start.1 = (f32[64,128]{1,0:T(8,128)S(1)}, f32[64,128]{1,0:T(8,128)S(1)}, u32[]{:S(2)}, u32[]{:S(2)}) collective-permute-start(f32[64,128]{1,0:T(8,128)S(1)} %get-tuple-element.44.send_b), channel_id=1, source_target_pairs={{1,2},{2,1},{5,6},{6,5},{9,10},{10,9},{13,14},{14,13},{17,18},{18,... | collective-permute-start | bytes 98312 | tf_op jit(solution)/shard_map/ppermute | solution.py:696
  14.9 2.5 %collective-permute-start.2 = (f32[24,640]{1,0:T(8,128)S(1)}, f32[24,640]{1,0:T(8,128)S(1)}, u32[]{:S(2)}, u32[]{:S(2)}) collective-permute-start(f32[24,640]{1,0:T(8,128)S(1)} %get-tuple-element.60), channel_id=1, source_target_pairs={{0,4},{4,0},{8,12},{12,8},{16,20},{20,16},{24,28},{28,24},{1,5},{5... | collective-permute-start | bytes 184328 | tf_op jit(solution)/shard_map/ppermute | solution.py:696
  15.0 2.4 %collective-permute-start.3 = (f32[24,640]{1,0:T(8,128)S(1)}, f32[24,640]{1,0:T(8,128)S(1)}, u32[]{:S(2)}, u32[]{:S(2)}) collective-permute-start(f32[24,640]{1,0:T(8,128)S(1)} %get-tuple-element.61), channel_id=1, source_target_pairs={{4,8},{8,4},{12,16},{16,12},{20,24},{24,20},{5,9},{9,5},{13,17},{1... | collective-permute-start | bytes 184328 | tf_op jit(solution)/shard_map/ppermute | solution.py:696

commit v4 on v3

--- a/solution.py
+++ b/solution.py
@@ -13,8 +13,10 @@
 LANES = 128
 ROWS = 8
 CHUNK = 32
-AHEAD = 3
+PIECE = 16
+AHEAD = 6
 UNROLL = 8
+PARTS = 4
 F32 = jnp.float32
 FLUX_LIMIT = 40 << 20
 VMEM = pl.BlockSpec(memory_space=pltpu.VMEM)
@@ -61,12 +63,13 @@
 
 def flux_kernel(
     thick_hbm, ocean_hbm, u_hbm, v_hbm, depth_hbm, cx_hbm, cy_hbm, cxy_hbm, cxm_hbm, ex_hbm,
-    fp_ref, cp_ref, edge_ref, pack_a, pack_b, ax, ay, axy, axm, inv, c0, masks,
+    fp_ref, cp_ref, edge_ref, pack_a, pack_b, ax, ay, axy, axm, masks,
     u_buf, v_buf, depth, ex, fu, fv, thick, ocean, sems, coef_sem, small_sem,
 ):
     levels, row_count, col_count = u_buf.shape
     tiles = col_count // LANES
     chunks = row_count // CHUNK
+    pieces = row_count // PIECE
     groups = row_count // ROWS
     steps = CHUNK // ROWS
     blk, sub = own_place()
@@ -83,7 +86,7 @@
     ]
 
     def flow_copies(c):
-        rows = pl.ds(pl.multiple_of(c * CHUNK, CHUNK), CHUNK)
+        rows = pl.ds(pl.multiple_of(c * PIECE, PIECE), PIECE)
         return (
             pltpu.make_async_copy(u_hbm.at[:, rows, :], u_buf.at[:, rows, :], sems.at[0, c]),
             pltpu.make_async_copy(v_hbm.at[:, rows, :], v_buf.at[:, rows, :], sems.at[1, c]),
@@ -169,10 +172,7 @@
         change = 0.5 * ((below - up_u) + (east_of(here_v) - west_of(here_v)))
         mask = masks[mask_group(g * ROWS // BLOCK), cols]
         partial = mask * change
-        inverse = mask * (1.0 / total)
         fp_ref[rows] = partial
-        inv[rows, cols] = inverse
-        c0[rows, cols] = partial * inverse
         fields = [partial, here_x, here_y, here_xy, here_xm, total, here_v, here_u]
         to_west = jnp.zeros((ROWS, LANES), F32)
         to_east = to_west
@@ -202,15 +202,21 @@
         return group_work(g, k, [jnp.where(g > 0, b, 0.0) for b in before])
 
     def chunk(c, _):
-        for copy in flow_copies(c):
-            copy.wait()
-
-        @pl.when(c + AHEAD < chunks)
-        def _():
-            for copy in flow_copies(c + AHEAD):
-                copy.start()
-
-        lax.fori_loop(0, steps, lambda i, _: (sum_group(c * steps + i), 0)[1], 0)
+        def piece(i, _):
+            p = c * (CHUNK // PIECE) + i
+            for copy in flow_copies(p):
+                copy.wait()
+
+            @pl.when(p + AHEAD < pieces)
+            def _():
+                for copy in flow_copies(p + AHEAD):
+                    copy.start()
+
+            for j in range(PIECE // ROWS):
+                sum_group(p * (PIECE // ROWS) + j)
+            return 0
+
+        lax.fori_loop(0, CHUNK // PIECE, piece, 0)
 
         @pl.when(c == 0)
         def _():
@@ -339,7 +345,7 @@
         rows_b[rows] = jnp.where(even_blk, results[0][pair], results[1][pair])
 
 
-def prepare_kernel(ax, ay, axy, axm, bly, nx, nxy, nxm, lxy, rxm):
+def prepare_kernel(fp, cp, masks, ax, ay, axy, axm, bly, nx, nxy, nxm, lxy, rxm, inv, c0):
     row_count, wide = ax.shape[0] - ROWS, ax.shape[1]
     cols = pl.ds(0, wide - LANES)
     lane8 = lane_of((ROWS, wide - LANES))
@@ -354,6 +360,9 @@
         rolled = tuple(down(v) for v in (ax[rows, cols], here_xy, here_xm))
         for ring, a, b in zip((nx, nxy, nxm), before, rolled):
             ring[rows, cols] = shifted_rows(a, b)
+        inverse = masks[mask_group(g * ROWS // BLOCK), cols] * (1.0 / cp[rows])
+        inv[rows, cols] = inverse
+        c0[rows, cols] = fp[rows] * inverse
         return rolled
 
     zero = jnp.zeros(lane8.shape, F32)
@@ -441,10 +450,76 @@
     lax.fori_loop(0, groups // 4, widen, (zero,) * 7)
 
 
+def group_rows(g):
+    return pl.ds(g * ROWS if isinstance(g, int) else pl.multiple_of(g * ROWS, ROWS), ROWS)
+
+
+def sides_of(source, g, width):
+    value = source[group_rows(g)]
+    return left(value)[:, :width], right(value)[:, :width]
+
+
+def terms(rings, source, g, width, turned):
+    ax, ay, bly, nx, nxy, nxm, lxy, rxm = rings
+    rows, cols = group_rows(g), pl.ds(0, width)
+    west, east = turned
+    here = source[rows, cols]
+    same = ay[rows, cols] * east + bly[rows, cols] * west
+    after = ax[rows, cols] * here + lxy[rows, cols] * west + rxm[rows, cols] * east
+    before = nx[rows, cols] * here + nxy[rows, cols] * east + nxm[rows, cols] * west
+    return same, down(after), pltpu.roll(before, ROWS - 1, 0)
+
+
+def sweep(rings, source, start, count, width, finish):
+    period = source.shape[0] // ROWS
+    at = lambda n: n % period
+    ahead, turned, following = [sides_of(source, at(start + d), width) for d in (-1, 0, 1)]
+    _, ring_after, _ = terms(rings, source, at(start - 1), width, ahead)
+    same, after, own_first = terms(rings, source, at(start), width, turned)
+    tail = row_of((ROWS, width)) == ROWS - 1
+
+    def advance(g, previous_group, next_group, carry):
+        partial, own, previous, turned = carry
+        following = sides_of(source, next_group, width)
+        same, after, later = terms(rings, source, g, width, turned)
+        finish(previous_group, partial + jnp.where(tail, later, own))
+        return same + shifted_rows(previous, after), later, after, following
+
+    carry = (same + shifted_rows(ring_after, after), own_first, after, following)
+    if start + count <= period:
+        body = lambda g, carry: advance(g, g - 1, jnp.minimum(g + 1, period - 1), carry)
+        carry = lax.fori_loop(start + 1, start + count, body, carry, unroll=UNROLL)
+    else:
+        for n in range(start + 1, start + count):
+            carry = advance(at(n), at(n - 1), at(n + 1), carry)
+    partial, own, _, turned = carry
+    if count == period:
+        later = own_first
+    else:
+        later = terms(rings, source, at(start + count), width, turned)[2]
+    finish(at(start + count - 1), partial + jnp.where(tail, later, own))
+
+
+def step(rings, inv, source, target, start, count, subtract):
+    def finish(g, total):
+        rows = group_rows(g)
+        moved = inv[rows] * total
+        target[rows] = source[rows] - moved if subtract else moved
+
+    sweep(rings, source, start, count, source.shape[1], finish)
+
+
+def early_kernel(ax, ay, bly, nx, nxy, nxm, lxy, rxm, inv, c0, c1, c2):
+    groups = c0.shape[0] // ROWS - 1
+    rings = (ax, ay, bly, nx, nxy, nxm, lxy, rxm)
+    step(rings, inv, c0, c1, 2, groups - 4, True)
+    step(rings, inv, c1, c2, 3, groups - 6, False)
+
+
 def basis_kernel(
     masks, outer_center, edges, send_a, send_b, recv_a, recv_b, rows_a, rows_b,
-    ax_in, ay_in, bly_in, nx_in, nxy_in, nxm_in, lxy_in, rxm_in, inv_in, c0_in, center_in,
-    c1, c2, c3, c4, gram_ref, ax, ay, bly, nx, nxy, nxm, lxy, rxm, inv, c0, center,
+    ax_in, ay_in, bly_in, nx_in, nxy_in, nxm_in, lxy_in, rxm_in, inv_in, c0_in, center_in, c1_in, c2_in,
+    c3, c4, gram_ref, ax, ay, bly, nx, nxy, nxm, lxy, rxm, inv, c0, center, c1, c2,
 ):
     row_count, col_count = center.shape
     tiles = col_count // LANES
@@ -529,58 +604,17 @@
     inv[ring_rows] = inverse
     c0[ring_rows] = inverse * out_f
 
-    def sides_of(source, g, width):
-        value = source[at(g)]
-        return left(value)[:, :width], right(value)[:, :width]
-
-    def terms(source, g, width, turned):
-        rows, cols = at(g), pl.ds(0, width)
-        west, east = turned
-        here = source[rows, cols]
-        same = ay[rows, cols] * east + bly[rows, cols] * west
-        after = ax[rows, cols] * here + lxy[rows, cols] * west + rxm[rows, cols] * east
-        before = nx[rows, cols] * here + nxy[rows, cols] * east + nxm[rows, cols] * west
-        return same, down(after), pltpu.roll(before, ROWS - 1, 0)
-
-    def sweep(source, count, width, finish):
-        ring_turned, turned, following = [sides_of(source, g, width) for g in (groups, 0, 1)]
-        _, ring_after, _ = terms(source, groups, width, ring_turned)
-        same, after, own_first = terms(source, 0, width, turned)
-        tail = row_of((ROWS, width)) == ROWS - 1
-
-        def body(g, carry):
-            partial, own, previous, turned = carry
-            following = sides_of(source, jnp.minimum(g + 1, groups), width)
-            same, after, later = terms(source, g, width, turned)
-            finish(g - 1, partial + jnp.where(tail, later, own))
-            return same + shifted_rows(previous, after), later, after, following
-
-        carry = (same + shifted_rows(ring_after, after), own_first, after, following)
-        partial, own, _, turned = lax.fori_loop(1, count, body, carry, unroll=UNROLL)
-        if count > groups:
-            later = own_first
-        else:
-            later = terms(source, groups, width, turned)[2]
-        finish(count - 1, partial + jnp.where(tail, later, own))
-
-    def step(source, target, subtract):
-        def finish(g, total):
-            rows = at(g)
-            moved = inv[rows] * total
-            target[rows] = source[rows] - moved if subtract else moved
-
-        sweep(source, groups + 1, wide, finish)
-
-    step(c0, c1, True)
-    step(c1, c2, False)
-    step(c2, c3, False)
+    rings = (ax, ay, bly, nx, nxy, nxm, lxy, rxm)
+    step(rings, inv, c0, c1, groups - 2, 5, True)
+    step(rings, inv, c1, c2, groups - 3, 7, False)
+    step(rings, inv, c2, c3, 0, groups + 1, False)
 
     cols = pl.ds(0, col_count)
 
     def last_finish(g, total):
         c4[at(g)] = inv[at(g), cols] * total
 
-    sweep(c3, groups, col_count, last_finish)
+    sweep(rings, c3, 0, groups, col_count, last_finish)
 
     def add_products(g, sums):
         rows = at(g)
@@ -618,7 +652,7 @@
     gram_ref[...] = jnp.broadcast_to(jnp.sum(packed, axis=0, keepdims=True), gram_ref.shape)
 
 
-def finish_kernel(gram_ref, c0, c1, c2, c3, c4, center_ref, height_ref, residual_ref):
+def finish_kernel(gram_ref, c0, c1, c2, c3, c4, center_ref, height_out, residual_out, height_ref, residual_ref, sems):
     lane1 = lane_of((1, LANES))
     high = gram_ref[...]
     low = jnp.zeros_like(high)
@@ -685,7 +719,17 @@
         residual_ref[rows] = center_ref[rows] * total
         return 0
 
-    lax.fori_loop(0, center_ref.shape[0] // ROWS, combine, 0, unroll=2)
+    row_count = center_ref.shape[0]
+    part = row_count // PARTS
+    copies = []
+    for p in range(PARTS):
+        lax.fori_loop(p * part // ROWS, (p + 1) * part // ROWS, combine, 0, unroll=4)
+        rows = pl.ds(p * part, part)
+        for i, (src, dst) in enumerate(((height_ref, height_out), (residual_ref, residual_out))):
+            copies.append(pltpu.make_async_copy(src.at[rows], dst.at[rows], sems.at[i, p]))
+            copies[-1].start()
+    for copy in copies:
+        copy.wait()
 
 
 def swap(value, axis, parity):
@@ -710,30 +754,30 @@
     fp, cp, edges, send_a, send_b, *rings, masks = pl.pallas_call(
         flux_kernel,
         out_shape=(plane, plane, shape(14 * ROWS, col_count), strip, strip)
-        + (ring,) * 6
+        + (ring,) * 4
         + (shape((row_count // BLOCK + 2) * ROWS, wide),),
         in_specs=[HBM] * 10,
-        out_specs=(VMEM,) * 12,
+        out_specs=(VMEM,) * 10,
         scratch_shapes=[flow, flow, pltpu.VMEM((row_count, col_count), jnp.int32)]
         + [field] * 3
         + [pltpu.SMEM(thickness.shape, F32), pltpu.SMEM(block_ocean.shape, jnp.int32)]
-        + [pltpu.SemaphoreType.DMA((2, row_count // CHUNK)), pltpu.SemaphoreType.DMA((6,)), pltpu.SemaphoreType.DMA((2,))],
+        + [pltpu.SemaphoreType.DMA((2, row_count // PIECE)), pltpu.SemaphoreType.DMA((6,)), pltpu.SemaphoreType.DMA((2,))],
         compiler_params=pltpu.CompilerParams(vmem_limit_bytes=FLUX_LIMIT),
         name="flux",
     )(
         *[far(a) for a in (thickness, block_ocean, u_flow, v_flow, depth_levels, coef_x, coef_y, coef_xy, coef_xm, extra_diagonal)],
     )
     recv_a, recv_b = swap(send_a, "sub", 0), swap(send_b, "sub", 1)
-    ax, ay, axy, axm, inv, c0 = rings
-    moved = pl.pallas_call(
+    ax, ay, axy, axm = rings
+    *moved, inv, c0 = pl.pallas_call(
         prepare_kernel,
-        out_shape=(ring,) * 6,
-        in_specs=[VMEM] * 4,
-        out_specs=(VMEM,) * 6,
+        out_shape=(ring,) * 8,
+        in_specs=[VMEM] * 7,
+        out_specs=(VMEM,) * 8,
         compiler_params=pltpu.CompilerParams(vmem_limit_bytes=8 << 20),
         cost_estimate=pl.CostEstimate(flops=10 << 20, bytes_accessed=4 << 20, transcendentals=0),
         name="prepare",
-    )(ax, ay, axy, axm)
+    )(fp, cp, masks, ax, ay, axy, axm)
     edge = shape(3 * ROWS, wide)
     edge_a, edge_b = pl.pallas_call(
         functools.partial(edge_kernel, row_count=row_count),
@@ -755,22 +799,32 @@
         name="widen",
     )(masks, fp, send_a, send_b, recv_a, recv_b, ax, ay, *moved, inv, c0, cp)
     devices = lax.axis_size("blk") * lax.axis_size("sub")
-    c1, c2, c3, c4, gram, *rest = pl.pallas_call(
+    early = pl.pallas_call(
+        early_kernel,
+        out_shape=(ring, ring),
+        in_specs=[VMEM] * 10,
+        out_specs=(VMEM,) * 2,
+        compiler_params=pltpu.CompilerParams(vmem_limit_bytes=8 << 20),
+        cost_estimate=pl.CostEstimate(flops=10 << 20, bytes_accessed=4 << 20, transcendentals=0),
+        name="early",
+    )(*rings[:10])
+    c3, c4, gram, *rest = pl.pallas_call(
         basis_kernel,
-        out_shape=(ring, ring, ring, plane, shape(devices, LANES)) + (ring,) * 10 + (plane,),
-        in_specs=[VMEM] * 20,
+        out_shape=(ring, plane, shape(devices, LANES)) + (ring,) * 10 + (plane, ring, ring),
+        in_specs=[VMEM] * 22,
         out_specs=(VMEM,) * 16,
-        input_output_aliases={9 + i: 5 + i for i in range(11)},
+        input_output_aliases={9 + i: 3 + i for i in range(13)},
         compiler_params=pltpu.CompilerParams(vmem_limit_bytes=8 << 20),
         name="basis",
-    )(masks, outer_center, edges, send_a, send_b, recv_a, recv_b, rows_a, rows_b, *rings)
-    c0, center = rest[-2], rest[-1]
+    )(masks, outer_center, edges, send_a, send_b, recv_a, recv_b, rows_a, rows_b, *rings, *early)
+    c0, center, c1, c2 = rest[-4:]
     gram = lax.all_to_all(gram, ("blk", "sub"), 0, 0, tiled=True)
     return pl.pallas_call(
         finish_kernel,
         out_shape=(final, final),
         in_specs=[VMEM] * 7,
-        out_specs=(VMEM,) * 2,
+        out_specs=(HBM,) * 2,
+        scratch_shapes=[field, field, pltpu.SemaphoreType.DMA((2, PARTS))],
         compiler_params=pltpu.CompilerParams(vmem_limit_bytes=8 << 20),
         name="finish",
     )(gram, c0, c1, c2, c3, c4, center)

time: 44.1 us -> 42.3 us (0.959)
  blocking collectives: 19.2 us -> 17.6 us
    all_to_all x1, blocking collectives: 19.2 us -> 17.6 us  [body(): gram = lax.all_to_all(gram, ('blk', 'sub'), 0, 0, tiled=True)]
    pallas_call x2 -> x3, Pallas kernels: 6.69 us -> 6.88 us  [the longest x1 4.01 us: body(): pl.pallas_call(basis_kernel, out_shape=(ring, plane, shape(devices, LANES...]
  transfers between devices with their start and end apart: 4 -> 4, of which waited for: 1 -> 1; matrix products, arithmetic and copies ran while one was open for 0% -> 0% of each run, Pallas kernels for 6% -> 11%
where the time goes in v4:
time: 42.3 us; the launch traced here: 42.2 us
  Pallas kernels  19.1 us (45%)
  blocking collectives  17.6 us (42%)
  starting transfers between devices  4.5 us (11%)
  between operations  0.71 us (2%)
    all_to_all x1, blocking collectives, body(): gram = lax.all_to_all(gram, ('blk', 'sub'), 0, 0, tiled=True)  17.6 us
    pallas_call x1, Pallas kernels, body(): pl.pallas_call(flux_kernel, out_shape=(plane, plane, shape(14 * ROWS, col...  9.02 us
    ppermute x4, starting transfers between devices, swap(): return lax.ppermute(value, axis, pairs)  4.5 us
    pallas_call x1, Pallas kernels, body(): pl.pallas_call(basis_kernel, out_shape=(ring, plane, shape(devices, LANES...  4.01 us
    pallas_call x1, Pallas kernels, body(): pl.pallas_call(early_kernel, out_shape=(ring, ring), in_specs=[VMEM] * 10...  1.87 us
    pallas_call x1, Pallas kernels, body(): pl.pallas_call(widen_kernel, out_shape=(shape(row_count, LANES),) + (ring...  1.69 us
    pallas_call x1, Pallas kernels, body(): pl.pallas_call(finish_kernel, out_shape=(final, final), in_specs=[VMEM] *...  1.37 us
    pallas_call x1, Pallas kernels, body(): pl.pallas_call(prepare_kernel, out_shape=(ring,) * 8, in_specs=[VMEM] * 7...  0.99 us
  transfers between devices with their start and end apart: 4, of which 1 were waited for; matrix products, arithmetic and copies ran while one was open for 0% of the time, Pallas kernels for 11%

profile of v4, /device:TPU:0, one launch (start us, length us, event | category | flops | bytes accessed | tf_op | source)
XLA Modules:
  0.0 42.2 jit_solution(10086697540294624654)
XLA Ops:
  0.6 9.0 %flux.1 = (f32[256,512]{1,0:T(8,128)S(1)}, f32[256,512]{1,0:T(8,128)S(1)}, f32[112,512]{1,0:T(8,128)S(1)}, f32[64,128]{1,0:T(8,128)S(1)}, f32[64,128]{1,0:T(8,12...) custom-call(f32[16]{0:T(128)} %thick_hbm.1, ...), custom_call_target="tpu_custom_call" | custom-call | tf_op jit(solution)/shard_map/flux/pallas_call | solution.py:754
  9.7 3.1 %collective-permute-start = (f32[64,128]{1,0:T(8,128)S(1)}, f32[64,128]{1,0:T(8,128)S(1)}, u32[]{:S(2)}, u32[]{:S(2)}) collective-permute-start(f32[64,128]{1,0:T(8,128)S(1)} %get-tuple-element.45.send_a), channel_id=1, source_target_pairs={{0,1},{1,0},{2,3},{3,2},{4,5},{5,4},{6,7},{7,6},{8,9},{9,8},{10,11... | collective-permute-start | bytes 98312 | tf_op jit(solution)/shard_map/ppermute | solution.py:740
  12.8 0.7 %collective-permute-start.1 = (f32[64,128]{1,0:T(8,128)S(1)}, f32[64,128]{1,0:T(8,128)S(1)}, u32[]{:S(2)}, u32[]{:S(2)}) collective-permute-start(f32[64,128]{1,0:T(8,128)S(1)} %get-tuple-element.46.send_b), channel_id=1, source_target_pairs={{1,2},{2,1},{5,6},{6,5},{9,10},{10,9},{13,14},{14,13},{17,18},{18,... | collective-permute-start | bytes 98312 | tf_op jit(solution)/shard_map/ppermute | solution.py:740
  13.4 1.0 %prepare.1 = (f32[264,640]{1,0:T(8,128)S(1)}, f32[264,640]{1,0:T(8,128)S(1)}, f32[264,640]{1,0:T(8,128)S(1)}, f32[264,640]{1,0:T(8,128)S(1)}, f32[264,640]{1,0:T...) custom-call(f32[256,512]{1,0:T(8,128)S(1)} %get-tuple-element.44.fp, ...), custom_call_target="tpu_custom_call" | custom-call | flops 10485760 | bytes 4194304 | tf_op jit(solution)/shard_map/prepare/pallas_call | solution.py:772
  14.4 0.2 collective-permute-done.recv_a
  14.7 0.0 collective-permute-done.1.recv_b
  14.7 0.2 edge.1
  14.8 0.1 collective-permute-start.2
  14.9 0.7 %collective-permute-start.3 = (f32[24,640]{1,0:T(8,128)S(1)}, f32[24,640]{1,0:T(8,128)S(1)}, u32[]{:S(2)}, u32[]{:S(2)}) collective-permute-start(f32[24,640]{1,0:T(8,128)S(1)} %get-tuple-element.63), channel_id=1, source_target_pairs={{4,8},{8,4},{12,16},{16,12},{20,24},{24,20},{5,9},{9,5},{13,17},{1... | collective-permute-start | bytes 184328 | tf_op jit(solution)/shard_map/ppermute | solution.py:740
  15.6 1.7 %widen.1 = (f32[256,128]{1,0:T(8,128)S(1)}, f32[264,640]{1,0:T(8,128)S(1)}, f32[264,640]{1,0:T(8,128)S(1)}, f32[264,640]{1,0:T(8,128)S(1)}, f32[264,640]{1,0:T(8...) custom-call(f32[32,640]{1,0:T(8,128)S(1)} %get-tuple-element.43.mask, ...), custom_call_target="tpu_custom_call", output_to_operand_aliasing={{1}: (6, {}), {2}: (7, {}), {3}: (8, {}), {4}: (9, {}), {5}... | custom-call | flops 10485760 | bytes 4194304 | tf_op jit(solution)/shard_map/widen/pallas_call | solution.py:791
  17.3 1.9 %early.1 = (f32[264,640]{1,0:T(8,128)S(1)}, f32[264,640]{1,0:T(8,128)S(1)}) custom-call(f32[264,640]{1,0:T(8,128)S(1)} %get-tuple-element.64.ax.ax_in, f32[264,640]{1,0:T(8,128)S(1)} %get-tuple-element.65.ay.ay_in, f32[264,640]{1,0:T(8,128)S(1)} %get-tuple-element.66.bly.bly_in, f32[264,640]{1,0:T(8,128)S(1)} %get-tuple-element.67.nx.nx_in, ...), custom_call_target="tpu_custom_call" | custom-call | flops 10485760 | bytes 4194304 | tf_op jit(solution)/shard_map/early/pallas_call | solution.py:802
  19.2 0.0 collective-permute-done.2.rows_a
  19.2 0.0 collective-permute-done.3.rows_b
  19.2 4.0 %basis.1 = (f32[264,640]{1,0:T(8,128)S(1)}, f32[256,512]{1,0:T(8,128)S(1)}, f32[32,128]{1,0:T(8,128)S(1)}, f32[264,640]{1,0:T(8,128)S(1)}, f32[264,640]{1,0:T(8,...) custom-call(f32[32,640]{1,0:T(8,128)S(1)} %get-tuple-element.43.mask, ...), custom_call_target="tpu_custom_call", output_to_operand_aliasing={{3}: (9, {}), {4}: (10, {}), {5}: (11, {}), {6}: (12, {}), ... | custom-call | tf_op jit(solution)/shard_map/basis/pallas_call | solution.py:811
  23.2 17.6 %all_to_all.11 = f32[32,1,128]{2,1,0:T(1,128)S(1)} all-to-all(f32[32,1,128]{2,1,0:T(1,128)S(1)} %bitcast.5), channel_id=1, replica_groups=mesh['blk'=8,'sub'=4] {'blk','sub'}, dimensions={0} | all-to-all | bytes 32768 | tf_op jit(solution)/shard_map/all_to_all | solution.py:821
  40.8 1.4 %finish.1 = (f32[256,512]{1,0:T(8,128)}, f32[256,512]{1,0:T(8,128)}) custom-call(f32[32,128]{1,0:T(8,128)S(1)} %bitcast.4, f32[264,640]{1,0:T(8,128)S(1)} %get-tuple-element.78.c0, f32[264,640]{1,0:T(8,128)S(1)} %get-tuple-element.79.c1, f32[264,640]{1,0:T(8,128)S(1)} %get-tuple-element.80.c2, f32[264,640]{1,0:T(8,128)S(1)} %get-tuple-element.81.c3, ...), custom_call_target="tpu_custom_call" | custom-call | tf_op jit(solution)/shard_map/finish/pallas_call | solution.py:822
Async XLA Ops:
  9.7 5.0 %collective-permute-start = (f32[64,128]{1,0:T(8,128)S(1)}, f32[64,128]{1,0:T(8,128)S(1)}, u32[]{:S(2)}, u32[]{:S(2)}) collective-permute-start(f32[64,128]{1,0:T(8,128)S(1)} %get-tuple-element.45.send_a), channel_id=1, source_target_pairs={{0,1},{1,0},{2,3},{3,2},{4,5},{5,4},{6,7},{7,6},{8,9},{9,8},{10,11... | collective-permute-start | bytes 98312 | tf_op jit(solution)/shard_map/ppermute | solution.py:740
  12.8 1.9 %collective-permute-start.1 = (f32[64,128]{1,0:T(8,128)S(1)}, f32[64,128]{1,0:T(8,128)S(1)}, u32[]{:S(2)}, u32[]{:S(2)}) collective-permute-start(f32[64,128]{1,0:T(8,128)S(1)} %get-tuple-element.46.send_b), channel_id=1, source_target_pairs={{1,2},{2,1},{5,6},{6,5},{9,10},{10,9},{13,14},{14,13},{17,18},{18,... | collective-permute-start | bytes 98312 | tf_op jit(solution)/shard_map/ppermute | solution.py:740
  14.8 4.3 %collective-permute-start.2 = (f32[24,640]{1,0:T(8,128)S(1)}, f32[24,640]{1,0:T(8,128)S(1)}, u32[]{:S(2)}, u32[]{:S(2)}) collective-permute-start(f32[24,640]{1,0:T(8,128)S(1)} %get-tuple-element.62), channel_id=1, source_target_pairs={{0,4},{4,0},{8,12},{12,8},{16,20},{20,16},{24,28},{28,24},{1,5},{5... | collective-permute-start | bytes 184328 | tf_op jit(solution)/shard_map/ppermute | solution.py:740
  14.9 4.3 %collective-permute-start.3 = (f32[24,640]{1,0:T(8,128)S(1)}, f32[24,640]{1,0:T(8,128)S(1)}, u32[]{:S(2)}, u32[]{:S(2)}) collective-permute-start(f32[24,640]{1,0:T(8,128)S(1)} %get-tuple-element.63), channel_id=1, source_target_pairs={{4,8},{8,4},{12,16},{16,12},{20,24},{24,20},{5,9},{9,5},{13,17},{1... | collective-permute-start | bytes 184328 | tf_op jit(solution)/shard_map/ppermute | solution.py:740

commit v5 on v4

--- a/solution.py
+++ b/solution.py
@@ -63,8 +63,8 @@
 
 def flux_kernel(
     thick_hbm, ocean_hbm, u_hbm, v_hbm, depth_hbm, cx_hbm, cy_hbm, cxy_hbm, cxm_hbm, ex_hbm,
-    fp_ref, cp_ref, edge_ref, pack_a, pack_b, ax, ay, axy, axm, masks,
-    u_buf, v_buf, depth, ex, fu, fv, thick, ocean, sems, coef_sem, small_sem,
+    fu, fv, ex, edge_ref, pack_a, pack_b, ax, ay, axy, axm, masks,
+    u_buf, v_buf, depth, thick, ocean, sems, coef_sem, small_sem,
 ):
     levels, row_count, col_count = u_buf.shape
     tiles = col_count // LANES
@@ -115,11 +115,14 @@
         )
     coef_copies[0].wait()
 
-    row8 = row_of((ROWS, col_count))
-    lane8 = lane_of((ROWS, col_count))
+    row8 = row_of((ROWS, 2 * LANES))
+    lane8 = lane_of((ROWS, 2 * LANES))
     lane1 = lane_of((ROWS, LANES))
-    cols = pl.ds(0, col_count)
+    first, final = pl.ds(0, LANES), pl.ds(col_count - LANES, LANES)
     even = (sub % 2) == 0
+
+    def ends(ref, rows):
+        return jnp.concatenate([ref[rows, first], ref[rows, final]], axis=1)
 
     def at(g):
         return pl.ds(pl.multiple_of(g * ROWS, ROWS), ROWS)
@@ -128,11 +131,11 @@
         return jnp.where(lane8 == 0, 0.0, left(value))
 
     def east_of(value):
-        return jnp.where(lane8 == col_count - 1, 0.0, right(value))
+        return jnp.where(lane8 == 2 * LANES - 1, 0.0, right(value))
 
     def rolled_fields(rows):
         return [
-            down(v) for v in (ax[rows, cols], west_of(axy[rows, cols]), east_of(axm[rows, cols]), fu[rows])
+            down(v) for v in (ends(ax, rows), west_of(ends(axy, rows)), east_of(ends(axm, rows)), ends(fu, rows))
         ]
 
     def sum_group(g):
@@ -152,12 +155,11 @@
 
     def group_work(g, k, before):
         rows = at(g)
-        here_x, here_y, here_xy, here_xm = ax[rows, cols], ay[rows, cols], axy[rows, cols], axm[rows, cols]
-        here_u, here_v = fu[rows], fv[rows]
+        here_x, here_y, here_xy, here_xm, here_u, here_v = [ends(ref, rows) for ref in (ax, ay, axy, axm, fu, fv)]
         west_xy, east_xm, west_y = west_of(here_xy), east_of(here_xm), west_of(here_y)
         rolled = [down(v) for v in (here_x, west_xy, east_xm, here_u)]
         up_x, up_west, up_east, up_u = [shifted_rows(a, b) for a, b in zip(before, rolled)]
-        total = ex[rows] + here_x
+        total = ends(ex, rows) + here_x
         total = total + up_x
         total = total + here_y
         total = total + west_y
@@ -165,14 +167,12 @@
         total = total + up_west
         total = total + here_xm
         total = total + up_east
-        cp_ref[rows] = total
-        after = fu[at(jnp.minimum(g + 1, groups - 1))]
+        after = ends(fu, at(jnp.minimum(g + 1, groups - 1)))
         after = jnp.where(g + 1 < groups, pltpu.roll(after, ROWS - 1, 0), 0.0)
         below = jnp.where(row8 == ROWS - 1, after, pltpu.roll(here_u, ROWS - 1, 0))
         change = 0.5 * ((below - up_u) + (east_of(here_v) - west_of(here_v)))
-        mask = masks[mask_group(g * ROWS // BLOCK), cols]
+        mask = ends(masks, mask_group(g * ROWS // BLOCK))
         partial = mask * change
-        fp_ref[rows] = partial
         fields = [partial, here_x, here_y, here_xy, here_xm, total, here_v, here_u]
         to_west = jnp.zeros((ROWS, LANES), F32)
         to_east = to_west
@@ -237,9 +237,9 @@
     for side, base in enumerate((0, row_count - ROWS)):
         rows = pl.ds(base, ROWS)
         for f, field in enumerate(
-            [fp_ref[rows], ax[rows, cols], ay[rows, cols], axy[rows, cols], axm[rows, cols], cp_ref[rows], fu[rows]]
+            [ax[rows, own[1]], ay[rows, own[1]], axy[rows, own[1]], axm[rows, own[1]], fu[rows]]
         ):
-            edge_ref[pl.ds((side * 7 + f) * ROWS, ROWS)] = field
+            edge_ref[pl.ds((side * 5 + f) * ROWS, ROWS)] = field
 
 
 def side_tiles(send_a, send_b, recv_a, recv_b, even, packed):
@@ -303,7 +303,7 @@
     return jnp.concatenate(parts, axis=1)
 
 
-def edge_kernel(masks, edges, send_a, send_b, recv_a, recv_b, _, rows_a, rows_b, *, row_count):
+def edge_kernel(masks, edges, made, send_a, send_b, recv_a, recv_b, rows_a, rows_b, *, row_count):
     col_count = edges.shape[1]
     tiles = col_count // LANES
     block_rows = row_count // BLOCK
@@ -318,7 +318,8 @@
     for side, top in enumerate((True, False)):
         k = 0 if top else 3
         packed = pl.ds(0 if top else (strips - 1) * ROWS, ROWS)
-        rows = [edges[pl.ds((side * 7 + f) * ROWS, ROWS)] for f in range(7)]
+        rows = [edges[pl.ds((side * 5 + f) * ROWS, ROWS)] for f in range(5)]
+        rows = [made[pl.ds(2 * side * ROWS, ROWS)], *rows[:4], made[pl.ds((2 * side + 1) * ROWS, ROWS)], rows[4]]
         sides = side_tiles(send_a, send_b, recv_a, recv_b, even_sub, packed)
         mask = masks[mask_group(0 if top else block_rows - 1)]
         fields = [force_with_sides(rows[0], mask, sides, k)]
@@ -345,28 +346,54 @@
         rows_b[rows] = jnp.where(even_blk, results[0][pair], results[1][pair])
 
 
-def prepare_kernel(fp, cp, masks, ax, ay, axy, axm, bly, nx, nxy, nxm, lxy, rxm, inv, c0):
-    row_count, wide = ax.shape[0] - ROWS, ax.shape[1]
-    cols = pl.ds(0, wide - LANES)
-    lane8 = lane_of((ROWS, wide - LANES))
-    end = lane8 == wide - LANES - 1
+def prepare_kernel(
+    fu, fv, ex, masks, ax, ay, axy, axm,
+    fp, cp, edge_ref, bly, nx, nxy, nxm, lxy, rxm, inv, c0,
+):
+    row_count, col_count = fp.shape
+    groups = row_count // ROWS
+    cols = pl.ds(0, col_count)
+    row8, lane8 = row_of((ROWS, col_count)), lane_of((ROWS, col_count))
+    begin, end = lane8 == 0, lane8 == col_count - 1
+    head, tail = row8 == 0, row8 == ROWS - 1
 
     def body(g, before):
-        rows = pl.ds(pl.multiple_of(g * ROWS, ROWS), ROWS)
-        here_xy, here_xm = axy[rows, cols], axm[rows, cols]
-        bly[rows, cols] = jnp.where(lane8 == 0, 0.0, left(ay[rows, cols]))
-        lxy[rows, cols] = jnp.where(lane8 == 0, 0.0, left(here_xy))
-        rxm[rows, cols] = jnp.where(end, 0.0, right(here_xm))
-        rolled = tuple(down(v) for v in (ax[rows, cols], here_xy, here_xm))
-        for ring, a, b in zip((nx, nxy, nxm), before, rolled):
-            ring[rows, cols] = shifted_rows(a, b)
-        inverse = masks[mask_group(g * ROWS // BLOCK), cols] * (1.0 / cp[rows])
+        rows = group_rows(g)
+        here_x, here_y, here_xy, here_xm = [ref[rows, cols] for ref in (ax, ay, axy, axm)]
+        here_u, here_v = fu[rows], fv[rows]
+        west_y = jnp.where(begin, 0.0, left(here_y))
+        west_xy = jnp.where(begin, 0.0, left(here_xy))
+        east_xm = jnp.where(end, 0.0, right(here_xm))
+        rolled = tuple(down(v) for v in (here_x, here_xy, here_xm, west_xy, east_xm, here_u))
+        up_x, up_xy, up_xm, up_west, up_east, up_u = [jnp.where(head, a, b) for a, b in zip(before, rolled)]
+        total = ex[rows] + here_x
+        total = total + up_x
+        total = total + here_y
+        total = total + west_y
+        total = total + here_xy
+        total = total + up_west
+        total = total + here_xm
+        total = total + up_east
+        cp[rows] = total
+        for ring, value in ((bly, west_y), (nx, up_x), (nxy, up_xy), (nxm, up_xm), (lxy, west_xy), (rxm, east_xm)):
+            ring[rows, cols] = value
+        after = pltpu.roll(fu[group_rows(jnp.minimum(g + 1, groups - 1))], ROWS - 1, 0)
+        below = jnp.where(tail, jnp.where(g + 1 < groups, after, 0.0), pltpu.roll(here_u, ROWS - 1, 0))
+        across = jnp.where(end, 0.0, right(here_v)) - jnp.where(begin, 0.0, left(here_v))
+        mask = masks[mask_group(g * ROWS // BLOCK), cols]
+        partial = mask * (0.5 * ((below - up_u) + across))
+        fp[rows] = partial
+        inverse = mask * (1.0 / total)
         inv[rows, cols] = inverse
-        c0[rows, cols] = fp[rows] * inverse
+        c0[rows, cols] = partial * inverse
         return rolled
 
-    zero = jnp.zeros(lane8.shape, F32)
-    lax.fori_loop(0, row_count // ROWS, body, (zero, zero, zero), unroll=4)
+    zero = jnp.zeros((ROWS, col_count), F32)
+    lax.fori_loop(0, groups, body, (zero,) * 6, unroll=4)
+    for side, base in enumerate((0, row_count - ROWS)):
+        rows = pl.ds(base, ROWS)
+        edge_ref[pl.ds(2 * side * ROWS, ROWS)] = fp[rows]
+        edge_ref[pl.ds((2 * side + 1) * ROWS, ROWS)] = cp[rows]
 
 
 def widen_kernel(
@@ -517,7 +544,7 @@
 
 
 def basis_kernel(
-    masks, outer_center, edges, send_a, send_b, recv_a, recv_b, rows_a, rows_b,
+    masks, outer_center, edges, made, send_a, send_b, recv_a, recv_b, rows_a, rows_b,
     ax_in, ay_in, bly_in, nx_in, nxy_in, nxm_in, lxy_in, rxm_in, inv_in, c0_in, center_in, c1_in, c2_in,
     c3, c4, gram_ref, ax, ay, bly, nx, nxy, nxm, lxy, rxm, inv, c0, center, c1, c2,
 ):
@@ -549,13 +576,13 @@
     def edge_group(side, k):
         strip = 0 if side == 0 else groups // 4 - 1
         sides = side_tiles(send_a, send_b, recv_a, recv_b, even_sub, at(strip))
-        get = lambda f: edges[pl.ds((side * 7 + f) * ROWS, ROWS)]
+        get = lambda f: edges[pl.ds((side * 5 + f) * ROWS, ROWS)]
         full = [
             jnp.concatenate([get(e), outer_tile(sides[2], sides[3], f, k)], axis=1)
-            for e, f in ((1, 1), (3, 3), (4, 4), (6, 7))
+            for e, f in ((0, 1), (2, 3), (3, 4), (4, 7))
         ]
         mask = masks[mask_group(0 if side == 0 else block_rows - 1)]
-        return full, mask, force_with_sides(get(0), mask, sides, k)
+        return full, mask, force_with_sides(made[pl.ds(2 * side * ROWS, ROWS)], mask, sides, k)
 
     (_, _, _, flux_first), mask_first, force_first = edge_group(0, 0)
     (x_last, xy_last, xm_last, flux_last), mask_last, force_last = edge_group(1, 3)
@@ -644,9 +671,10 @@
             error = error + pltpu.roll(error, shift, 0) + rounding
         high = jnp.where(place == index, total[0:1], high)
         low = jnp.where(place == index, error[0:1], low)
-    for shift in (64, 32, 16, 8, 4, 2, 1):
-        high, rounding = two_sum(high, pltpu.roll(high, shift, 1))
-        low = low + pltpu.roll(low, shift, 1) + rounding
+    scale = (2.0 * LANES) * jnp.max(jnp.abs(high), axis=1, keepdims=True)
+    coarse = (high + scale) - scale
+    low = jnp.sum(low + (high - coarse), axis=1, keepdims=True)
+    high = jnp.sum(coarse, axis=1, keepdims=True)
     lane2 = lane_of((2 * ROWS, LANES))
     packed = jnp.where(lane2 == place, high, jnp.where(lane2 == place + LANES // 2, low, 0.0))
     gram_ref[...] = jnp.broadcast_to(jnp.sum(packed, axis=0, keepdims=True), gram_ref.shape)
@@ -751,15 +779,14 @@
     strip = shape(row_count // 4, LANES)
     flow = pltpu.VMEM((levels, row_count, col_count), F32)
     field = pltpu.VMEM((row_count, col_count), F32)
-    fp, cp, edges, send_a, send_b, *rings, masks = pl.pallas_call(
+    flux_u, flux_v, extra, edges, send_a, send_b, *rings, masks = pl.pallas_call(
         flux_kernel,
-        out_shape=(plane, plane, shape(14 * ROWS, col_count), strip, strip)
+        out_shape=(plane, plane, plane, shape(10 * ROWS, col_count), strip, strip)
         + (ring,) * 4
         + (shape((row_count // BLOCK + 2) * ROWS, wide),),
         in_specs=[HBM] * 10,
-        out_specs=(VMEM,) * 10,
+        out_specs=(VMEM,) * 11,
         scratch_shapes=[flow, flow, pltpu.VMEM((row_count, col_count), jnp.int32)]
-        + [field] * 3
         + [pltpu.SMEM(thickness.shape, F32), pltpu.SMEM(block_ocean.shape, jnp.int32)]
         + [pltpu.SemaphoreType.DMA((2, row_count // PIECE)), pltpu.SemaphoreType.DMA((6,)), pltpu.SemaphoreType.DMA((2,))],
         compiler_params=pltpu.CompilerParams(vmem_limit_bytes=FLUX_LIMIT),
@@ -769,15 +796,15 @@
     )
     recv_a, recv_b = swap(send_a, "sub", 0), swap(send_b, "sub", 1)
     ax, ay, axy, axm = rings
-    *moved, inv, c0 = pl.pallas_call(
+    fp, cp, made, *moved, inv, c0 = pl.pallas_call(
         prepare_kernel,
-        out_shape=(ring,) * 8,
-        in_specs=[VMEM] * 7,
-        out_specs=(VMEM,) * 8,
+        out_shape=(plane, plane, shape(4 * ROWS, col_count)) + (ring,) * 8,
+        in_specs=[VMEM] * 8,
+        out_specs=(VMEM,) * 11,
         compiler_params=pltpu.CompilerParams(vmem_limit_bytes=8 << 20),
         cost_estimate=pl.CostEstimate(flops=10 << 20, bytes_accessed=4 << 20, transcendentals=0),
         name="prepare",
-    )(fp, cp, masks, ax, ay, axy, axm)
+    )(flux_u, flux_v, extra, masks, ax, ay, axy, axm)
     edge = shape(3 * ROWS, wide)
     edge_a, edge_b = pl.pallas_call(
         functools.partial(edge_kernel, row_count=row_count),
@@ -786,7 +813,7 @@
         out_specs=(VMEM,) * 2,
         compiler_params=pltpu.CompilerParams(vmem_limit_bytes=8 << 20),
         name="edge",
-    )(masks, edges, send_a, send_b, recv_a, recv_b, moved[0])
+    )(masks, edges, made, send_a, send_b, recv_a, recv_b)
     rows_a, rows_b = swap(edge_a, "blk", 0), swap(edge_b, "blk", 1)
     outer_center, *rings = pl.pallas_call(
         widen_kernel,
@@ -811,12 +838,12 @@
     c3, c4, gram, *rest = pl.pallas_call(
         basis_kernel,
         out_shape=(ring, plane, shape(devices, LANES)) + (ring,) * 10 + (plane, ring, ring),
-        in_specs=[VMEM] * 22,
+        in_specs=[VMEM] * 23,
         out_specs=(VMEM,) * 16,
-        input_output_aliases={9 + i: 3 + i for i in range(13)},
+        input_output_aliases={10 + i: 3 + i for i in range(13)},
         compiler_params=pltpu.CompilerParams(vmem_limit_bytes=8 << 20),
         name="basis",
-    )(masks, outer_center, edges, send_a, send_b, recv_a, recv_b, rows_a, rows_b, *rings, *early)
+    )(masks, outer_center, edges, made, send_a, send_b, recv_a, recv_b, rows_a, rows_b, *rings, *early)
     c0, center, c1, c2 = rest[-4:]
     gram = lax.all_to_all(gram, ("blk", "sub"), 0, 0, tiled=True)
     return pl.pallas_call(

time: 42.3 us -> 41.5 us (0.981)
  Pallas kernels: 19.1 us -> 18.6 us
  transfers between devices with their start and end apart: 4 -> 4, of which waited for: 1 -> 0; matrix products, arithmetic and copies ran while one was open for 0% -> 0% of each run, Pallas kernels for 11% -> 12%
where the time goes in v5:
time: 41.5 us; the launch traced here: 41.3 us
  Pallas kernels  18.6 us (45%)
  blocking collectives  17.5 us (42%)
  starting transfers between devices  4.5 us (11%)
  between operations  0.72 us (2%)
    all_to_all x1, blocking collectives, body(): gram = lax.all_to_all(gram, ('blk', 'sub'), 0, 0, tiled=True)  17.5 us
    pallas_call x1, Pallas kernels, body(): pl.pallas_call(flux_kernel, out_shape=(plane, plane, plane, shape(10 * RO...  8.56 us
    ppermute x4, starting transfers between devices, swap(): return lax.ppermute(value, axis, pairs)  4.5 us
    pallas_call x1, Pallas kernels, body(): pl.pallas_call(basis_kernel, out_shape=(ring, plane, shape(devices, LANES...  3.6 us
    pallas_call x1, Pallas kernels, body(): pl.pallas_call(early_kernel, out_shape=(ring, ring), in_specs=[VMEM] * 10...  1.84 us
    pallas_call x1, Pallas kernels, body(): pl.pallas_call(widen_kernel, out_shape=(shape(row_count, LANES),) + (ring...  1.69 us
    pallas_call x1, Pallas kernels, body(): pl.pallas_call(prepare_kernel, out_shape=(plane, plane, shape(4 * ROWS, c...  1.37 us
    pallas_call x1, Pallas kernels, body(): pl.pallas_call(finish_kernel, out_shape=(final, final), in_specs=[VMEM] *...  1.36 us
  transfers between devices with their start and end apart: 4, of which 0 were waited for; matrix products, arithmetic and copies ran while one was open for 0% of the time, Pallas kernels for 12%

profile of v5, /device:TPU:0, one launch (start us, length us, event | category | flops | bytes accessed | tf_op | source)
XLA Modules:
  0.0 41.3 jit_solution(6785400142651547813)
XLA Ops:
  0.6 8.6 %flux.1 = (f32[256,512]{1,0:T(8,128)S(1)}, f32[256,512]{1,0:T(8,128)S(1)}, f32[256,512]{1,0:T(8,128)S(1)}, f32[80,512]{1,0:T(8,128)S(1)}, f32[64,128]{1,0:T(8,12...) custom-call(f32[16]{0:T(128)} %thick_hbm.1, ...), custom_call_target="tpu_custom_call" | custom-call | tf_op jit(solution)/shard_map/flux/pallas_call | solution.py:782
  9.2 3.1 %collective-permute-start = (f32[64,128]{1,0:T(8,128)S(1)}, f32[64,128]{1,0:T(8,128)S(1)}, u32[]{:S(2)}, u32[]{:S(2)}) collective-permute-start(f32[64,128]{1,0:T(8,128)S(1)} %get-tuple-element.56.send_a), channel_id=1, source_target_pairs={{0,1},{1,0},{2,3},{3,2},{4,5},{5,4},{6,7},{7,6},{8,9},{9,8},{10,11... | collective-permute-start | bytes 98312 | tf_op jit(solution)/shard_map/ppermute | solution.py:768
  12.3 0.7 %collective-permute-start.1 = (f32[64,128]{1,0:T(8,128)S(1)}, f32[64,128]{1,0:T(8,128)S(1)}, u32[]{:S(2)}, u32[]{:S(2)}) collective-permute-start(f32[64,128]{1,0:T(8,128)S(1)} %get-tuple-element.57.send_b), channel_id=1, source_target_pairs={{1,2},{2,1},{5,6},{6,5},{9,10},{10,9},{13,14},{14,13},{17,18},{18,... | collective-permute-start | bytes 98312 | tf_op jit(solution)/shard_map/ppermute | solution.py:768
  13.0 1.4 %prepare.1 = (f32[256,512]{1,0:T(8,128)S(1)}, f32[256,512]{1,0:T(8,128)S(1)}, f32[32,512]{1,0:T(8,128)S(1)}, f32[264,640]{1,0:T(8,128)S(1)}, f32[264,640]{1,0:T(...) custom-call(f32[256,512]{1,0:T(8,128)S(1)} %get-tuple-element.48.fu,, ...), custom_call_target="tpu_custom_call" | custom-call | flops 10485760 | bytes 4194304 | tf_op jit(solution)/shard_map/prepare/pallas_call | solution.py:799
  14.4 0.0 collective-permute-done.recv_a
  14.4 0.0 collective-permute-done.1.recv_b
  14.4 0.2 edge.1
  14.5 0.1 collective-permute-start.2
  14.6 0.7 %collective-permute-start.3 = (f32[24,640]{1,0:T(8,128)S(1)}, f32[24,640]{1,0:T(8,128)S(1)}, u32[]{:S(2)}, u32[]{:S(2)}) collective-permute-start(f32[24,640]{1,0:T(8,128)S(1)} %get-tuple-element.71), channel_id=1, source_target_pairs={{4,8},{8,4},{12,16},{16,12},{20,24},{24,20},{5,9},{9,5},{13,17},{1... | collective-permute-start | bytes 184328 | tf_op jit(solution)/shard_map/ppermute | solution.py:768
  15.3 1.7 %widen.1 = (f32[256,128]{1,0:T(8,128)S(1)}, f32[264,640]{1,0:T(8,128)S(1)}, f32[264,640]{1,0:T(8,128)S(1)}, f32[264,640]{1,0:T(8,128)S(1)}, f32[264,640]{1,0:T(8...) custom-call(f32[32,640]{1,0:T(8,128)S(1)} %get-tuple-element.47.mask, ...), custom_call_target="tpu_custom_call", output_to_operand_aliasing={{1}: (6, {}), {2}: (7, {}), {3}: (8, {}), {4}: (9, {}), {5}... | custom-call | flops 10485760 | bytes 4194304 | tf_op jit(solution)/shard_map/widen/pallas_call | solution.py:818
  17.0 1.8 %early.1 = (f32[264,640]{1,0:T(8,128)S(1)}, f32[264,640]{1,0:T(8,128)S(1)}) custom-call(f32[264,640]{1,0:T(8,128)S(1)} %get-tuple-element.72.ax.ax_in, f32[264,640]{1,0:T(8,128)S(1)} %get-tuple-element.73.ay.ay_in, f32[264,640]{1,0:T(8,128)S(1)} %get-tuple-element.74.bly.bly_in, f32[264,640]{1,0:T(8,128)S(1)} %get-tuple-element.75.nx.nx_in, ...), custom_call_target="tpu_custom_call" | custom-call | flops 10485760 | bytes 4194304 | tf_op jit(solution)/shard_map/early/pallas_call | solution.py:829
  18.8 0.0 collective-permute-done.2.rows_a
  18.8 0.0 collective-permute-done.3.rows_b
  18.9 3.6 %basis.1 = (f32[264,640]{1,0:T(8,128)S(1)}, f32[256,512]{1,0:T(8,128)S(1)}, f32[32,128]{1,0:T(8,128)S(1)}, f32[264,640]{1,0:T(8,128)S(1)}, f32[264,640]{1,0:T(8,...) custom-call(f32[32,640]{1,0:T(8,128)S(1)} %get-tuple-element.47.mask, ...), custom_call_target="tpu_custom_call", output_to_operand_aliasing={{3}: (10, {}), {4}: (11, {}), {5}: (12, {}), {6}: (13, {}),... | custom-call | tf_op jit(solution)/shard_map/basis/pallas_call | solution.py:838
  22.5 17.5 %all_to_all.11 = f32[32,1,128]{2,1,0:T(1,128)S(1)} all-to-all(f32[32,1,128]{2,1,0:T(1,128)S(1)} %bitcast.5), channel_id=1, replica_groups=mesh['blk'=8,'sub'=4] {'blk','sub'}, dimensions={0} | all-to-all | bytes 32768 | tf_op jit(solution)/shard_map/all_to_all | solution.py:848
  39.9 1.4 %finish.1 = (f32[256,512]{1,0:T(8,128)}, f32[256,512]{1,0:T(8,128)}) custom-call(f32[32,128]{1,0:T(8,128)S(1)} %bitcast.4, f32[264,640]{1,0:T(8,128)S(1)} %get-tuple-element.86.c0, f32[264,640]{1,0:T(8,128)S(1)} %get-tuple-element.87.c1, f32[264,640]{1,0:T(8,128)S(1)} %get-tuple-element.88.c2, f32[264,640]{1,0:T(8,128)S(1)} %get-tuple-element.89.c3, ...), custom_call_target="tpu_custom_call" | custom-call | tf_op jit(solution)/shard_map/finish/pallas_call | solution.py:849
Async XLA Ops:
  9.2 5.2 %collective-permute-start = (f32[64,128]{1,0:T(8,128)S(1)}, f32[64,128]{1,0:T(8,128)S(1)}, u32[]{:S(2)}, u32[]{:S(2)}) collective-permute-start(f32[64,128]{1,0:T(8,128)S(1)} %get-tuple-element.56.send_a), channel_id=1, source_target_pairs={{0,1},{1,0},{2,3},{3,2},{4,5},{5,4},{6,7},{7,6},{8,9},{9,8},{10,11... | collective-permute-start | bytes 98312 | tf_op jit(solution)/shard_map/ppermute | solution.py:768
  12.3 2.0 %collective-permute-start.1 = (f32[64,128]{1,0:T(8,128)S(1)}, f32[64,128]{1,0:T(8,128)S(1)}, u32[]{:S(2)}, u32[]{:S(2)}) collective-permute-start(f32[64,128]{1,0:T(8,128)S(1)} %get-tuple-element.57.send_b), channel_id=1, source_target_pairs={{1,2},{2,1},{5,6},{6,5},{9,10},{10,9},{13,14},{14,13},{17,18},{18,... | collective-permute-start | bytes 98312 | tf_op jit(solution)/shard_map/ppermute | solution.py:768
  14.5 4.3 %collective-permute-start.2 = (f32[24,640]{1,0:T(8,128)S(1)}, f32[24,640]{1,0:T(8,128)S(1)}, u32[]{:S(2)}, u32[]{:S(2)}) collective-permute-start(f32[24,640]{1,0:T(8,128)S(1)} %get-tuple-element.70), channel_id=1, source_target_pairs={{0,4},{4,0},{8,12},{12,8},{16,20},{20,16},{24,28},{28,24},{1,5},{5... | collective-permute-start | bytes 184328 | tf_op jit(solution)/shard_map/ppermute | solution.py:768
  14.6 4.2 %collective-permute-start.3 = (f32[24,640]{1,0:T(8,128)S(1)}, f32[24,640]{1,0:T(8,128)S(1)}, u32[]{:S(2)}, u32[]{:S(2)}) collective-permute-start(f32[24,640]{1,0:T(8,128)S(1)} %get-tuple-element.71), channel_id=1, source_target_pairs={{4,8},{8,4},{12,16},{16,12},{20,24},{24,20},{5,9},{9,5},{13,17},{1... | collective-permute-start | bytes 184328 | tf_op jit(solution)/shard_map/ppermute | solution.py:768

commit v6 on v5

--- a/solution.py
+++ b/solution.py
@@ -13,8 +13,8 @@
 LANES = 128
 ROWS = 8
 CHUNK = 32
-PIECE = 16
-AHEAD = 6
+PIECE = 32
+AHEAD = 3
 UNROLL = 8
 PARTS = 4
 F32 = jnp.float32

time: 41.5 us -> 41 us (0.988)
    pallas_call x1, Pallas kernels: 8.56 us -> 8.14 us  [body(): pl.pallas_call(flux_kernel, out_shape=(plane, plane, plane, shape(10 * RO...]
where the time goes in v6:
time: 41 us; the launch traced here: 40.9 us
  Pallas kernels  18.2 us (44%)
  blocking collectives  17.5 us (43%)
  starting transfers between devices  4.5 us (11%)
  between operations  0.72 us (2%)
    all_to_all x1, blocking collectives, body(): gram = lax.all_to_all(gram, ('blk', 'sub'), 0, 0, tiled=True)  17.5 us
    pallas_call x1, Pallas kernels, body(): pl.pallas_call(flux_kernel, out_shape=(plane, plane, plane, shape(10 * RO...  8.14 us
    ppermute x4, starting transfers between devices, swap(): return lax.ppermute(value, axis, pairs)  4.5 us
    pallas_call x1, Pallas kernels, body(): pl.pallas_call(basis_kernel, out_shape=(ring, plane, shape(devices, LANES...  3.6 us
    pallas_call x1, Pallas kernels, body(): pl.pallas_call(early_kernel, out_shape=(ring, ring), in_specs=[VMEM] * 10...  1.84 us
    pallas_call x1, Pallas kernels, body(): pl.pallas_call(widen_kernel, out_shape=(shape(row_count, LANES),) + (ring...  1.69 us
    pallas_call x1, Pallas kernels, body(): pl.pallas_call(prepare_kernel, out_shape=(plane, plane, shape(4 * ROWS, c...  1.37 us
    pallas_call x1, Pallas kernels, body(): pl.pallas_call(finish_kernel, out_shape=(final, final), in_specs=[VMEM] *...  1.36 us
  transfers between devices with their start and end apart: 4, of which 0 were waited for; matrix products, arithmetic and copies ran while one was open for 0% of the time, Pallas kernels for 12%

profile of v6, /device:TPU:0, one launch (start us, length us, event | category | flops | bytes accessed | tf_op | source)
XLA Modules:
  0.0 40.9 jit_solution(1692766734616160679)
XLA Ops:
  0.6 8.1 %flux.1 = (f32[256,512]{1,0:T(8,128)S(1)}, f32[256,512]{1,0:T(8,128)S(1)}, f32[256,512]{1,0:T(8,128)S(1)}, f32[80,512]{1,0:T(8,128)S(1)}, f32[64,128]{1,0:T(8,12...) custom-call(f32[16]{0:T(128)} %thick_hbm.1, ...), custom_call_target="tpu_custom_call" | custom-call | tf_op jit(solution)/shard_map/flux/pallas_call | solution.py:782
  8.8 3.1 %collective-permute-start = (f32[64,128]{1,0:T(8,128)S(1)}, f32[64,128]{1,0:T(8,128)S(1)}, u32[]{:S(2)}, u32[]{:S(2)}) collective-permute-start(f32[64,128]{1,0:T(8,128)S(1)} %get-tuple-element.56.send_a), channel_id=1, source_target_pairs={{0,1},{1,0},{2,3},{3,2},{4,5},{5,4},{6,7},{7,6},{8,9},{9,8},{10,11... | collective-permute-start | bytes 98312 | tf_op jit(solution)/shard_map/ppermute | solution.py:768
  11.9 0.7 %collective-permute-start.1 = (f32[64,128]{1,0:T(8,128)S(1)}, f32[64,128]{1,0:T(8,128)S(1)}, u32[]{:S(2)}, u32[]{:S(2)}) collective-permute-start(f32[64,128]{1,0:T(8,128)S(1)} %get-tuple-element.57.send_b), channel_id=1, source_target_pairs={{1,2},{2,1},{5,6},{6,5},{9,10},{10,9},{13,14},{14,13},{17,18},{18,... | collective-permute-start | bytes 98312 | tf_op jit(solution)/shard_map/ppermute | solution.py:768
  12.6 1.4 %prepare.1 = (f32[256,512]{1,0:T(8,128)S(1)}, f32[256,512]{1,0:T(8,128)S(1)}, f32[32,512]{1,0:T(8,128)S(1)}, f32[264,640]{1,0:T(8,128)S(1)}, f32[264,640]{1,0:T(...) custom-call(f32[256,512]{1,0:T(8,128)S(1)} %get-tuple-element.48.fu,, ...), custom_call_target="tpu_custom_call" | custom-call | flops 10485760 | bytes 4194304 | tf_op jit(solution)/shard_map/prepare/pallas_call | solution.py:799
  13.9 0.0 collective-permute-done.recv_a
  13.9 0.0 collective-permute-done.1.recv_b
  14.0 0.2 edge.1
  14.1 0.1 collective-permute-start.2
  14.2 0.7 %collective-permute-start.3 = (f32[24,640]{1,0:T(8,128)S(1)}, f32[24,640]{1,0:T(8,128)S(1)}, u32[]{:S(2)}, u32[]{:S(2)}) collective-permute-start(f32[24,640]{1,0:T(8,128)S(1)} %get-tuple-element.71), channel_id=1, source_target_pairs={{4,8},{8,4},{12,16},{16,12},{20,24},{24,20},{5,9},{9,5},{13,17},{1... | collective-permute-start | bytes 184328 | tf_op jit(solution)/shard_map/ppermute | solution.py:768
  14.9 1.7 %widen.1 = (f32[256,128]{1,0:T(8,128)S(1)}, f32[264,640]{1,0:T(8,128)S(1)}, f32[264,640]{1,0:T(8,128)S(1)}, f32[264,640]{1,0:T(8,128)S(1)}, f32[264,640]{1,0:T(8...) custom-call(f32[32,640]{1,0:T(8,128)S(1)} %get-tuple-element.47.mask, ...), custom_call_target="tpu_custom_call", output_to_operand_aliasing={{1}: (6, {}), {2}: (7, {}), {3}: (8, {}), {4}: (9, {}), {5}... | custom-call | flops 10485760 | bytes 4194304 | tf_op jit(solution)/shard_map/widen/pallas_call | solution.py:818
  16.6 1.8 %early.1 = (f32[264,640]{1,0:T(8,128)S(1)}, f32[264,640]{1,0:T(8,128)S(1)}) custom-call(f32[264,640]{1,0:T(8,128)S(1)} %get-tuple-element.72.ax.ax_in, f32[264,640]{1,0:T(8,128)S(1)} %get-tuple-element.73.ay.ay_in, f32[264,640]{1,0:T(8,128)S(1)} %get-tuple-element.74.bly.bly_in, f32[264,640]{1,0:T(8,128)S(1)} %get-tuple-element.75.nx.nx_in, ...), custom_call_target="tpu_custom_call" | custom-call | flops 10485760 | bytes 4194304 | tf_op jit(solution)/shard_map/early/pallas_call | solution.py:829
  18.4 0.0 collective-permute-done.2.rows_a
  18.4 0.0 collective-permute-done.3.rows_b
  18.4 3.6 %basis.1 = (f32[264,640]{1,0:T(8,128)S(1)}, f32[256,512]{1,0:T(8,128)S(1)}, f32[32,128]{1,0:T(8,128)S(1)}, f32[264,640]{1,0:T(8,128)S(1)}, f32[264,640]{1,0:T(8,...) custom-call(f32[32,640]{1,0:T(8,128)S(1)} %get-tuple-element.47.mask, ...), custom_call_target="tpu_custom_call", output_to_operand_aliasing={{3}: (10, {}), {4}: (11, {}), {5}: (12, {}), {6}: (13, {}),... | custom-call | tf_op jit(solution)/shard_map/basis/pallas_call | solution.py:838
  22.0 17.5 %all_to_all.11 = f32[32,1,128]{2,1,0:T(1,128)S(1)} all-to-all(f32[32,1,128]{2,1,0:T(1,128)S(1)} %bitcast.5), channel_id=1, replica_groups=mesh['blk'=8,'sub'=4] {'blk','sub'}, dimensions={0} | all-to-all | bytes 32768 | tf_op jit(solution)/shard_map/all_to_all | solution.py:848
  39.5 1.4 %finish.1 = (f32[256,512]{1,0:T(8,128)}, f32[256,512]{1,0:T(8,128)}) custom-call(f32[32,128]{1,0:T(8,128)S(1)} %bitcast.4, f32[264,640]{1,0:T(8,128)S(1)} %get-tuple-element.86.c0, f32[264,640]{1,0:T(8,128)S(1)} %get-tuple-element.87.c1, f32[264,640]{1,0:T(8,128)S(1)} %get-tuple-element.88.c2, f32[264,640]{1,0:T(8,128)S(1)} %get-tuple-element.89.c3, ...), custom_call_target="tpu_custom_call" | custom-call | tf_op jit(solution)/shard_map/finish/pallas_call | solution.py:849
Async XLA Ops:
  8.8 5.2 %collective-permute-start = (f32[64,128]{1,0:T(8,128)S(1)}, f32[64,128]{1,0:T(8,128)S(1)}, u32[]{:S(2)}, u32[]{:S(2)}) collective-permute-start(f32[64,128]{1,0:T(8,128)S(1)} %get-tuple-element.56.send_a), channel_id=1, source_target_pairs={{0,1},{1,0},{2,3},{3,2},{4,5},{5,4},{6,7},{7,6},{8,9},{9,8},{10,11... | collective-permute-start | bytes 98312 | tf_op jit(solution)/shard_map/ppermute | solution.py:768
  11.9 2.0 %collective-permute-start.1 = (f32[64,128]{1,0:T(8,128)S(1)}, f32[64,128]{1,0:T(8,128)S(1)}, u32[]{:S(2)}, u32[]{:S(2)}) collective-permute-start(f32[64,128]{1,0:T(8,128)S(1)} %get-tuple-element.57.send_b), channel_id=1, source_target_pairs={{1,2},{2,1},{5,6},{6,5},{9,10},{10,9},{13,14},{14,13},{17,18},{18,... | collective-permute-start | bytes 98312 | tf_op jit(solution)/shard_map/ppermute | solution.py:768
  14.1 4.3 %collective-permute-start.2 = (f32[24,640]{1,0:T(8,128)S(1)}, f32[24,640]{1,0:T(8,128)S(1)}, u32[]{:S(2)}, u32[]{:S(2)}) collective-permute-start(f32[24,640]{1,0:T(8,128)S(1)} %get-tuple-element.70), channel_id=1, source_target_pairs={{0,4},{4,0},{8,12},{12,8},{16,20},{20,16},{24,28},{28,24},{1,5},{5... | collective-permute-start | bytes 184328 | tf_op jit(solution)/shard_map/ppermute | solution.py:768
  14.2 4.2 %collective-permute-start.3 = (f32[24,640]{1,0:T(8,128)S(1)}, f32[24,640]{1,0:T(8,128)S(1)}, u32[]{:S(2)}, u32[]{:S(2)}) collective-permute-start(f32[24,640]{1,0:T(8,128)S(1)} %get-tuple-element.71), channel_id=1, source_target_pairs={{4,8},{8,4},{12,16},{16,12},{20,24},{24,20},{5,9},{9,5},{13,17},{1... | collective-permute-start | bytes 184328 | tf_op jit(solution)/shard_map/ppermute | solution.py:768
